TPU v7x, 256 devices: a whole 4x4x8 slice. The times are simulated.
256 devices in a mesh: dp: 16 (over z_hi, x, core), tp: 4 (over z_lo), section: 4 (over y).
Axes of the slice: x: 4, y: 4, z: 8 (z_hi: 2, z_lo: 4; z = z_hi * 4 + z_lo), core: 2. Of those that a mesh axis runs over, the one named last changes fastest.
Arguments:
- tokens: bfloat16 [2048, 2304], P('dp', 'section'), may hold values from -6 to 6
- hidden_grad: bfloat16 [2048, 18432], P('dp', ('tp', 'section')), may hold values from -6 to 6
- norm_gain: float32 [2304], replicated, may hold values from 0.5 to 1.5
- w_gate: bfloat16 [2304, 18432], P('dp', ('tp', 'section')), may hold values from -0.125 to 0.125
- w_up: bfloat16 [2304, 18432], P('dp', ('tp', 'section')), may hold values from -0.125 to 0.125
Outputs:
- grad_tokens: bfloat16 [2048, 2304], P('dp', ('tp', 'section'))
- grad_gain: float32 [2304], P(('tp', 'section'))
- grad_gate: bfloat16 [2304, 18432], P('dp', ('tp', 'section'))
- grad_up: bfloat16 [2304, 18432], P('dp', ('tp', 'section'))
All inputs are finite; a program needn't handle non-finite values.
Results may differ from a plain program's by a relative error of at most 0.018.
Values may be sent and summed in bfloat16 or wider, within the bound.
No kernel may reach another device: no remote copies, remote signals or barrier semaphores. Data moves between devices by JAX's collectives and lax.ppermute only.
A program may use at most 128 MiB of HBM per device.

v0:
```python
import functools

import jax
import jax.numpy as jnp
from jax import lax
from jax.experimental import pallas as pl
from jax.experimental.pallas import tpu as pltpu
from jax.sharding import Mesh
from jax.sharding import PartitionSpec as P

DP = ("zh", "x", "core")
COLS = ("tp", "sec")
EPS = 1e-06
LANES = 128
EXTRA = 16
F32 = jnp.float32
BF16 = jnp.bfloat16
SDS = jax.ShapeDtypeStruct


def turned(array, axis, by):
    n = lax.axis_size(axis)
    return lax.ppermute(array, axis, [(i, (i + by) % n) for i in range(n)])


def swapped(array, axis):
    return turned(array, axis, 1)


def unsigned(index):
    return index.astype(jnp.uint32)


def as_block(array, *lead):
    n = len(lead)
    zeros = [jnp.uint32(0)] * (array.ndim - n)
    part = lax.dynamic_slice(array, (*lead, *zeros), (*([1] * n), *array.shape[n:]))
    return part.reshape(array.shape[n:])


def put(array, part, *lead):
    zeros = [jnp.uint32(0)] * (array.ndim - len(lead))
    part = part.reshape(*([1] * len(lead)), *array.shape[len(lead) :])
    return lax.dynamic_update_slice(array, part, (*lead, *zeros))


def parts_of(width):
    main = width // LANES // 4 * LANES
    rest = width // 4 - main
    return main, rest


def pack_kernel(main, rest, aways, gate_ref, up_ref, back_ref, *outs):
    half = back_ref.shape[0] // 2
    zh, core = lax.axis_index("zh"), lax.axis_index("core")
    rows = gate_ref.shape[0]
    if aways:
        weights, backs = outs[:2], [outs[2].at[0], outs[2].at[1]]
    else:
        weights = [out.at[pl.ds(0, rows)] for out in outs]
        backs = [out.at[pl.ds(rows, half)] for out in outs]
    sources = (
        (weights, gate_ref, up_ref),
        (backs, back_ref.at[pl.ds(0, half)], back_ref.at[pl.ds(half, half)]),
    )
    for other in range(2):
        q = (zh ^ aways) * 2 + (core ^ other)
        wide = pl.ds(pl.multiple_of(q * main, LANES), main)
        for targets, first, second in sources:
            out = targets[other]
            out[:, pl.ds(0, main)] = first[:, wide]
            out[:, pl.ds(main, main)] = second[:, wide]
            thin = []
            for ref in (first, second):
                tail = ref[:, pl.ds(4 * main, 4 * rest)]
                pick = tail[:, :rest]
                for k in range(1, 4):
                    pick = jnp.where(q == k, tail[:, k * rest : (k + 1) * rest], pick)
                thin.append(pick)
            out[:, pl.ds(2 * main, 2 * rest)] = jnp.concatenate(thin, axis=1)


def packed(aways, w_gate, w_up, hidden_grad):
    rows, width = w_gate.shape
    main, rest = parts_of(width)
    half = hidden_grad.shape[0] // 2
    if aways:
        outs = [(rows, width // 2), (rows, width // 2), (2, half, width // 2)]
    else:
        outs = [(rows + half, width // 2)] * 2
    return pl.pallas_call(
        functools.partial(pack_kernel, main, rest, aways),
        out_shape=[pltpu.VMEM(shape, BF16) for shape in outs],
        in_specs=[pl.BlockSpec(memory_space=pltpu.VMEM)] * 3,
        out_specs=[pl.BlockSpec(memory_space=pltpu.VMEM)] * len(outs),
        name="pack",
    )(w_gate, w_up, hidden_grad)


def join_kernel(main, rest, near_ref, keep_ref, give_ref, gate_ref, up_ref):
    zh, core = lax.axis_index("zh"), lax.axis_index("core")
    tails = [[None] * 4, [None] * 4]
    for aways in range(2):
        for other in range(2):
            ref = give_ref.at[aways] if other else keep_ref if aways else near_ref.at[core]
            q = (zh ^ aways) * 2 + (core ^ other)
            wide = pl.ds(pl.multiple_of(q * main, LANES), main)
            gate_ref[:, wide] = ref[:, pl.ds(0, main)]
            up_ref[:, wide] = ref[:, pl.ds(main, main)]
            tail = ref[:, pl.ds(2 * main, 2 * rest)]
            for i in range(2):
                thin = tail[:, i * rest : (i + 1) * rest]
                for k in range(4):
                    old = tails[i][k]
                    tails[i][k] = thin if old is None else jnp.where(q == k, thin, old)
    gate_ref[:, pl.ds(4 * main, 4 * rest)] = jnp.concatenate(tails[0], axis=1)
    up_ref[:, pl.ds(4 * main, 4 * rest)] = jnp.concatenate(tails[1], axis=1)


def joined(near, keep, give):
    rows, half = keep.shape
    main, rest = parts_of(half * 2)
    out = SDS((rows, half * 2), BF16)
    return pl.pallas_call(
        functools.partial(join_kernel, main, rest),
        out_shape=(out, out),
        in_specs=[pl.BlockSpec(memory_space=pltpu.VMEM)] * 3,
        out_specs=(pl.BlockSpec(memory_space=pltpu.VMEM),) * 2,
        name="join",
    )(near, keep, give)


def split_pair(block):
    main, rest = parts_of(block.shape[1] * 2)
    first = jnp.concatenate([block[:, :main], block[:, 2 * main : 2 * main + rest]], axis=1)
    second = jnp.concatenate([block[:, main : 2 * main], block[:, 2 * main + rest :]], axis=1)
    return first, second


def join_pair(first, second):
    main, rest = parts_of(first.shape[1] * 4)
    return jnp.concatenate(
        [first[:, :main], second[:, :main], first[:, main:], second[:, main:]], axis=1
    )


def ordered(own, other, first):
    return jnp.where(first, jnp.stack([own, other]), jnp.stack([other, own]))


def halves(row):
    high = row.astype(BF16)
    return high, (row - high.astype(F32)).astype(BF16)


def with_rows(block, *rows):
    shape = (EXTRA, block.shape[1])
    which = lax.broadcasted_iota(jnp.int32, shape, 0)
    tail = jnp.zeros(shape, BF16)
    for k, half in enumerate([half for row in rows for half in halves(row)]):
        tail = jnp.where(which == k, half[None, :], tail)
    return jnp.concatenate([block.astype(BF16), tail], axis=0)


def row_of(packed_rows, k=0):
    at_row = packed_rows.shape[0] - EXTRA + 2 * k
    return packed_rows[at_row].astype(F32) + packed_rows[at_row + 1].astype(F32)


def block_of(packed_rows):
    return packed_rows[: packed_rows.shape[0] - EXTRA].astype(F32)


def derivatives(gate, up, back):
    hidden, pull = jax.vjp(lambda g, u: jax.nn.gelu(g, approximate=True) * u, gate, up)
    return pull(back)


def shards(tokens, hidden_grad, norm_gain, w_gate, w_up):
    rows, width = w_gate.shape
    group = tokens.shape[0]
    features = norm_gain.shape[0]
    own_rows = features // 16
    barrier = lax.optimization_barrier

    zh, x, core, tp, sec = (unsigned(lax.axis_index(a)) for a in (*DP, *COLS))
    steps = (1, 3, 2)
    far_zh, other_core = 1 - zh, 1 - core
    first_core = core == 0
    x_to = {by: (x + by) & 3 for by in range(4)}
    sec_to = {by: (sec + by) & 3 for by in range(4)}
    tp_to = {by: (tp + by) & 3 for by in range(4)}
    offset = (tp * 4 + sec) * own_rows

    own_t = tokens.T
    far_t = swapped(own_t, "zh")

    near_own, near_other = packed(0, w_gate, w_up, hidden_grad)
    hidden_grad, near_own = barrier((hidden_grad, near_own))
    away_own, away_other, backs = packed(1, w_gate, w_up, hidden_grad)
    near_other = swapped(near_other, "core")
    away_other, far_t = barrier((away_other, far_t))
    away_own, away_other = swapped(away_own, "zh"), swapped(away_other, "zh")

    near = ordered(near_own[:rows], near_other[:rows], first_core)
    near, own_t = barrier((near, own_t))
    near_got = [turned(near, "x", by) for by in steps]

    both = jnp.concatenate([own_t, far_t], axis=1)
    section_got = [turned(both, "sec", by) for by in steps]

    near_got[0], near_got[1], backs, late_first = barrier(
        (near_got[0], near_got[1], backs, first_core)
    )
    away_other = swapped(away_other, "core")
    backs = swapped(backs, "zh")
    away = ordered(away_own, away_other, late_first)
    late = {}
    away, late[0], late[1], late[2], late[3] = barrier((away, *(sec_to[by] for by in range(4))))
    away_got = [turned(away, "x", by) for by in steps]

    inputs = jnp.zeros((4, *both.shape), BF16)
    for by, piece in zip((0, 3, 1, 2), (both, *section_got)):
        inputs = put(inputs, piece, late[by])
    inputs = inputs.reshape(features, 2 * group)
    wide = inputs.astype(F32)
    inv_rms = lax.rsqrt(jnp.mean(wide * wide, axis=0) + EPS)
    normed = (wide * inv_rms * norm_gain[:, None]).astype(BF16)
    normed, away_got[0] = barrier((normed, away_got[0]))
    normed = jnp.concatenate([normed, swapped(normed, "core")], axis=1)

    backs, *away_got = barrier((backs, *away_got))
    full = jnp.zeros((2, 4, 2, rows, width // 2), BF16)
    for pieces, place in (((near, *near_got), zh), ((away, *away_got), far_zh)):
        for by, piece in zip((0, 3, 1, 2), pieces):
            full = put(full, piece, place, x_to[by])
    full = full.reshape(features, -1)
    back = jnp.concatenate(
        [
            half
            for block in (near_own[rows:], backs[0], near_other[rows:], swapped(backs[1], "core"))
            for half in split_pair(block)
        ],
        axis=0,
    )

    product = lax.dot_general(
        normed, full, (((0,), (0,)), ((), ())), preferred_element_type=F32
    )
    gate, up = split_pair(product)
    d_gate, d_up = derivatives(gate, up, back.astype(F32))
    d_gate, d_up = d_gate.astype(BF16), d_up.astype(BF16)
    row_part = jnp.sum(d_gate.astype(F32) * gate + d_up.astype(F32) * up, axis=1)
    d_both = join_pair(d_gate, d_up)

    def d_normed(d):
        return lax.dot_general(full, d, (((1,), (1,)), ((), ())), preferred_element_type=F32)

    by_rows = normed.reshape(2, 4, 2 * rows, 4 * group)

    def part(zplace, xplace):
        return jnp.dot(as_block(by_rows, zplace, xplace), d_both, preferred_element_type=F32)

    away_parts = [part(far_zh, x_to[by]).astype(BF16) for by in steps]
    near_parts = [part(zh, x_to[by]).astype(BF16) for by in steps]
    away_got = [turned(away_parts[k], "x", steps[k]) for k in (0, 1)]

    got = swapped(d_normed(d_both[2 * group :]).astype(BF16), "core")
    row = row_part[: 2 * group] + swapped(row_part[2 * group :], "core")
    mine = d_normed(d_both[: 2 * group]) + got.astype(F32)
    mine = mine.reshape(4, 4, own_rows, 2 * group)

    def section(index):
        zero = jnp.uint32(0)
        block = lax.dynamic_slice(
            mine, (zero, index, zero, zero), (4, 1, own_rows, 2 * group)
        )
        return block.reshape(4 * own_rows, 2 * group)

    sends = [with_rows(section(sec_to[by]), row) for by in steps]
    *away_got, away_parts[2], sends[0], sends[1], sends[2] = barrier(
        (*away_got, away_parts[2], *sends)
    )
    away_got.append(turned(away_parts[2], "x", 2))
    got = [turned(s, "sec", by) for s, by in zip(sends, steps)]
    away_got[2], *near_parts = barrier((away_got[2], *near_parts))
    near_got = [turned(p, "x", by) for p, by in zip(near_parts, steps)]
    g_away = part(far_zh, x) + sum(g.astype(F32) for g in away_got)
    g_away = g_away.astype(BF16).reshape(2, rows, -1)
    late = {}
    g_away, late[1], late[3], late[2] = barrier((g_away, *(tp_to[by] for by in steps)))
    away_keep = swapped(as_block(g_away, core), "zh")
    away_give = swapped(as_block(g_away, other_core), "zh")

    total = section(sec) + sum(block_of(g) for g in got)
    row = row + sum(row_of(g) for g in got)
    mine = total.reshape(4, own_rows, 2 * group)
    sends = [with_rows(as_block(mine, late[by]), row) for by in steps]
    got = [turned(s, "tp", by) for s, by in zip(sends, steps)]
    total = as_block(mine, tp) + sum(block_of(g) for g in got)
    row = row + sum(row_of(g) for g in got)

    own_inputs = lax.dynamic_slice(inputs, (offset, jnp.uint32(0)), (own_rows, 2 * group))
    own_inputs = own_inputs.astype(F32)
    own_gain = lax.dynamic_slice(norm_gain, (offset,), (own_rows,))[:, None]
    gain_part = jnp.sum(total * own_inputs * inv_rms, axis=1)
    gain_rows = jnp.pad(gain_part, (0, 2 * group - own_rows)).reshape(2, group)
    send = with_rows(total[:, group:], row[group:], gain_rows[0], gain_rows[1])
    send, near_got[0], near_got[1], late_zh = barrier((send, near_got[0], near_got[1], zh))
    got = swapped(send, "zh")
    g_near = part(late_zh, x) + sum(g.astype(F32) for g in near_got)
    g_near = g_near.astype(BF16).reshape(2, rows, -1)
    give = swapped(jnp.stack([as_block(g_near, other_core), away_give]), "core")
    grad_gain = gain_part + jnp.concatenate([row_of(got, 1), row_of(got, 2)])[:own_rows]
    grad_gain = grad_gain + swapped(grad_gain, "core")
    grad_gain = grad_gain + sum(turned(grad_gain, "x", by) for by in steps)
    d_own, row_sum = total[:, :group] + block_of(got), row[:group] + row_of(got)
    inv = inv_rms[:group]
    own_inputs = own_inputs[:, :group]
    grad_tokens = inv * own_gain * d_own - own_inputs * (inv**2 * row_sum / features)
    grad_gate, grad_up = joined(g_near, away_keep, give)
    return grad_tokens.T.astype(BF16), grad_gain, grad_gate, grad_up


def solution(mesh):
    split = Mesh(
        mesh.devices.reshape(2, 4, 2, mesh.shape["tp"], mesh.shape["section"]),
        (*DP, *COLS),
    )
    weights = P(DP, COLS)
    return jax.shard_map(
        shards,
        mesh=split,
        in_specs=(P(DP, "sec"), weights, P(), weights, weights),
        out_specs=(weights, P(COLS), weights, weights),
        check_vma=False,
    )
```

profile of v0, /device:TPU:24, one launch (start us, length us, event | category | flops | bytes accessed | tf_op | source)
XLA Modules:
  0.0 160.4 jit_solution(2601603075848892244)
XLA Ops:
  0.7 2.0 %pack.2 = (bf16[208,576]{1,0:T(8,128)(2,1)S(1)}, bf16[208,576]{1,0:T(8,128)(2,1)S(1)}) custom-call(bf16[144,1152]{1,0:T(8,128)(2,1)} %gate_ref.3, bf16[144,1152]{1,0:T(8,128)(2,1)} %up_ref.3, bf16[128,1152]{1,0:T(8,128)(2,1)} %back_ref.2), custom_call_target="tpu_custom_call" | custom-call | tf_op jit(solution)/shard_map/pack/pallas_call | solution.py:91
  2.8 7.3 %collective-permute-start.1 = (bf16[576,128]{1,0:T(8,128)(2,1)}, bf16[576,128]{1,0:T(8,128)(2,1)S(1)}, u32[]{:S(2)}, u32[]{:S(2)}) collective-permute-start(bf16[576,128]{1,0:T(8,128)(2,1)} %bitcast.140), channel_id=1, source_target_pairs={{0,128},{128,0},{1,129},{129,1},{2,130},{130,2},{3,131},{131,3},{4... | collective-permute-start | bytes 442376 | tf_op jit(solution)/shard_map/ppermute | solution.py:23
  10.1 2.0 %pack.3 = (bf16[144,576]{1,0:T(8,128)(2,1)S(1)}, bf16[144,576]{1,0:T(8,128)(2,1)S(1)}, bf16[2,64,576]{2,1,0:T(8,128)(2,1)S(1)}) custom-call(bf16[144,1152]{1,0:T(8,128)(2,1)} %gate_ref.3, bf16[144,1152]{1,0:T(8,128)(2,1)} %up_ref.3, bf16[128,1152]{1,0:T(8,128)(2,1)} %back_ref.2), custom_call_target="tpu_custom_call" | custom-call | tf_op jit(solution)/shard_map/pack/pallas_call | solution.py:91
  12.5 4.4 %collective-permute-done.1 = bf16[576,128]{1,0:T(8,128)(2,1)S(1)} collective-permute-done((bf16[576,128]{1,0:T(8,128)(2,1)}, bf16[576,128]{1,0:T(8,128)(2,1)S(1)}, u32[]{:S(2)}, u32[]{:S(2)}) %collective-permute-start.1) | collective-permute-done | bytes 147488 | tf_op jit(solution)/shard_map/ppermute | solution.py:23
  16.9 6.6 %collective-permute-start.5 = (bf16[144,576]{1,0:T(8,128)(2,1)S(1)}, bf16[144,576]{1,0:T(8,128)(2,1)S(1)}, u32[]{:S(2)}, u32[]{:S(2)}) collective-permute-start(bf16[144,576]{1,0:T(8,128)(2,1)S(1)} %get-tuple-element.61), channel_id=1, source_target_pairs={{0,128},{128,0},{1,129},{129,1},{2,130},{130,2},{3,131},{131,3},{4... | collective-permute-start | bytes 497672 | tf_op jit(solution)/shard_map/ppermute | solution.py:23
  23.6 1.6 collective-permute-start.2
  25.2 1.7 %collective-permute-start.3 = (bf16[2,144,576]{2,1,0:T(8,128)(2,1)S(1)}, bf16[2,144,576]{2,1,0:T(8,128)(2,1)S(1)}, u32[]{:S(2)}, u32[]{:S(2)}) collective-permute-start(bf16[2,144,576]{2,1,0:T(8,128)(2,1)S(1)} %maximum_select_fusion), channel_id=1, source_target_pairs={{0,96},{32,0},{64,32},{96,64},{1,97},{33,1},{65,33},{97,65},{2,98}... | collective-permute-start | bytes 995336 | tf_op jit(solution)/shard_map/ppermute | solution.py:23
  27.4 9.4 %collective-permute-done.5 = bf16[144,576]{1,0:T(8,128)(2,1)S(1)} collective-permute-done((bf16[144,576]{1,0:T(8,128)(2,1)S(1)}, bf16[144,576]{1,0:T(8,128)(2,1)S(1)}, u32[]{:S(2)}, u32[]{:S(2)}) %collective-permute-start.5) | collective-permute-done | bytes 165920 | tf_op jit(solution)/shard_map/ppermute | solution.py:23
  38.7 3.0 %collective-permute-start.10 = (bf16[2,144,576]{2,1,0:T(8,128)(2,1)S(1)}, bf16[2,144,576]{2,1,0:T(8,128)(2,1)S(1)}, u32[]{:S(2)}, u32[]{:S(2)}) collective-permute-start(bf16[2,144,576]{2,1,0:T(8,128)(2,1)S(1)} %maximum_select_fusion), channel_id=1, source_target_pairs={{0,64},{32,96},{64,0},{96,32},{1,65},{33,97},{65,1},{97,33},{2,66}... | collective-permute-start | bytes 995336 | tf_op jit(solution)/shard_map/ppermute | solution.py:23
  42.6 2.7 %collective-permute-start.13 = (bf16[2,144,576]{2,1,0:T(8,128)(2,1)S(1)}, bf16[2,144,576]{2,1,0:T(8,128)(2,1)S(1)}, u32[]{:S(2)}, u32[]{:S(2)}) collective-permute-start(bf16[2,144,576]{2,1,0:T(8,128)(2,1)S(1)} %maximum_select_fusion.1), channel_id=1, source_target_pairs={{0,96},{32,0},{64,32},{96,64},{1,97},{33,1},{65,33},{97,65},{2,98}... | collective-permute-start | bytes 995336 | tf_op jit(solution)/shard_map/ppermute | solution.py:23
  45.3 8.6 %collective-permute-done.8 = bf16[576,256]{1,0:T(8,128)(2,1)S(1)} collective-permute-done((bf16[576,256]{1,0:T(8,128)(2,1)S(1)}, bf16[576,256]{1,0:T(8,128)(2,1)S(1)}, u32[]{:S(2)}, u32[]{:S(2)}) %collective-permute-start.8) | collective-permute-done | bytes 294944 | tf_op jit(solution)/shard_map/ppermute | solution.py:23
  53.9 3.0 %collective-permute-start.14 = (bf16[2,144,576]{2,1,0:T(8,128)(2,1)S(1)}, bf16[2,144,576]{2,1,0:T(8,128)(2,1)S(1)}, u32[]{:S(2)}, u32[]{:S(2)}) collective-permute-start(bf16[2,144,576]{2,1,0:T(8,128)(2,1)S(1)} %maximum_select_fusion.1), channel_id=1, source_target_pairs={{0,64},{32,96},{64,0},{96,32},{1,65},{33,97},{65,1},{97,33},{2,66}... | collective-permute-start | bytes 995336 | tf_op jit(solution)/shard_map/ppermute | solution.py:23
  57.8 2.2 %collective-permute-start.11 = (bf16[2,64,576]{2,1,0:T(8,128)(2,1)S(1)}, bf16[2,64,576]{2,1,0:T(8,128)(2,1)S(1)}, u32[]{:S(2)}, u32[]{:S(2)}) collective-permute-start(bf16[2,64,576]{2,1,0:T(8,128)(2,1)S(1)} %get-tuple-element.69), channel_id=1, source_target_pairs={{0,128},{128,0},{1,129},{129,1},{2,130},{130,2},{3,131},{131,3},{4... | collective-permute-start | bytes 442376 | tf_op jit(solution)/shard_map/ppermute | solution.py:23
  60.2 8.4 %collective-permute-done.11 = bf16[2,64,576]{2,1,0:T(8,128)(2,1)S(1)} collective-permute-done((bf16[2,64,576]{2,1,0:T(8,128)(2,1)S(1)}, bf16[2,64,576]{2,1,0:T(8,128)(2,1)S(1)}, u32[]{:S(2)}, u32[]{:S(2)}) %collective-permute-start.11) | collective-permute-done | bytes 147488 | tf_op jit(solution)/shard_map/ppermute | solution.py:23
  70.2 1.6 collective-permute-done.16
  71.9 2.1 %fusion.82 = f32[512,576]{1,0:T(8,128)S(1)} fusion(bf16[2304,512]{1,0:T(8,128)(2,1)S(1)} %constant_dynamic-update-slice_fusion.2, bf16[2304,576]{1,0:T(8,128)(2,1)S(1)} %bitcast.114), kind=kOutput, calls=%fused_computation.192 | convolution fusion | flops 1358954496 | bytes 6193152 | tf_op jit(solution)/shard_map/dot_general | solution.py:247
  79.0 1.2 collective-permute-start.19
  82.5 7.4 %collective-permute-done.19 = bf16[288,576]{1,0:T(8,128)(2,1)S(1)} collective-permute-done((bf16[288,576]{1,0:T(8,128)(2,1)S(1)}, bf16[288,576]{1,0:T(8,128)(2,1)S(1)}, u32[]{:S(2)}, u32[]{:S(2)}) %collective-permute-start.19) | collective-permute-done | bytes 331808 | tf_op jit(solution)/shard_map/ppermute | solution.py:23
  89.9 2.1 %collective-permute-done.18 = bf16[288,576]{1,0:T(8,128)(2,1)S(1)} collective-permute-done((bf16[288,576]{1,0:T(8,128)(2,1)S(1)}, bf16[288,576]{1,0:T(8,128)(2,1)S(1)}, u32[]{:S(2)}, u32[]{:S(2)}) %collective-permute-start.18) | collective-permute-done | bytes 331808 | tf_op jit(solution)/shard_map/ppermute | solution.py:23
  92.0 1.6 collective-permute-start.21
  94.0 2.0 %collective-permute-start.23 = (bf16[592,256]{1,0:T(8,128)(2,1)S(1)}, bf16[592,256]{1,0:T(8,128)(2,1)S(1)}, u32[]{:S(2)}, u32[]{:S(2)}) collective-permute-start(bf16[592,256]{1,0:T(8,128)(2,1)S(1)} %get-tuple-element.78), channel_id=1, source_target_pairs={{0,2},{1,3},{2,0},{3,1},{4,6},{5,7},{6,4},{7,5},{8,10},{9,11},{10,... | collective-permute-start | bytes 909320 | tf_op jit(solution)/shard_map/ppermute | solution.py:23
  96.6 5.5 %collective-permute-done.21 = bf16[592,256]{1,0:T(8,128)(2,1)S(1)} collective-permute-done((bf16[592,256]{1,0:T(8,128)(2,1)S(1)}, bf16[592,256]{1,0:T(8,128)(2,1)S(1)}, u32[]{:S(2)}, u32[]{:S(2)}) %collective-permute-start.21) | collective-permute-done | bytes 303136 | tf_op jit(solution)/shard_map/ppermute | solution.py:23
  102.1 7.2 %collective-permute-done.22 = bf16[592,256]{1,0:T(8,128)(2,1)S(1)} collective-permute-done((bf16[592,256]{1,0:T(8,128)(2,1)S(1)}, bf16[592,256]{1,0:T(8,128)(2,1)S(1)}, u32[]{:S(2)}, u32[]{:S(2)}) %collective-permute-start.22) | collective-permute-done | bytes 303136 | tf_op jit(solution)/shard_map/ppermute | solution.py:23
  110.2 3.8 %collective-permute-start.26 = (bf16[160,256]{1,0:T(8,128)(2,1)S(1)}, bf16[160,256]{1,0:T(8,128)(2,1)S(1)}, u32[]{:S(2)}, u32[]{:S(2)}) collective-permute-start(bf16[160,256]{1,0:T(8,128)(2,1)S(1)} %get-tuple-element.139), channel_id=1, source_target_pairs={{0,12},{4,0},{8,4},{12,8},{1,13},{5,1},{9,5},{13,9},{2,14},{6,2},{... | collective-permute-start | bytes 245768 | tf_op jit(solution)/shard_map/ppermute | solution.py:23
  114.0 3.2 %collective-permute-start.29 = (bf16[288,576]{1,0:T(8,128)(2,1)S(1)}, bf16[288,576]{1,0:T(8,128)(2,1)S(1)}, u32[]{:S(2)}, u32[]{:S(2)}) collective-permute-start(bf16[288,576]{1,0:T(8,128)(2,1)S(1)} %convolution_convert_fusion.2), channel_id=1, source_target_pairs={{0,96},{32,0},{64,32},{96,64},{1,97},{33,1},{65,33},{97,65},{2,98}... | collective-permute-start | bytes 995336 | tf_op jit(solution)/shard_map/ppermute | solution.py:23
  117.4 2.1 %collective-permute-start.37 = (bf16[144,576]{1,0:T(8,128)(2,1)S(1)}, bf16[144,576]{1,0:T(8,128)(2,1)S(1)}, u32[]{:S(2)}, u32[]{:S(2)}) collective-permute-start(bf16[144,576]{1,0:T(8,128)(2,1)S(1)} %get-tuple-element.116), channel_id=1, source_target_pairs={{0,128},{128,0},{1,129},{129,1},{2,130},{130,2},{3,131},{131,3},{4... | collective-permute-start | bytes 497672 | tf_op jit(solution)/shard_map/ppermute | solution.py:23
  119.5 17.2 %collective-permute-done.27 = bf16[160,256]{1,0:T(8,128)(2,1)S(1)} collective-permute-done((bf16[160,256]{1,0:T(8,128)(2,1)S(1)}, bf16[160,256]{1,0:T(8,128)(2,1)S(1)}, u32[]{:S(2)}, u32[]{:S(2)}) %collective-permute-start.27) | collective-permute-done | bytes 81952 | tf_op jit(solution)/shard_map/ppermute | solution.py:23
  137.0 6.0 %collective-permute-start.30 = (bf16[160,128]{1,0:T(8,128)(2,1)S(1)}, bf16[160,128]{1,0:T(8,128)(2,1)S(1)}, u32[]{:S(2)}, u32[]{:S(2)}) collective-permute-start(bf16[160,128]{1,0:T(8,128)(2,1)S(1)} %pad_maximum_fusion.10), channel_id=1, source_target_pairs={{0,128},{128,0},{1,129},{129,1},{2,130},{130,2},{3,131},{131,3},{4... | collective-permute-start | bytes 122888 | tf_op jit(solution)/shard_map/ppermute | solution.py:23
  143.7 2.9 %collective-permute-done.30 = bf16[160,128]{1,0:T(8,128)(2,1)S(1)} collective-permute-done((bf16[160,128]{1,0:T(8,128)(2,1)S(1)}, bf16[160,128]{1,0:T(8,128)(2,1)S(1)}, u32[]{:S(2)}, u32[]{:S(2)}) %collective-permute-start.30) | collective-permute-done | bytes 40992 | tf_op jit(solution)/shard_map/ppermute | solution.py:23
  147.8 3.2 %collective-permute-start.33 = (f32[144]{0:T(256)S(1)}, f32[144]{0:T(256)S(1)}, u32[]{:S(2)}, u32[]{:S(2)}) collective-permute-start(f32[144]{0:T(256)S(1)} %add.232), channel_id=1, source_target_pairs={{0,96},{32,0},{64,32},{96,64},{1,97},{33,1},{65,33},{97,65},{2,98}... | collective-permute-start | bytes 1736 | tf_op jit(solution)/shard_map/ppermute | solution.py:23
  152.6 3.5 %collective-permute-done.34 = f32[144]{0:T(256)S(1)} collective-permute-done((f32[144]{0:T(256)S(1)}, f32[144]{0:T(256)S(1)}, u32[]{:S(2)}, u32[]{:S(2)}) %collective-permute-start.34) | collective-permute-done | bytes 608 | tf_op jit(solution)/shard_map/ppermute | solution.py:23
  158.1 2.2 %join.1 = (bf16[144,1152]{1,0:T(8,128)(2,1)}, bf16[144,1152]{1,0:T(8,128)(2,1)}) custom-call(bf16[2,144,576]{2,1,0:T(8,128)(2,1)} %bitcast.130, bf16[144,576]{1,0:T(8,128)(2,1)} %copy-done.2, bf16[2,144,576]{2,1,0:T(8,128)(2,1)} %copy-done.1), custom_call_target="tpu_custom_call" | custom-call | tf_op jit(solution)/shard_map/join/pallas_call | solution.py:124
  (157 shorter events, 21.0 us)
Async XLA Ops:
  2.7 20.8 %collective-permute-start = (bf16[208,576]{1,0:T(8,128)(2,1)S(1)}, bf16[208,576]{1,0:T(8,128)(2,1)S(1)}, u32[]{:S(2)}, u32[]{:S(2)}) collective-permute-start(bf16[208,576]{1,0:T(8,128)(2,1)S(1)} %get-tuple-element.52), channel_id=1, source_target_pairs={{0,16},{16,0},{1,17},{17,1},{2,18},{18,2},{3,19},{19,3},{4,20},{20... | collective-permute-start | bytes 718856 | tf_op jit(solution)/shard_map/ppermute | solution.py:23
  2.8 14.1 %collective-permute-start.1 = (bf16[576,128]{1,0:T(8,128)(2,1)}, bf16[576,128]{1,0:T(8,128)(2,1)S(1)}, u32[]{:S(2)}, u32[]{:S(2)}) collective-permute-start(bf16[576,128]{1,0:T(8,128)(2,1)} %bitcast.140), channel_id=1, source_target_pairs={{0,128},{128,0},{1,129},{129,1},{2,130},{130,2},{3,131},{131,3},{4... | collective-permute-start | bytes 442376 | tf_op jit(solution)/shard_map/ppermute | solution.py:23
  12.1 26.6 %collective-permute-start.4 = (bf16[144,576]{1,0:T(8,128)(2,1)S(1)}, bf16[144,576]{1,0:T(8,128)(2,1)S(1)}, u32[]{:S(2)}, u32[]{:S(2)}) collective-permute-start(bf16[144,576]{1,0:T(8,128)(2,1)S(1)} %get-tuple-element.60), channel_id=1, source_target_pairs={{0,128},{128,0},{1,129},{129,1},{2,130},{130,2},{3,131},{131,3},{4... | collective-permute-start | bytes 497672 | tf_op jit(solution)/shard_map/ppermute | solution.py:23
  16.9 20.0 %collective-permute-start.5 = (bf16[144,576]{1,0:T(8,128)(2,1)S(1)}, bf16[144,576]{1,0:T(8,128)(2,1)S(1)}, u32[]{:S(2)}, u32[]{:S(2)}) collective-permute-start(bf16[144,576]{1,0:T(8,128)(2,1)S(1)} %get-tuple-element.61), channel_id=1, source_target_pairs={{0,128},{128,0},{1,129},{129,1},{2,130},{130,2},{3,131},{131,3},{4... | collective-permute-start | bytes 497672 | tf_op jit(solution)/shard_map/ppermute | solution.py:23
  23.6 13.3 %collective-permute-start.2 = (bf16[2,144,576]{2,1,0:T(8,128)(2,1)S(1)}, bf16[2,144,576]{2,1,0:T(8,128)(2,1)S(1)}, u32[]{:S(2)}, u32[]{:S(2)}) collective-permute-start(bf16[2,144,576]{2,1,0:T(8,128)(2,1)S(1)} %maximum_select_fusion), channel_id=1, source_target_pairs={{0,32},{32,64},{64,96},{96,0},{1,33},{33,65},{65,97},{97,1},{2,34}... | collective-permute-start | bytes 995336 | tf_op jit(solution)/shard_map/ppermute | solution.py:23
  25.2 12.5 %collective-permute-start.3 = (bf16[2,144,576]{2,1,0:T(8,128)(2,1)S(1)}, bf16[2,144,576]{2,1,0:T(8,128)(2,1)S(1)}, u32[]{:S(2)}, u32[]{:S(2)}) collective-permute-start(bf16[2,144,576]{2,1,0:T(8,128)(2,1)S(1)} %maximum_select_fusion), channel_id=1, source_target_pairs={{0,96},{32,0},{64,32},{96,64},{1,97},{33,1},{65,33},{97,65},{2,98}... | collective-permute-start | bytes 995336 | tf_op jit(solution)/shard_map/ppermute | solution.py:23
  27.0 15.6 %collective-permute-start.7 = (bf16[576,256]{1,0:T(8,128)(2,1)S(1)}, bf16[576,256]{1,0:T(8,128)(2,1)S(1)}, u32[]{:S(2)}, u32[]{:S(2)}) collective-permute-start(bf16[576,256]{1,0:T(8,128)(2,1)S(1)} %constant_dynamic-update-slice_fusion), channel_id=1, source_target_pairs={{0,1},{1,2},{2,3},{3,0},{4,5},{5,6},{6,7},{7,4},{8,9},{9,10},{10,1... | collective-permute-start | bytes 884744 | tf_op jit(solution)/shard_map/ppermute | solution.py:23
  36.9 4.8 %collective-permute-start.6 = (bf16[144,576]{1,0:T(8,128)(2,1)S(1)}, bf16[144,576]{1,0:T(8,128)(2,1)S(1)}, u32[]{:S(2)}, u32[]{:S(2)}) collective-permute-start(bf16[144,576]{1,0:T(8,128)(2,1)S(1)} %collective-permute-done.5), channel_id=1, source_target_pairs={{0,16},{16,0},{1,17},{17,1},{2,18},{18,2},{3,19},{19,3},{4,20},{20... | collective-permute-start | bytes 497672 | tf_op jit(solution)/shard_map/ppermute | solution.py:23
  36.9 17.0 %collective-permute-start.8 = (bf16[576,256]{1,0:T(8,128)(2,1)S(1)}, bf16[576,256]{1,0:T(8,128)(2,1)S(1)}, u32[]{:S(2)}, u32[]{:S(2)}) collective-permute-start(bf16[576,256]{1,0:T(8,128)(2,1)S(1)} %constant_dynamic-update-slice_fusion), channel_id=1, source_target_pairs={{0,3},{1,0},{2,1},{3,2},{4,7},{5,4},{6,5},{7,6},{8,11},{9,8},{10,9... | collective-permute-start | bytes 884744 | tf_op jit(solution)/shard_map/ppermute | solution.py:23
  37.7 19.3 %collective-permute-start.9 = (bf16[576,256]{1,0:T(8,128)(2,1)S(1)}, bf16[576,256]{1,0:T(8,128)(2,1)S(1)}, u32[]{:S(2)}, u32[]{:S(2)}) collective-permute-start(bf16[576,256]{1,0:T(8,128)(2,1)S(1)} %constant_dynamic-update-slice_fusion), channel_id=1, source_target_pairs={{0,2},{1,3},{2,0},{3,1},{4,6},{5,7},{6,4},{7,5},{8,10},{9,11},{10,... | collective-permute-start | bytes 884744 | tf_op jit(solution)/shard_map/ppermute | solution.py:23
  38.7 21.3 %collective-permute-start.10 = (bf16[2,144,576]{2,1,0:T(8,128)(2,1)S(1)}, bf16[2,144,576]{2,1,0:T(8,128)(2,1)S(1)}, u32[]{:S(2)}, u32[]{:S(2)}) collective-permute-start(bf16[2,144,576]{2,1,0:T(8,128)(2,1)S(1)} %maximum_select_fusion), channel_id=1, source_target_pairs={{0,64},{32,96},{64,0},{96,32},{1,65},{33,97},{65,1},{97,33},{2,66}... | collective-permute-start | bytes 995336 | tf_op jit(solution)/shard_map/ppermute | solution.py:23
  41.8 18.4 %collective-permute-start.12 = (bf16[2,144,576]{2,1,0:T(8,128)(2,1)S(1)}, bf16[2,144,576]{2,1,0:T(8,128)(2,1)S(1)}, u32[]{:S(2)}, u32[]{:S(2)}) collective-permute-start(bf16[2,144,576]{2,1,0:T(8,128)(2,1)S(1)} %maximum_select_fusion.1), channel_id=1, source_target_pairs={{0,32},{32,64},{64,96},{96,0},{1,33},{33,65},{65,97},{97,1},{2,34}... | collective-permute-start | bytes 995336 | tf_op jit(solution)/shard_map/ppermute | solution.py:23
  42.6 26.1 %collective-permute-start.13 = (bf16[2,144,576]{2,1,0:T(8,128)(2,1)S(1)}, bf16[2,144,576]{2,1,0:T(8,128)(2,1)S(1)}, u32[]{:S(2)}, u32[]{:S(2)}) collective-permute-start(bf16[2,144,576]{2,1,0:T(8,128)(2,1)S(1)} %maximum_select_fusion.1), channel_id=1, source_target_pairs={{0,96},{32,0},{64,32},{96,64},{1,97},{33,1},{65,33},{97,65},{2,98}... | collective-permute-start | bytes 995336 | tf_op jit(solution)/shard_map/ppermute | solution.py:23
  53.9 14.7 %collective-permute-start.14 = (bf16[2,144,576]{2,1,0:T(8,128)(2,1)S(1)}, bf16[2,144,576]{2,1,0:T(8,128)(2,1)S(1)}, u32[]{:S(2)}, u32[]{:S(2)}) collective-permute-start(bf16[2,144,576]{2,1,0:T(8,128)(2,1)S(1)} %maximum_select_fusion.1), channel_id=1, source_target_pairs={{0,64},{32,96},{64,0},{96,32},{1,65},{33,97},{65,1},{97,33},{2,66}... | collective-permute-start | bytes 995336 | tf_op jit(solution)/shard_map/ppermute | solution.py:23
  57.8 10.9 %collective-permute-start.11 = (bf16[2,64,576]{2,1,0:T(8,128)(2,1)S(1)}, bf16[2,64,576]{2,1,0:T(8,128)(2,1)S(1)}, u32[]{:S(2)}, u32[]{:S(2)}) collective-permute-start(bf16[2,64,576]{2,1,0:T(8,128)(2,1)S(1)} %get-tuple-element.69), channel_id=1, source_target_pairs={{0,128},{128,0},{1,129},{129,1},{2,130},{130,2},{3,131},{131,3},{4... | collective-permute-start | bytes 442376 | tf_op jit(solution)/shard_map/ppermute | solution.py:23
  79.0 10.9 %collective-permute-start.19 = (bf16[288,576]{1,0:T(8,128)(2,1)S(1)}, bf16[288,576]{1,0:T(8,128)(2,1)S(1)}, u32[]{:S(2)}, u32[]{:S(2)}) collective-permute-start(bf16[288,576]{1,0:T(8,128)(2,1)S(1)} %convolution_convert_fusion.5), channel_id=1, source_target_pairs={{0,96},{32,0},{64,32},{96,64},{1,97},{33,1},{65,33},{97,65},{2,98}... | collective-permute-start | bytes 995336 | tf_op jit(solution)/shard_map/ppermute | solution.py:23
  80.2 11.8 %collective-permute-start.18 = (bf16[288,576]{1,0:T(8,128)(2,1)S(1)}, bf16[288,576]{1,0:T(8,128)(2,1)S(1)}, u32[]{:S(2)}, u32[]{:S(2)}) collective-permute-start(bf16[288,576]{1,0:T(8,128)(2,1)S(1)} %convolution_convert_fusion.6), channel_id=1, source_target_pairs={{0,32},{32,64},{64,96},{96,0},{1,33},{33,65},{65,97},{97,1},{2,34}... | collective-permute-start | bytes 995336 | tf_op jit(solution)/shard_map/ppermute | solution.py:23
  92.0 10.1 %collective-permute-start.21 = (bf16[592,256]{1,0:T(8,128)(2,1)S(1)}, bf16[592,256]{1,0:T(8,128)(2,1)S(1)}, u32[]{:S(2)}, u32[]{:S(2)}) collective-permute-start(bf16[592,256]{1,0:T(8,128)(2,1)S(1)} %get-tuple-element.76), channel_id=1, source_target_pairs={{0,1},{1,2},{2,3},{3,0},{4,5},{5,6},{6,7},{7,4},{8,9},{9,10},{10,1... | collective-permute-start | bytes 909320 | tf_op jit(solution)/shard_map/ppermute | solution.py:23
  93.6 15.8 %collective-permute-start.22 = (bf16[592,256]{1,0:T(8,128)(2,1)S(1)}, bf16[592,256]{1,0:T(8,128)(2,1)S(1)}, u32[]{:S(2)}, u32[]{:S(2)}) collective-permute-start(bf16[592,256]{1,0:T(8,128)(2,1)S(1)} %get-tuple-element.77), channel_id=1, source_target_pairs={{0,3},{1,0},{2,1},{3,2},{4,7},{5,4},{6,5},{7,6},{8,11},{9,8},{10,9... | collective-permute-start | bytes 909320 | tf_op jit(solution)/shard_map/ppermute | solution.py:23
  94.0 15.3 %collective-permute-start.23 = (bf16[592,256]{1,0:T(8,128)(2,1)S(1)}, bf16[592,256]{1,0:T(8,128)(2,1)S(1)}, u32[]{:S(2)}, u32[]{:S(2)}) collective-permute-start(bf16[592,256]{1,0:T(8,128)(2,1)S(1)} %get-tuple-element.78), channel_id=1, source_target_pairs={{0,2},{1,3},{2,0},{3,1},{4,6},{5,7},{6,4},{7,5},{8,10},{9,11},{10,... | collective-permute-start | bytes 909320 | tf_op jit(solution)/shard_map/ppermute | solution.py:23
  96.4 13.2 %collective-permute-start.24 = (bf16[288,576]{1,0:T(8,128)(2,1)S(1)}, bf16[288,576]{1,0:T(8,128)(2,1)S(1)}, u32[]{:S(2)}, u32[]{:S(2)}) collective-permute-start(bf16[288,576]{1,0:T(8,128)(2,1)S(1)} %convolution_convert_fusion.4), channel_id=1, source_target_pairs={{0,64},{32,96},{64,0},{96,32},{1,65},{33,97},{65,1},{97,33},{2,66}... | collective-permute-start | bytes 995336 | tf_op jit(solution)/shard_map/ppermute | solution.py:23
  110.1 7.2 %collective-permute-start.25 = (bf16[160,256]{1,0:T(8,128)(2,1)S(1)}, bf16[160,256]{1,0:T(8,128)(2,1)S(1)}, u32[]{:S(2)}, u32[]{:S(2)}) collective-permute-start(bf16[160,256]{1,0:T(8,128)(2,1)S(1)} %get-tuple-element.138), channel_id=1, source_target_pairs={{0,4},{4,8},{8,12},{12,0},{1,5},{5,9},{9,13},{13,1},{2,6},{6,10},{... | collective-permute-start | bytes 245768 | tf_op jit(solution)/shard_map/ppermute | solution.py:23
  110.2 7.2 %collective-permute-start.26 = (bf16[160,256]{1,0:T(8,128)(2,1)S(1)}, bf16[160,256]{1,0:T(8,128)(2,1)S(1)}, u32[]{:S(2)}, u32[]{:S(2)}) collective-permute-start(bf16[160,256]{1,0:T(8,128)(2,1)S(1)} %get-tuple-element.139), channel_id=1, source_target_pairs={{0,12},{4,0},{8,4},{12,8},{1,13},{5,1},{9,5},{13,9},{2,14},{6,2},{... | collective-permute-start | bytes 245768 | tf_op jit(solution)/shard_map/ppermute | solution.py:23
  114.0 22.7 %collective-permute-start.27 = (bf16[160,256]{1,0:T(8,128)(2,1)S(1)}, bf16[160,256]{1,0:T(8,128)(2,1)S(1)}, u32[]{:S(2)}, u32[]{:S(2)}) collective-permute-start(bf16[160,256]{1,0:T(8,128)(2,1)S(1)} %get-tuple-element.140), channel_id=1, source_target_pairs={{0,8},{4,12},{8,0},{12,4},{1,9},{5,13},{9,1},{13,5},{2,10},{6,14},... | collective-permute-start | bytes 245768 | tf_op jit(solution)/shard_map/ppermute | solution.py:23
  114.0 23.1 %collective-permute-start.28 = (bf16[288,576]{1,0:T(8,128)(2,1)S(1)}, bf16[288,576]{1,0:T(8,128)(2,1)S(1)}, u32[]{:S(2)}, u32[]{:S(2)}) collective-permute-start(bf16[288,576]{1,0:T(8,128)(2,1)S(1)} %convolution_convert_fusion.3), channel_id=1, source_target_pairs={{0,32},{32,64},{64,96},{96,0},{1,33},{33,65},{65,97},{97,1},{2,34}... | collective-permute-start | bytes 995336 | tf_op jit(solution)/shard_map/ppermute | solution.py:23
  114.0 23.1 %collective-permute-start.29 = (bf16[288,576]{1,0:T(8,128)(2,1)S(1)}, bf16[288,576]{1,0:T(8,128)(2,1)S(1)}, u32[]{:S(2)}, u32[]{:S(2)}) collective-permute-start(bf16[288,576]{1,0:T(8,128)(2,1)S(1)} %convolution_convert_fusion.2), channel_id=1, source_target_pairs={{0,96},{32,0},{64,32},{96,64},{1,97},{33,1},{65,33},{97,65},{2,98}... | collective-permute-start | bytes 995336 | tf_op jit(solution)/shard_map/ppermute | solution.py:23
  117.3 25.8 %collective-permute-start.35 = (bf16[288,576]{1,0:T(8,128)(2,1)S(1)}, bf16[288,576]{1,0:T(8,128)(2,1)S(1)}, u32[]{:S(2)}, u32[]{:S(2)}) collective-permute-start(bf16[288,576]{1,0:T(8,128)(2,1)S(1)} %convolution_convert_fusion.1), channel_id=1, source_target_pairs={{0,64},{32,96},{64,0},{96,32},{1,65},{33,97},{65,1},{97,33},{2,66}... | collective-permute-start | bytes 995336 | tf_op jit(solution)/shard_map/ppermute | solution.py:23
  117.4 26.1 %collective-permute-start.37 = (bf16[144,576]{1,0:T(8,128)(2,1)S(1)}, bf16[144,576]{1,0:T(8,128)(2,1)S(1)}, u32[]{:S(2)}, u32[]{:S(2)}) collective-permute-start(bf16[144,576]{1,0:T(8,128)(2,1)S(1)} %get-tuple-element.116), channel_id=1, source_target_pairs={{0,128},{128,0},{1,129},{129,1},{2,130},{130,2},{3,131},{131,3},{4... | collective-permute-start | bytes 497672 | tf_op jit(solution)/shard_map/ppermute | solution.py:23
  136.7 20.0 %collective-permute-start.36 = (bf16[144,576]{1,0:T(8,128)(2,1)S(1)}, bf16[144,576]{1,0:T(8,128)(2,1)S(1)}, u32[]{:S(2)}, u32[]{:S(2)}) collective-permute-start(bf16[144,576]{1,0:T(8,128)(2,1)S(1)} %get-tuple-element.117), channel_id=1, source_target_pairs={{0,128},{128,0},{1,129},{129,1},{2,130},{130,2},{3,131},{131,3},{4... | collective-permute-start | bytes 497672 | tf_op jit(solution)/shard_map/ppermute | solution.py:23
  137.0 9.5 %collective-permute-start.30 = (bf16[160,128]{1,0:T(8,128)(2,1)S(1)}, bf16[160,128]{1,0:T(8,128)(2,1)S(1)}, u32[]{:S(2)}, u32[]{:S(2)}) collective-permute-start(bf16[160,128]{1,0:T(8,128)(2,1)S(1)} %pad_maximum_fusion.10), channel_id=1, source_target_pairs={{0,128},{128,0},{1,129},{129,1},{2,130},{130,2},{3,131},{131,3},{4... | collective-permute-start | bytes 122888 | tf_op jit(solution)/shard_map/ppermute | solution.py:23
  143.6 13.1 %collective-permute-start.38 = (bf16[2,144,576]{2,1,0:T(8,128)(2,1)S(1)}, bf16[2,144,576]{2,1,0:T(8,128)(2,1)S(1)}, u32[]{:S(2)}, u32[]{:S(2)}) collective-permute-start(bf16[2,144,576]{2,1,0:T(8,128)(2,1)S(1)} %pad_maximum_fusion.6), channel_id=1, source_target_pairs={{0,16},{16,0},{1,17},{17,1},{2,18},{18,2},{3,19},{19,3},{4,20},{20... | collective-permute-start | bytes 995336 | tf_op jit(solution)/shard_map/ppermute | solution.py:23
  151.1 5.1 %collective-permute-start.34 = (f32[144]{0:T(256)S(1)}, f32[144]{0:T(256)S(1)}, u32[]{:S(2)}, u32[]{:S(2)}) collective-permute-start(f32[144]{0:T(256)S(1)} %add.232), channel_id=1, source_target_pairs={{0,64},{32,96},{64,0},{96,32},{1,65},{33,97},{65,1},{97,33},{2,66}... | collective-permute-start | bytes 1736 | tf_op jit(solution)/shard_map/ppermute | solution.py:23
  (12 other events, 75.3 us)
where the time goes:
time: 161 us; the launch traced here: 160 us
  waiting for transfers between devices  80.7 us (50%)
  starting transfers between devices  57 us (35%)
  matrix products  7.48 us (5%)
  Pallas kernels  6.27 us (4%)
  other arithmetic  4.1 us (3%)
  local copies, waits for them, and re-layouts  3.45 us (2%)
    ppermute x39, waiting for transfers between devices, turned(): return lax.ppermute(array, axis, [(i, (i + by) % n) for i in range(n)])  80.7 us
    ppermute x39, starting transfers between devices, turned(): return lax.ppermute(array, axis, [(i, (i + by) % n) for i in range(n)])  57 us
    pallas_call x2, Pallas kernels, packed(): pl.pallas_call(functools.partial(pack_kernel, main, rest, aways), out_sha...  4.05 us
  transfers between devices with their start and end apart: 39, of which 15 were waited for; matrix products, arithmetic and copies ran while one was open for 5% of the time, Pallas kernels for 1%

commit v1 on v0

--- a/solution.py
+++ b/solution.py
@@ -207,7 +207,8 @@
     near_got = [turned(near, "x", by) for by in steps]
 
     both = jnp.concatenate([own_t, far_t], axis=1)
-    section_got = [turned(both, "sec", by) for by in steps]
+    copies = jnp.broadcast_to(both, (4, *both.shape))
+    inputs = lax.all_to_all(copies, "sec", 0, 0, tiled=True)
 
     near_got[0], near_got[1], backs, late_first = barrier(
         (near_got[0], near_got[1], backs, first_core)
@@ -215,13 +216,7 @@
     away_other = swapped(away_other, "core")
     backs = swapped(backs, "zh")
     away = ordered(away_own, away_other, late_first)
-    late = {}
-    away, late[0], late[1], late[2], late[3] = barrier((away, *(sec_to[by] for by in range(4))))
     away_got = [turned(away, "x", by) for by in steps]
-
-    inputs = jnp.zeros((4, *both.shape), BF16)
-    for by, piece in zip((0, 3, 1, 2), (both, *section_got)):
-        inputs = put(inputs, piece, late[by])
     inputs = inputs.reshape(features, 2 * group)
     wide = inputs.astype(F32)
     inv_rms = lax.rsqrt(jnp.mean(wide * wide, axis=0) + EPS)
@@ -258,14 +253,21 @@
 
     by_rows = normed.reshape(2, 4, 2 * rows, 4 * group)
 
-    def part(zplace, xplace):
-        return jnp.dot(as_block(by_rows, zplace, xplace), d_both, preferred_element_type=F32)
-
-    away_parts = [part(far_zh, x_to[by]).astype(BF16) for by in steps]
-    near_parts = [part(zh, x_to[by]).astype(BF16) for by in steps]
-    away_got = [turned(away_parts[k], "x", steps[k]) for k in (0, 1)]
-
-    got = swapped(d_normed(d_both[2 * group :]).astype(BF16), "core")
+    def parts(zplace):
+        mine = as_block(by_rows, zplace)
+        out = [jnp.dot(mine[k], d_both, preferred_element_type=F32) for k in range(4)]
+        return jnp.stack([o.astype(BF16) for o in out])
+
+    def summed(parts_of_x):
+        got = lax.all_to_all(parts_of_x, "x", 0, 0, tiled=True)
+        return sum(got[k].astype(F32) for k in range(4)).astype(BF16)
+
+    away_parts, near_parts = parts(far_zh), parts(zh)
+
+    theirs = d_normed(d_both[2 * group :]).astype(BF16)
+    theirs, away_parts = barrier((theirs, away_parts))
+    got = swapped(theirs, "core")
+    g_away = summed(away_parts)
     row = row_part[: 2 * group] + swapped(row_part[2 * group :], "core")
     mine = d_normed(d_both[: 2 * group]) + got.astype(F32)
     mine = mine.reshape(4, 4, own_rows, 2 * group)
@@ -278,17 +280,14 @@
         return block.reshape(4 * own_rows, 2 * group)
 
     sends = [with_rows(section(sec_to[by]), row) for by in steps]
-    *away_got, away_parts[2], sends[0], sends[1], sends[2] = barrier(
-        (*away_got, away_parts[2], *sends)
-    )
-    away_got.append(turned(away_parts[2], "x", 2))
+    g_away, near_parts, *sends = barrier((g_away, near_parts, *sends))
     got = [turned(s, "sec", by) for s, by in zip(sends, steps)]
-    away_got[2], *near_parts = barrier((away_got[2], *near_parts))
-    near_got = [turned(p, "x", by) for p, by in zip(near_parts, steps)]
-    g_away = part(far_zh, x) + sum(g.astype(F32) for g in away_got)
-    g_away = g_away.astype(BF16).reshape(2, rows, -1)
+    g_away = g_away.reshape(2, rows, -1)
     late = {}
-    g_away, late[1], late[3], late[2] = barrier((g_away, *(tp_to[by] for by in steps)))
+    g_near, late[1], late[3], late[2] = barrier(
+        (summed(near_parts), *(tp_to[by] for by in steps))
+    )
+    g_near = g_near.reshape(2, rows, -1)
     away_keep = swapped(as_block(g_away, core), "zh")
     away_give = swapped(as_block(g_away, other_core), "zh")
 
@@ -306,10 +305,8 @@
     gain_part = jnp.sum(total * own_inputs * inv_rms, axis=1)
     gain_rows = jnp.pad(gain_part, (0, 2 * group - own_rows)).reshape(2, group)
     send = with_rows(total[:, group:], row[group:], gain_rows[0], gain_rows[1])
-    send, near_got[0], near_got[1], late_zh = barrier((send, near_got[0], near_got[1], zh))
+    send, away_give = barrier((send, away_give))
     got = swapped(send, "zh")
-    g_near = part(late_zh, x) + sum(g.astype(F32) for g in near_got)
-    g_near = g_near.astype(BF16).reshape(2, rows, -1)
     give = swapped(jnp.stack([as_block(g_near, other_core), away_give]), "core")
     grad_gain = gain_part + jnp.concatenate([row_of(got, 1), row_of(got, 2)])[:own_rows]
     grad_gain = grad_gain + swapped(grad_gain, "core")

time: 161 us -> 169 us (1.050)
  the two profiles are of different devices: /device:TPU:24 before, /device:TPU:1 now
where the time goes in v1:
time: 169 us; the launch traced here: 168 us
  starting transfers between devices  75.7 us (45%)
  waiting for transfers between devices  32.1 us (19%)
  other arithmetic  22.1 us (13%)
  local copies, waits for them, and re-layouts  16.5 us (10%)
  matrix products  13.6 us (8%)
  Pallas kernels  6.23 us (4%)
    ppermute x30, starting transfers between devices, turned(): return lax.ppermute(array, axis, [(i, (i + by) % n) for i in range(n)])  63.1 us
    all_to_all x2, waiting for transfers between devices, summed(): got = lax.all_to_all(parts_of_x, 'x', 0, 0, tiled=True)  21.2 us
    ppermute x30, waiting for transfers between devices, turned(): return lax.ppermute(array, axis, [(i, (i + by) % n) for i in range(n)])  10.9 us
    all_to_all x2, starting transfers between devices, summed(): got = lax.all_to_all(parts_of_x, 'x', 0, 0, tiled=True)  8.34 us
    dynamic_update_slice x7, local copies, waits for them, and re-layouts, put(): return lax.dynamic_update_slice(array, part, (*lead, *zeros))  7.25 us
    dot_general x8, matrix products, parts(): jnp.dot(mine[k], d_both, preferred_element_type=F32)  6.04 us
    dot_general x2, matrix products, d_normed(): lax.dot_general(full, d, (((1,), (1,)), ((), ())), preferred_element_type...  5.43 us
    all_to_all x1, starting transfers between devices, shards(): inputs = lax.all_to_all(copies, 'sec', 0, 0, tiled=True)  4.26 us
  transfers between devices with their start and end apart: 33, of which 11 were waited for; matrix products, arithmetic and copies ran while one was open for 21% of the time, Pallas kernels for 2%

profile of v1, /device:TPU:1, one launch (start us, length us, event | category | flops | bytes accessed | tf_op | source)
XLA Modules:
  0.0 167.5 jit_solution(17124141654886152432)
XLA Ops:
  0.6 7.8 %collective-permute-start.1 = (bf16[576,128]{1,0:T(8,128)(2,1)}, bf16[576,128]{1,0:T(8,128)(2,1)S(1)}, u32[]{:S(2)}, u32[]{:S(2)}) collective-permute-start(bf16[576,128]{1,0:T(8,128)(2,1)} %bitcast.150), channel_id=1, source_target_pairs={{0,128},{128,0},{1,129},{129,1},{2,130},{130,2},{3,131},{131,3},{4... | collective-permute-start | bytes 442376 | tf_op jit(solution)/shard_map/ppermute | solution.py:23
  8.5 2.0 %pack.2 = (bf16[208,576]{1,0:T(8,128)(2,1)S(1)}, bf16[208,576]{1,0:T(8,128)(2,1)S(1)}) custom-call(bf16[144,1152]{1,0:T(8,128)(2,1)} %gate_ref.3, bf16[144,1152]{1,0:T(8,128)(2,1)} %up_ref.3, bf16[128,1152]{1,0:T(8,128)(2,1)} %back_ref.2), custom_call_target="tpu_custom_call" | custom-call | tf_op jit(solution)/shard_map/pack/pallas_call | solution.py:91
  11.5 2.0 %pack.3 = (bf16[144,576]{1,0:T(8,128)(2,1)S(1)}, bf16[144,576]{1,0:T(8,128)(2,1)S(1)}, bf16[2,64,576]{2,1,0:T(8,128)(2,1)S(1)}) custom-call(bf16[144,1152]{1,0:T(8,128)(2,1)} %gate_ref.3, bf16[144,1152]{1,0:T(8,128)(2,1)} %up_ref.3, bf16[128,1152]{1,0:T(8,128)(2,1)} %back_ref.2), custom_call_target="tpu_custom_call" | custom-call | tf_op jit(solution)/shard_map/pack/pallas_call | solution.py:91
  18.1 5.2 %collective-permute-start.6 = (bf16[144,576]{1,0:T(8,128)(2,1)S(1)}, bf16[144,576]{1,0:T(8,128)(2,1)}, u32[]{:S(2)}, u32[]{:S(2)}) collective-permute-start(bf16[144,576]{1,0:T(8,128)(2,1)S(1)} %get-tuple-element.53), channel_id=1, source_target_pairs={{0,128},{128,0},{1,129},{129,1},{2,130},{130,2},{3,131},{131,3},{4... | collective-permute-start | bytes 497672 | tf_op jit(solution)/shard_map/ppermute | solution.py:23
  25.4 1.5 collective-permute-start.3
  26.8 1.5 collective-permute-start.4
  29.5 4.3 %all-to-all-start = ((bf16[4,576,256]{2,1,0:T(8,128)(2,1)}), bf16[4,576,256]{2,1,0:T(8,128)(2,1)}, u32[]{:S(2)}, u32[]{:S(2)}) async-start(bf16[4,576,256]{2,1,0:T(8,128)(2,1)} %broadcast_in_dim.113), calls=%async_computation | async-start | bytes 2359296 | tf_op jit(solution)/shard_map/all_to_all | solution.py:211
  37.5 1.5 fusion.67
  39.1 1.9 %maximum_select_fusion.2 = bf16[2,144,576]{2,1,0:T(8,128)(2,1)} fusion(bf16[1,144,576]{2,1,0:T(8,128)(2,1)S(1)} %bitcast.147, bf16[1,144,576]{2,1,0:T(8,128)(2,1)} %bitcast.10, pred[]{:T(512)S(6)} %eq.63), kind=kLoop, calls=%fused_computation.52 | loop fusion | flops 497664 | bytes 663553 | tf_op jit(solution)/shard_map/jit(_where)/select_n | solution.py:148
  41.4 2.3 %collective-permute-start.10 = (bf16[2,144,576]{2,1,0:T(8,128)(2,1)}, bf16[2,144,576]{2,1,0:T(8,128)(2,1)}, u32[]{:S(2)}, u32[]{:S(2)}) collective-permute-start(bf16[2,144,576]{2,1,0:T(8,128)(2,1)} %maximum_select_fusion.2), channel_id=1, source_target_pairs={{0,96},{32,0},{64,32},{96,64},{1,97},{33,1},{65,33},{97,65},{2,98}... | collective-permute-start | bytes 995336 | tf_op jit(solution)/shard_map/ppermute | solution.py:23
  44.4 3.8 %collective-permute-start.8 = (bf16[2,64,576]{2,1,0:T(8,128)(2,1)S(1)}, bf16[2,64,576]{2,1,0:T(8,128)(2,1)S(1)}, u32[]{:S(2)}, u32[]{:S(2)}) collective-permute-start(bf16[2,64,576]{2,1,0:T(8,128)(2,1)S(1)} %get-tuple-element.54), channel_id=1, source_target_pairs={{0,128},{128,0},{1,129},{129,1},{2,130},{130,2},{3,131},{131,3},{4... | collective-permute-start | bytes 442376 | tf_op jit(solution)/shard_map/ppermute | solution.py:23
  52.5 1.6 multiply_reduce_fusion
  54.1 1.7 %multiply_convert_fusion = bf16[2304,256]{1,0:T(8,128)(2,1)S(1)} fusion(f32[2304]{0:T(1024)S(1)} %copy-done.11, f32[256]{0:T(256)S(1)} %add_rsqrt_fusion, bf16[4,576,256]{2,1,0:T(8,128)(2,1)} %all-to-all-done), kind=kLoop, calls=%fused_computation.2 | loop fusion | flops 2359296 | bytes 2369536 | tf_op jit(solution)/shard_map/convert_element_type | solution.py:223
  55.9 5.8 %collective-permute-start.13 = (bf16[2304,256]{1,0:T(8,128)(2,1)S(1)}, bf16[2304,256]{1,0:T(8,128)(2,1)S(1)}, u32[]{:S(2)}, u32[]{:S(2)}) collective-permute-start(bf16[2304,256]{1,0:T(8,128)(2,1)S(1)} %multiply_convert_fusion), channel_id=1, source_target_pairs={{0,16},{16,0},{1,17},{17,1},{2,18},{18,2},{3,19},{19,3},{4,20},{20... | collective-permute-start | bytes 3538952 | tf_op jit(solution)/shard_map/ppermute | solution.py:23
  66.7 2.1 %fusion.75 = f32[512,576]{1,0:T(8,128)S(1)} fusion(bf16[2304,512]{1,0:T(8,128)(2,1)S(1)} %constant_dynamic-update-slice_fusion, bf16[2304,576]{1,0:T(8,128)(2,1)S(1)} %bitcast.126), kind=kOutput, calls=%fused_computation.192 | convolution fusion | flops 1358954496 | bytes 6193152 | tf_op jit(solution)/shard_map/dot_general | solution.py:242
  70.8 2.2 %convolution_convert_fusion = bf16[2304,256]{1,0:T(8,128)(2,1)} fusion(bf16[2304,576]{1,0:T(8,128)(2,1)S(1)} %bitcast.128, bf16[512,576]{1,0:T(8,128)(2,1)S(1)} %pad_maximum_fusion.4), kind=kOutput, calls=%fused_computation | convolution fusion | flops 680067072 | bytes 4456448 | tf_op jit(solution)/shard_map/dot_general | solution.py:252
  76.4 3.8 %all-to-all-start.1 = ((bf16[4,288,576]{2,1,0:T(8,128)(2,1)}), bf16[4,288,576]{2,1,0:T(8,128)(2,1)S(1)}, u32[]{:S(2)}, u32[]{:S(2)}) async-start(bf16[4,288,576]{2,1,0:T(8,128)(2,1)} %pad_maximum_fusion), calls=%async_computation.1 | async-start | bytes 2949120 | tf_op jit(solution)/shard_map/all_to_all | solution.py:262
  86.4 13.0 %all-to-all-done.1 = bf16[4,288,576]{2,1,0:T(8,128)(2,1)S(1)} async-done(((bf16[4,288,576]{2,1,0:T(8,128)(2,1)}), bf16[4,288,576]{2,1,0:T(8,128)(2,1)S(1)}, u32[]{:S(2)}, u32[]{:S(2)}) %all-to-all-start.1) | async-done | bytes 1327136 | tf_op jit(solution)/shard_map/all_to_all | solution.py:262
  99.7 3.3 %convert_add_fusion = f32[2304,256]{1,0:T(8,128)S(1)} fusion(bf16[2304,256]{1,0:T(8,128)(2,1)} %collective-permute-done.14, bf16[2304,576]{1,0:T(8,128)(2,1)} %bitcast.127, bf16[512,576]{1,0:T(8,128)(2,1)S(1)} %pad_maximum_fusion.4), kind=kOutput, calls=%fused_computation.1 | convolution fusion | flops 680656896 | bytes 6520832 | tf_op jit(solution)/shard_map/dot_general | solution.py:252
  103.8 3.3 %collective-permute-start.18 = (bf16[592,256]{1,0:T(8,128)(2,1)}, bf16[592,256]{1,0:T(8,128)(2,1)}, u32[]{:S(2)}, u32[]{:S(2)}) collective-permute-start(bf16[592,256]{1,0:T(8,128)(2,1)} %get-tuple-element.65), channel_id=1, source_target_pairs={{0,2},{1,3},{2,0},{3,1},{4,6},{5,7},{6,4},{7,5},{8,10},{9,11},{10,... | collective-permute-start | bytes 909320 | tf_op jit(solution)/shard_map/ppermute | solution.py:23
  109.5 4.6 %all-to-all-start.2 = ((bf16[4,288,576]{2,1,0:T(8,128)(2,1)}), bf16[4,288,576]{2,1,0:T(8,128)(2,1)}, u32[]{:S(2)}, u32[]{:S(2)}) async-start(bf16[4,288,576]{2,1,0:T(8,128)(2,1)} %pad_maximum_fusion.1), calls=%async_computation.2 | async-start | bytes 2949120 | tf_op jit(solution)/shard_map/all_to_all | solution.py:262
  114.1 3.6 %collective-permute-start.22 = (bf16[144,576]{1,0:T(8,128)(2,1)S(1)}, bf16[144,576]{1,0:T(8,128)(2,1)S(1)}, u32[]{:S(2)}, u32[]{:S(2)}) collective-permute-start(bf16[144,576]{1,0:T(8,128)(2,1)S(1)} %get-tuple-element.97), channel_id=1, source_target_pairs={{0,128},{128,0},{1,129},{129,1},{2,130},{130,2},{3,131},{131,3},{4... | collective-permute-start | bytes 497672 | tf_op jit(solution)/shard_map/ppermute | solution.py:23
  117.8 1.8 %collective-permute-start.28 = (bf16[144,576]{1,0:T(8,128)(2,1)S(1)}, bf16[144,576]{1,0:T(8,128)(2,1)S(1)}, u32[]{:S(2)}, u32[]{:S(2)}) collective-permute-start(bf16[144,576]{1,0:T(8,128)(2,1)S(1)} %get-tuple-element.96), channel_id=1, source_target_pairs={{0,128},{128,0},{1,129},{129,1},{2,130},{130,2},{3,131},{131,3},{4... | collective-permute-start | bytes 497672 | tf_op jit(solution)/shard_map/ppermute | solution.py:23
  123.4 8.2 %all-to-all-done.2 = bf16[4,288,576]{2,1,0:T(8,128)(2,1)} async-done(((bf16[4,288,576]{2,1,0:T(8,128)(2,1)}), bf16[4,288,576]{2,1,0:T(8,128)(2,1)}, u32[]{:S(2)}, u32[]{:S(2)}) %all-to-all-start.2) | async-done | bytes 1327136 | tf_op jit(solution)/shard_map/all_to_all | solution.py:262
  131.6 1.5 fusion.17
  133.2 4.4 %collective-permute-start.21 = (bf16[160,256]{1,0:T(8,128)(2,1)S(1)}, bf16[160,256]{1,0:T(8,128)(2,1)S(1)}, u32[]{:S(2)}, u32[]{:S(2)}) collective-permute-start(bf16[160,256]{1,0:T(8,128)(2,1)S(1)} %get-tuple-element.120), channel_id=1, source_target_pairs={{0,8},{4,12},{8,0},{12,4},{1,9},{5,13},{9,1},{13,5},{2,10},{6,14},... | collective-permute-start | bytes 245768 | tf_op jit(solution)/shard_map/ppermute | solution.py:23
  140.9 3.7 %collective-permute-done.19 = bf16[160,256]{1,0:T(8,128)(2,1)S(1)} collective-permute-done((bf16[160,256]{1,0:T(8,128)(2,1)S(1)}, bf16[160,256]{1,0:T(8,128)(2,1)S(1)}, u32[]{:S(2)}, u32[]{:S(2)}) %collective-permute-start.19) | collective-permute-done | bytes 81952 | tf_op jit(solution)/shard_map/ppermute | solution.py:23
  146.1 4.4 %collective-permute-start.29 = (bf16[2,144,576]{2,1,0:T(8,128)(2,1)S(1)}, bf16[2,144,576]{2,1,0:T(8,128)(2,1)S(1)}, u32[]{:S(2)}, u32[]{:S(2)}) collective-permute-start(bf16[2,144,576]{2,1,0:T(8,128)(2,1)S(1)} %pad_maximum_fusion.8), channel_id=1, source_target_pairs={{0,16},{16,0},{1,17},{17,1},{2,18},{18,2},{3,19},{19,3},{4,20},{20... | collective-permute-start | bytes 995336 | tf_op jit(solution)/shard_map/ppermute | solution.py:23
  150.4 2.3 %collective-permute-done.23 = bf16[160,128]{1,0:T(8,128)(2,1)S(1)} collective-permute-done((bf16[160,128]{1,0:T(8,128)(2,1)S(1)}, bf16[160,128]{1,0:T(8,128)(2,1)S(1)}, u32[]{:S(2)}, u32[]{:S(2)}) %collective-permute-start.23) | collective-permute-done | bytes 40992 | tf_op jit(solution)/shard_map/ppermute | solution.py:23
  152.8 5.5 %collective-permute-start.24 = (f32[144]{0:T(256)S(1)}, f32[144]{0:T(256)S(1)}, u32[]{:S(2)}, u32[]{:S(2)}) collective-permute-start(f32[144]{0:T(256)S(1)} %slice_add_fusion.1), channel_id=1, source_target_pairs={{0,16},{16,0},{1,17},{17,1},{2,18},{18,2},{3,19},{19,3},{4,20},{20... | collective-permute-start | bytes 1736 | tf_op jit(solution)/shard_map/ppermute | solution.py:23
  160.5 1.9 %collective-permute-start.26 = (f32[144]{0:T(256)S(1)}, f32[144]{0:T(256)S(1)}, u32[]{:S(2)}, u32[]{:S(2)}) collective-permute-start(f32[144]{0:T(256)S(1)} %add.247), channel_id=1, source_target_pairs={{0,96},{32,0},{64,32},{96,64},{1,97},{33,1},{65,33},{97,65},{2,98}... | collective-permute-start | bytes 1736 | tf_op jit(solution)/shard_map/ppermute | solution.py:23
  165.3 2.2 %join.1 = (bf16[144,1152]{1,0:T(8,128)(2,1)}, bf16[144,1152]{1,0:T(8,128)(2,1)}) custom-call(bf16[2,144,576]{2,1,0:T(8,128)(2,1)} %bitcast.140, bf16[144,576]{1,0:T(8,128)(2,1)} %copy-done.7, bf16[2,144,576]{2,1,0:T(8,128)(2,1)} %copy-done.5), custom_call_target="tpu_custom_call" | custom-call | tf_op jit(solution)/shard_map/join/pallas_call | solution.py:124
  (170 shorter events, 51.6 us)
Async XLA Ops:
  0.6 17.5 %collective-permute-start.1 = (bf16[576,128]{1,0:T(8,128)(2,1)}, bf16[576,128]{1,0:T(8,128)(2,1)S(1)}, u32[]{:S(2)}, u32[]{:S(2)}) collective-permute-start(bf16[576,128]{1,0:T(8,128)(2,1)} %bitcast.150), channel_id=1, source_target_pairs={{0,128},{128,0},{1,129},{129,1},{2,130},{130,2},{3,131},{131,3},{4... | collective-permute-start | bytes 442376 | tf_op jit(solution)/shard_map/ppermute | solution.py:23
  10.5 12.8 %collective-permute-start = (bf16[208,576]{1,0:T(8,128)(2,1)S(1)}, bf16[208,576]{1,0:T(8,128)(2,1)S(1)}, u32[]{:S(2)}, u32[]{:S(2)}) collective-permute-start(bf16[208,576]{1,0:T(8,128)(2,1)S(1)} %get-tuple-element.42), channel_id=1, source_target_pairs={{0,16},{16,0},{1,17},{17,1},{2,18},{18,2},{3,19},{19,3},{4,20},{20... | collective-permute-start | bytes 718856 | tf_op jit(solution)/shard_map/ppermute | solution.py:23
  13.5 25.5 %collective-permute-start.5 = (bf16[144,576]{1,0:T(8,128)(2,1)S(1)}, bf16[144,576]{1,0:T(8,128)(2,1)}, u32[]{:S(2)}, u32[]{:S(2)}) collective-permute-start(bf16[144,576]{1,0:T(8,128)(2,1)S(1)} %get-tuple-element.52), channel_id=1, source_target_pairs={{0,128},{128,0},{1,129},{129,1},{2,130},{130,2},{3,131},{131,3},{4... | collective-permute-start | bytes 497672 | tf_op jit(solution)/shard_map/ppermute | solution.py:23
  18.1 18.1 %collective-permute-start.6 = (bf16[144,576]{1,0:T(8,128)(2,1)S(1)}, bf16[144,576]{1,0:T(8,128)(2,1)}, u32[]{:S(2)}, u32[]{:S(2)}) collective-permute-start(bf16[144,576]{1,0:T(8,128)(2,1)S(1)} %get-tuple-element.53), channel_id=1, source_target_pairs={{0,128},{128,0},{1,129},{129,1},{2,130},{130,2},{3,131},{131,3},{4... | collective-permute-start | bytes 497672 | tf_op jit(solution)/shard_map/ppermute | solution.py:23
  24.2 14.9 %collective-permute-start.2 = (bf16[2,144,576]{2,1,0:T(8,128)(2,1)}, bf16[2,144,576]{2,1,0:T(8,128)(2,1)}, u32[]{:S(2)}, u32[]{:S(2)}) collective-permute-start(bf16[2,144,576]{2,1,0:T(8,128)(2,1)} %maximum_select_fusion), channel_id=1, source_target_pairs={{0,32},{32,64},{64,96},{96,0},{1,33},{33,65},{65,97},{97,1},{2,34}... | collective-permute-start | bytes 995336 | tf_op jit(solution)/shard_map/ppermute | solution.py:23
  25.4 13.7 %collective-permute-start.3 = (bf16[2,144,576]{2,1,0:T(8,128)(2,1)}, bf16[2,144,576]{2,1,0:T(8,128)(2,1)}, u32[]{:S(2)}, u32[]{:S(2)}) collective-permute-start(bf16[2,144,576]{2,1,0:T(8,128)(2,1)} %maximum_select_fusion), channel_id=1, source_target_pairs={{0,96},{32,0},{64,32},{96,64},{1,97},{33,1},{65,33},{97,65},{2,98}... | collective-permute-start | bytes 995336 | tf_op jit(solution)/shard_map/ppermute | solution.py:23
  26.8 23.4 %collective-permute-start.4 = (bf16[2,144,576]{2,1,0:T(8,128)(2,1)}, bf16[2,144,576]{2,1,0:T(8,128)(2,1)}, u32[]{:S(2)}, u32[]{:S(2)}) collective-permute-start(bf16[2,144,576]{2,1,0:T(8,128)(2,1)} %maximum_select_fusion), channel_id=1, source_target_pairs={{0,64},{32,96},{64,0},{96,32},{1,65},{33,97},{65,1},{97,33},{2,66}... | collective-permute-start | bytes 995336 | tf_op jit(solution)/shard_map/ppermute | solution.py:23
  29.5 22.9 %all-to-all-start = ((bf16[4,576,256]{2,1,0:T(8,128)(2,1)}), bf16[4,576,256]{2,1,0:T(8,128)(2,1)}, u32[]{:S(2)}, u32[]{:S(2)}) async-start(bf16[4,576,256]{2,1,0:T(8,128)(2,1)} %broadcast_in_dim.113), calls=%async_computation | async-start | bytes 2359296 | tf_op jit(solution)/shard_map/all_to_all | solution.py:211
  40.9 14.9 %collective-permute-start.9 = (bf16[2,144,576]{2,1,0:T(8,128)(2,1)}, bf16[2,144,576]{2,1,0:T(8,128)(2,1)}, u32[]{:S(2)}, u32[]{:S(2)}) collective-permute-start(bf16[2,144,576]{2,1,0:T(8,128)(2,1)} %maximum_select_fusion.2), channel_id=1, source_target_pairs={{0,32},{32,64},{64,96},{96,0},{1,33},{33,65},{65,97},{97,1},{2,34}... | collective-permute-start | bytes 995336 | tf_op jit(solution)/shard_map/ppermute | solution.py:23
  41.4 14.5 %collective-permute-start.10 = (bf16[2,144,576]{2,1,0:T(8,128)(2,1)}, bf16[2,144,576]{2,1,0:T(8,128)(2,1)}, u32[]{:S(2)}, u32[]{:S(2)}) collective-permute-start(bf16[2,144,576]{2,1,0:T(8,128)(2,1)} %maximum_select_fusion.2), channel_id=1, source_target_pairs={{0,96},{32,0},{64,32},{96,64},{1,97},{33,1},{65,33},{97,65},{2,98}... | collective-permute-start | bytes 995336 | tf_op jit(solution)/shard_map/ppermute | solution.py:23
  43.6 12.2 %collective-permute-start.11 = (bf16[2,144,576]{2,1,0:T(8,128)(2,1)}, bf16[2,144,576]{2,1,0:T(8,128)(2,1)}, u32[]{:S(2)}, u32[]{:S(2)}) collective-permute-start(bf16[2,144,576]{2,1,0:T(8,128)(2,1)} %maximum_select_fusion.2), channel_id=1, source_target_pairs={{0,64},{32,96},{64,0},{96,32},{1,65},{33,97},{65,1},{97,33},{2,66}... | collective-permute-start | bytes 995336 | tf_op jit(solution)/shard_map/ppermute | solution.py:23
  44.4 11.5 %collective-permute-start.8 = (bf16[2,64,576]{2,1,0:T(8,128)(2,1)S(1)}, bf16[2,64,576]{2,1,0:T(8,128)(2,1)S(1)}, u32[]{:S(2)}, u32[]{:S(2)}) collective-permute-start(bf16[2,64,576]{2,1,0:T(8,128)(2,1)S(1)} %get-tuple-element.54), channel_id=1, source_target_pairs={{0,128},{128,0},{1,129},{129,1},{2,130},{130,2},{3,131},{131,3},{4... | collective-permute-start | bytes 442376 | tf_op jit(solution)/shard_map/ppermute | solution.py:23
  55.9 9.6 %collective-permute-start.13 = (bf16[2304,256]{1,0:T(8,128)(2,1)S(1)}, bf16[2304,256]{1,0:T(8,128)(2,1)S(1)}, u32[]{:S(2)}, u32[]{:S(2)}) collective-permute-start(bf16[2304,256]{1,0:T(8,128)(2,1)S(1)} %multiply_convert_fusion), channel_id=1, source_target_pairs={{0,16},{16,0},{1,17},{17,1},{2,18},{18,2},{3,19},{19,3},{4,20},{20... | collective-permute-start | bytes 3538952 | tf_op jit(solution)/shard_map/ppermute | solution.py:23
  61.7 3.6 %collective-permute-start.12 = (bf16[64,576]{1,0:T(8,128)(2,1)S(1)}, bf16[64,576]{1,0:T(8,128)(2,1)S(1)}, u32[]{:S(2)}, u32[]{:S(2)}) collective-permute-start(bf16[64,576]{1,0:T(8,128)(2,1)S(1)} %get-tuple-element.106), channel_id=1, source_target_pairs={{0,16},{16,0},{1,17},{17,1},{2,18},{18,2},{3,19},{19,3},{4,20},{20... | collective-permute-start | bytes 221192 | tf_op jit(solution)/shard_map/ppermute | solution.py:23
  76.4 23.0 %all-to-all-start.1 = ((bf16[4,288,576]{2,1,0:T(8,128)(2,1)}), bf16[4,288,576]{2,1,0:T(8,128)(2,1)S(1)}, u32[]{:S(2)}, u32[]{:S(2)}) async-start(bf16[4,288,576]{2,1,0:T(8,128)(2,1)} %pad_maximum_fusion), calls=%async_computation.1 | async-start | bytes 2949120 | tf_op jit(solution)/shard_map/all_to_all | solution.py:262
  80.2 19.4 %collective-permute-start.14 = (bf16[2304,256]{1,0:T(8,128)(2,1)}, bf16[2304,256]{1,0:T(8,128)(2,1)}, u32[]{:S(2)}, u32[]{:S(2)}) collective-permute-start(bf16[2304,256]{1,0:T(8,128)(2,1)} %convolution_convert_fusion), channel_id=1, source_target_pairs={{0,16},{16,0},{1,17},{17,1},{2,18},{18,2},{3,19},{19,3},{4,20},{20... | collective-permute-start | bytes 3538952 | tf_op jit(solution)/shard_map/ppermute | solution.py:23
  82.1 4.3 %collective-permute-start.15 = (f32[256]{0:T(256)S(1)}, f32[256]{0:T(256)S(1)}, u32[]{:S(2)}, u32[]{:S(2)}) collective-permute-start(f32[256]{0:T(256)S(1)} %slice.312), channel_id=1, source_target_pairs={{0,16},{16,0},{1,17},{17,1},{2,18},{18,2},{3,19},{19,3},{4,20},{20... | collective-permute-start | bytes 3080 | tf_op jit(solution)/shard_map/ppermute | solution.py:23
  103.8 15.8 %collective-permute-start.18 = (bf16[592,256]{1,0:T(8,128)(2,1)}, bf16[592,256]{1,0:T(8,128)(2,1)}, u32[]{:S(2)}, u32[]{:S(2)}) collective-permute-start(bf16[592,256]{1,0:T(8,128)(2,1)} %get-tuple-element.65), channel_id=1, source_target_pairs={{0,2},{1,3},{2,0},{3,1},{4,6},{5,7},{6,4},{7,5},{8,10},{9,11},{10,... | collective-permute-start | bytes 909320 | tf_op jit(solution)/shard_map/ppermute | solution.py:23
  107.1 13.6 %collective-permute-start.17 = (bf16[592,256]{1,0:T(8,128)(2,1)S(1)}, bf16[592,256]{1,0:T(8,128)(2,1)}, u32[]{:S(2)}, u32[]{:S(2)}) collective-permute-start(bf16[592,256]{1,0:T(8,128)(2,1)S(1)} %get-tuple-element.64), channel_id=1, source_target_pairs={{0,3},{1,0},{2,1},{3,2},{4,7},{5,4},{6,5},{7,6},{8,11},{9,8},{10,9... | collective-permute-start | bytes 909320 | tf_op jit(solution)/shard_map/ppermute | solution.py:23
  108.0 13.2 %collective-permute-start.16 = (bf16[592,256]{1,0:T(8,128)(2,1)S(1)}, bf16[592,256]{1,0:T(8,128)(2,1)}, u32[]{:S(2)}, u32[]{:S(2)}) collective-permute-start(bf16[592,256]{1,0:T(8,128)(2,1)S(1)} %get-tuple-element.63), channel_id=1, source_target_pairs={{0,1},{1,2},{2,3},{3,0},{4,5},{5,6},{6,7},{7,4},{8,9},{9,10},{10,1... | collective-permute-start | bytes 909320 | tf_op jit(solution)/shard_map/ppermute | solution.py:23
  109.5 22.2 %all-to-all-start.2 = ((bf16[4,288,576]{2,1,0:T(8,128)(2,1)}), bf16[4,288,576]{2,1,0:T(8,128)(2,1)}, u32[]{:S(2)}, u32[]{:S(2)}) async-start(bf16[4,288,576]{2,1,0:T(8,128)(2,1)} %pad_maximum_fusion.1), calls=%async_computation.2 | async-start | bytes 2949120 | tf_op jit(solution)/shard_map/all_to_all | solution.py:262
  114.1 31.7 %collective-permute-start.22 = (bf16[144,576]{1,0:T(8,128)(2,1)S(1)}, bf16[144,576]{1,0:T(8,128)(2,1)S(1)}, u32[]{:S(2)}, u32[]{:S(2)}) collective-permute-start(bf16[144,576]{1,0:T(8,128)(2,1)S(1)} %get-tuple-element.97), channel_id=1, source_target_pairs={{0,128},{128,0},{1,129},{129,1},{2,130},{130,2},{3,131},{131,3},{4... | collective-permute-start | bytes 497672 | tf_op jit(solution)/shard_map/ppermute | solution.py:23
  117.8 46.1 %collective-permute-start.28 = (bf16[144,576]{1,0:T(8,128)(2,1)S(1)}, bf16[144,576]{1,0:T(8,128)(2,1)S(1)}, u32[]{:S(2)}, u32[]{:S(2)}) collective-permute-start(bf16[144,576]{1,0:T(8,128)(2,1)S(1)} %get-tuple-element.96), channel_id=1, source_target_pairs={{0,128},{128,0},{1,129},{129,1},{2,130},{130,2},{3,131},{131,3},{4... | collective-permute-start | bytes 497672 | tf_op jit(solution)/shard_map/ppermute | solution.py:23
  133.2 6.3 %collective-permute-start.21 = (bf16[160,256]{1,0:T(8,128)(2,1)S(1)}, bf16[160,256]{1,0:T(8,128)(2,1)S(1)}, u32[]{:S(2)}, u32[]{:S(2)}) collective-permute-start(bf16[160,256]{1,0:T(8,128)(2,1)S(1)} %get-tuple-element.120), channel_id=1, source_target_pairs={{0,8},{4,12},{8,0},{12,4},{1,9},{5,13},{9,1},{13,5},{2,10},{6,14},... | collective-permute-start | bytes 245768 | tf_op jit(solution)/shard_map/ppermute | solution.py:23
  137.6 3.3 %collective-permute-start.20 = (bf16[160,256]{1,0:T(8,128)(2,1)S(1)}, bf16[160,256]{1,0:T(8,128)(2,1)S(1)}, u32[]{:S(2)}, u32[]{:S(2)}) collective-permute-start(bf16[160,256]{1,0:T(8,128)(2,1)S(1)} %get-tuple-element.119), channel_id=1, source_target_pairs={{0,12},{4,0},{8,4},{12,8},{1,13},{5,1},{9,5},{13,9},{2,14},{6,2},{... | collective-permute-start | bytes 245768 | tf_op jit(solution)/shard_map/ppermute | solution.py:23
  138.9 5.8 %collective-permute-start.19 = (bf16[160,256]{1,0:T(8,128)(2,1)S(1)}, bf16[160,256]{1,0:T(8,128)(2,1)S(1)}, u32[]{:S(2)}, u32[]{:S(2)}) collective-permute-start(bf16[160,256]{1,0:T(8,128)(2,1)S(1)} %get-tuple-element.118), channel_id=1, source_target_pairs={{0,4},{4,8},{8,12},{12,0},{1,5},{5,9},{9,13},{13,1},{2,6},{6,10},{... | collective-permute-start | bytes 245768 | tf_op jit(solution)/shard_map/ppermute | solution.py:23
  145.9 6.8 %collective-permute-start.23 = (bf16[160,128]{1,0:T(8,128)(2,1)S(1)}, bf16[160,128]{1,0:T(8,128)(2,1)S(1)}, u32[]{:S(2)}, u32[]{:S(2)}) collective-permute-start(bf16[160,128]{1,0:T(8,128)(2,1)S(1)} %pad_maximum_fusion.13), channel_id=1, source_target_pairs={{0,128},{128,0},{1,129},{129,1},{2,130},{130,2},{3,131},{131,3},{4... | collective-permute-start | bytes 122888 | tf_op jit(solution)/shard_map/ppermute | solution.py:23
  146.1 17.9 %collective-permute-start.29 = (bf16[2,144,576]{2,1,0:T(8,128)(2,1)S(1)}, bf16[2,144,576]{2,1,0:T(8,128)(2,1)S(1)}, u32[]{:S(2)}, u32[]{:S(2)}) collective-permute-start(bf16[2,144,576]{2,1,0:T(8,128)(2,1)S(1)} %pad_maximum_fusion.8), channel_id=1, source_target_pairs={{0,16},{16,0},{1,17},{17,1},{2,18},{18,2},{3,19},{19,3},{4,20},{20... | collective-permute-start | bytes 995336 | tf_op jit(solution)/shard_map/ppermute | solution.py:23
  152.8 6.3 %collective-permute-start.24 = (f32[144]{0:T(256)S(1)}, f32[144]{0:T(256)S(1)}, u32[]{:S(2)}, u32[]{:S(2)}) collective-permute-start(f32[144]{0:T(256)S(1)} %slice_add_fusion.1), channel_id=1, source_target_pairs={{0,16},{16,0},{1,17},{17,1},{2,18},{18,2},{3,19},{19,3},{4,20},{20... | collective-permute-start | bytes 1736 | tf_op jit(solution)/shard_map/ppermute | solution.py:23
  159.1 4.0 %collective-permute-start.27 = (f32[144]{0:T(256)S(1)}, f32[144]{0:T(256)S(1)}, u32[]{:S(2)}, u32[]{:S(2)}) collective-permute-start(f32[144]{0:T(256)S(1)} %add.247), channel_id=1, source_target_pairs={{0,64},{32,96},{64,0},{96,32},{1,65},{33,97},{65,1},{97,33},{2,66}... | collective-permute-start | bytes 1736 | tf_op jit(solution)/shard_map/ppermute | solution.py:23
  159.7 3.6 %collective-permute-start.25 = (f32[144]{0:T(256)S(1)}, f32[144]{0:T(256)S(1)}, u32[]{:S(2)}, u32[]{:S(2)}) collective-permute-start(f32[144]{0:T(256)S(1)} %add.247), channel_id=1, source_target_pairs={{0,32},{32,64},{64,96},{96,0},{1,33},{33,65},{65,97},{97,1},{2,34}... | collective-permute-start | bytes 1736 | tf_op jit(solution)/shard_map/ppermute | solution.py:23
  160.5 2.9 %collective-permute-start.26 = (f32[144]{0:T(256)S(1)}, f32[144]{0:T(256)S(1)}, u32[]{:S(2)}, u32[]{:S(2)}) collective-permute-start(f32[144]{0:T(256)S(1)} %add.247), channel_id=1, source_target_pairs={{0,96},{32,0},{64,32},{96,64},{1,97},{33,1},{65,33},{97,65},{2,98}... | collective-permute-start | bytes 1736 | tf_op jit(solution)/shard_map/ppermute | solution.py:23
  (19 other events, 253.7 us)

commit v2 on v0

--- a/solution.py
+++ b/solution.py
@@ -55,7 +55,7 @@
     zh, core = lax.axis_index("zh"), lax.axis_index("core")
     rows = gate_ref.shape[0]
     if aways:
-        weights, backs = outs[:2], [outs[2].at[0], outs[2].at[1]]
+        weights, backs = [[out.at[0], out.at[1]] for out in outs]
     else:
         weights = [out.at[pl.ds(0, rows)] for out in outs]
         backs = [out.at[pl.ds(rows, half)] for out in outs]
@@ -85,7 +85,7 @@
     main, rest = parts_of(width)
     half = hidden_grad.shape[0] // 2
     if aways:
-        outs = [(rows, width // 2), (rows, width // 2), (2, half, width // 2)]
+        outs = [(2, rows, width // 2), (2, half, width // 2)]
     else:
         outs = [(rows + half, width // 2)] * 2
     return pl.pallas_call(
@@ -197,10 +197,9 @@
 
     near_own, near_other = packed(0, w_gate, w_up, hidden_grad)
     hidden_grad, near_own = barrier((hidden_grad, near_own))
-    away_own, away_other, backs = packed(1, w_gate, w_up, hidden_grad)
+    away, backs = packed(1, w_gate, w_up, hidden_grad)
     near_other = swapped(near_other, "core")
-    away_other, far_t = barrier((away_other, far_t))
-    away_own, away_other = swapped(away_own, "zh"), swapped(away_other, "zh")
+    away = swapped(away, "zh")
 
     near = ordered(near_own[:rows], near_other[:rows], first_core)
     near, own_t = barrier((near, own_t))
@@ -212,7 +211,7 @@
     near_got[0], near_got[1], backs, late_first = barrier(
         (near_got[0], near_got[1], backs, first_core)
     )
-    away_other = swapped(away_other, "core")
+    away_own, away_other = away[0], swapped(away[1], "core")
     backs = swapped(backs, "zh")
     away = ordered(away_own, away_other, late_first)
     late = {}
@@ -227,7 +226,8 @@
     inv_rms = lax.rsqrt(jnp.mean(wide * wide, axis=0) + EPS)
     normed = (wide * inv_rms * norm_gain[:, None]).astype(BF16)
     normed, away_got[0] = barrier((normed, away_got[0]))
-    normed = jnp.concatenate([normed, swapped(normed, "core")], axis=1)
+    normed_other, away_got[2] = barrier((swapped(normed, "core"), away_got[2]))
+    normed = jnp.concatenate([normed, normed_other], axis=1)
 
     backs, *away_got = barrier((backs, *away_got))
     full = jnp.zeros((2, 4, 2, rows, width // 2), BF16)

time: 161 us -> 163 us (1.012)
  the two profiles are of different devices: /device:TPU:24 before, /device:TPU:1 now
where the time goes in v2:
time: 163 us; the launch traced here: 162 us
  starting transfers between devices  96.9 us (59%)
  waiting for transfers between devices  42.7 us (26%)
  matrix products  7.46 us (5%)
  Pallas kernels  6.27 us (4%)
  other arithmetic  4.26 us (3%)
  local copies, waits for them, and re-layouts  3.47 us (2%)
    ppermute x38, starting transfers between devices, turned(): return lax.ppermute(array, axis, [(i, (i + by) % n) for i in range(n)])  96.9 us
    ppermute x38, waiting for transfers between devices, turned(): return lax.ppermute(array, axis, [(i, (i + by) % n) for i in range(n)])  42.7 us
    pallas_call x2, Pallas kernels, packed(): pl.pallas_call(functools.partial(pack_kernel, main, rest, aways), out_sha...  4.05 us
  transfers between devices with their start and end apart: 38, of which 12 were waited for; matrix products, arithmetic and copies ran while one was open for 5% of the time, Pallas kernels for 1%

profile of v2, /device:TPU:1, one launch (start us, length us, event | category | flops | bytes accessed | tf_op | source)
XLA Modules:
  0.0 162.3 jit_solution(10027173147328914295)
XLA Ops:
  0.7 2.0 %pack.2 = (bf16[208,576]{1,0:T(8,128)(2,1)S(1)}, bf16[208,576]{1,0:T(8,128)(2,1)S(1)}) custom-call(bf16[144,1152]{1,0:T(8,128)(2,1)} %gate_ref.3, bf16[144,1152]{1,0:T(8,128)(2,1)} %up_ref.3, bf16[128,1152]{1,0:T(8,128)(2,1)} %back_ref.2), custom_call_target="tpu_custom_call" | custom-call | tf_op jit(solution)/shard_map/pack/pallas_call | solution.py:91
  2.7 3.3 %collective-permute-start = (bf16[208,576]{1,0:T(8,128)(2,1)S(1)}, bf16[208,576]{1,0:T(8,128)(2,1)S(1)}, u32[]{:S(2)}, u32[]{:S(2)}) collective-permute-start(bf16[208,576]{1,0:T(8,128)(2,1)S(1)} %get-tuple-element.51), channel_id=1, source_target_pairs={{0,16},{16,0},{1,17},{17,1},{2,18},{18,2},{3,19},{19,3},{4,20},{20... | collective-permute-start | bytes 718856 | tf_op jit(solution)/shard_map/ppermute | solution.py:23
  6.0 2.0 %pack.3 = (bf16[2,144,576]{2,1,0:T(8,128)(2,1)S(1)}, bf16[2,64,576]{2,1,0:T(8,128)(2,1)S(1)}) custom-call(bf16[144,1152]{1,0:T(8,128)(2,1)} %gate_ref.3, bf16[144,1152]{1,0:T(8,128)(2,1)} %up_ref.3, bf16[128,1152]{1,0:T(8,128)(2,1)} %back_ref.2), custom_call_target="tpu_custom_call" | custom-call | tf_op jit(solution)/shard_map/pack/pallas_call | solution.py:91
  8.0 5.3 %collective-permute-start.4 = (bf16[2,144,576]{2,1,0:T(8,128)(2,1)S(1)}, bf16[2,144,576]{2,1,0:T(8,128)(2,1)S(1)}, u32[]{:S(2)}, u32[]{:S(2)}) collective-permute-start(bf16[2,144,576]{2,1,0:T(8,128)(2,1)S(1)} %get-tuple-element.57), channel_id=1, source_target_pairs={{0,128},{128,0},{1,129},{129,1},{2,130},{130,2},{3,131},{131,3},{4... | collective-permute-start | bytes 995336 | tf_op jit(solution)/shard_map/ppermute | solution.py:23
  15.1 1.6 collective-permute-start.3
  16.7 10.9 %collective-permute-done.1 = bf16[576,128]{1,0:T(8,128)(2,1)S(1)} collective-permute-done((bf16[576,128]{1,0:T(8,128)(2,1)}, bf16[576,128]{1,0:T(8,128)(2,1)S(1)}, u32[]{:S(2)}, u32[]{:S(2)}) %collective-permute-start.1) | collective-permute-done | bytes 147488 | tf_op jit(solution)/shard_map/ppermute | solution.py:23
  29.0 1.5 collective-permute-start.7
  33.9 2.7 %collective-permute-start.9 = (bf16[2,144,576]{2,1,0:T(8,128)(2,1)S(1)}, bf16[2,144,576]{2,1,0:T(8,128)(2,1)S(1)}, u32[]{:S(2)}, u32[]{:S(2)}) collective-permute-start(bf16[2,144,576]{2,1,0:T(8,128)(2,1)S(1)} %maximum_select_fusion), channel_id=1, source_target_pairs={{0,64},{32,96},{64,0},{96,32},{1,65},{33,97},{65,1},{97,33},{2,66}... | collective-permute-start | bytes 995336 | tf_op jit(solution)/shard_map/ppermute | solution.py:23
  37.2 2.4 %collective-permute-start.14 = (bf16[2,144,576]{2,1,0:T(8,128)(2,1)S(1)}, bf16[2,144,576]{2,1,0:T(8,128)(2,1)S(1)}, u32[]{:S(2)}, u32[]{:S(2)}) collective-permute-start(bf16[2,144,576]{2,1,0:T(8,128)(2,1)S(1)} %maximum_select_fusion.1), channel_id=1, source_target_pairs={{0,64},{32,96},{64,0},{96,32},{1,65},{33,97},{65,1},{97,33},{2,66}... | collective-permute-start | bytes 995336 | tf_op jit(solution)/shard_map/ppermute | solution.py:23
  40.6 3.7 %collective-permute-done.8 = bf16[576,256]{1,0:T(8,128)(2,1)S(1)} collective-permute-done((bf16[576,256]{1,0:T(8,128)(2,1)S(1)}, bf16[576,256]{1,0:T(8,128)(2,1)S(1)}, u32[]{:S(2)}, u32[]{:S(2)}) %collective-permute-start.8) | collective-permute-done | bytes 294944 | tf_op jit(solution)/shard_map/ppermute | solution.py:23
  45.1 12.0 %collective-permute-start.10 = (bf16[2,64,576]{2,1,0:T(8,128)(2,1)S(1)}, bf16[2,64,576]{2,1,0:T(8,128)(2,1)S(1)}, u32[]{:S(2)}, u32[]{:S(2)}) collective-permute-start(bf16[2,64,576]{2,1,0:T(8,128)(2,1)S(1)} %get-tuple-element.65), channel_id=1, source_target_pairs={{0,128},{128,0},{1,129},{129,1},{2,130},{130,2},{3,131},{131,3},{4... | collective-permute-start | bytes 442376 | tf_op jit(solution)/shard_map/ppermute | solution.py:23
  57.1 1.8 %collective-permute-start.13 = (bf16[2304,256]{1,0:T(8,128)(2,1)S(1)}, bf16[2304,256]{1,0:T(8,128)(2,1)S(1)}, u32[]{:S(2)}, u32[]{:S(2)}) collective-permute-start(bf16[2304,256]{1,0:T(8,128)(2,1)S(1)} %multiply_convert_fusion), channel_id=1, source_target_pairs={{0,16},{16,0},{1,17},{17,1},{2,18},{18,2},{3,19},{19,3},{4,20},{20... | collective-permute-start | bytes 3538952 | tf_op jit(solution)/shard_map/ppermute | solution.py:23
  59.2 1.9 %collective-permute-done.14 = bf16[2,144,576]{2,1,0:T(8,128)(2,1)S(1)} collective-permute-done((bf16[2,144,576]{2,1,0:T(8,128)(2,1)S(1)}, bf16[2,144,576]{2,1,0:T(8,128)(2,1)S(1)}, u32[]{:S(2)}, u32[]{:S(2)}) %collective-permute-start.14) | collective-permute-done | bytes 331808 | tf_op jit(solution)/shard_map/ppermute | solution.py:23
  61.8 2.1 %fusion.85 = f32[512,576]{1,0:T(8,128)S(1)} fusion(bf16[2304,512]{1,0:T(8,128)(2,1)S(1)} %constant_dynamic-update-slice_fusion.2, bf16[2304,576]{1,0:T(8,128)(2,1)S(1)} %bitcast.117), kind=kOutput, calls=%fused_computation.194 | convolution fusion | flops 1358954496 | bytes 6193152 | tf_op jit(solution)/shard_map/dot_general | solution.py:247
  71.3 2.7 %collective-permute-start.18 = (bf16[288,576]{1,0:T(8,128)(2,1)S(1)}, bf16[288,576]{1,0:T(8,128)(2,1)S(1)}, u32[]{:S(2)}, u32[]{:S(2)}) collective-permute-start(bf16[288,576]{1,0:T(8,128)(2,1)S(1)} %convolution_convert_fusion.5), channel_id=1, source_target_pairs={{0,96},{32,0},{64,32},{96,64},{1,97},{33,1},{65,33},{97,65},{2,98}... | collective-permute-start | bytes 995336 | tf_op jit(solution)/shard_map/ppermute | solution.py:23
  75.4 6.2 %collective-permute-done.18 = bf16[288,576]{1,0:T(8,128)(2,1)S(1)} collective-permute-done((bf16[288,576]{1,0:T(8,128)(2,1)S(1)}, bf16[288,576]{1,0:T(8,128)(2,1)S(1)}, u32[]{:S(2)}, u32[]{:S(2)}) %collective-permute-start.18) | collective-permute-done | bytes 331808 | tf_op jit(solution)/shard_map/ppermute | solution.py:23
  81.6 3.1 %collective-permute-done.17 = bf16[288,576]{1,0:T(8,128)(2,1)S(1)} collective-permute-done((bf16[288,576]{1,0:T(8,128)(2,1)S(1)}, bf16[288,576]{1,0:T(8,128)(2,1)S(1)}, u32[]{:S(2)}, u32[]{:S(2)}) %collective-permute-start.17) | collective-permute-done | bytes 331808 | tf_op jit(solution)/shard_map/ppermute | solution.py:23
  84.7 3.0 %collective-permute-start.20 = (bf16[592,256]{1,0:T(8,128)(2,1)S(1)}, bf16[592,256]{1,0:T(8,128)(2,1)S(1)}, u32[]{:S(2)}, u32[]{:S(2)}) collective-permute-start(bf16[592,256]{1,0:T(8,128)(2,1)S(1)} %get-tuple-element.74), channel_id=1, source_target_pairs={{0,1},{1,2},{2,3},{3,0},{4,5},{5,6},{6,7},{7,4},{8,9},{9,10},{10,1... | collective-permute-start | bytes 909320 | tf_op jit(solution)/shard_map/ppermute | solution.py:23
  87.7 1.5 collective-permute-start.21
  90.9 4.2 %collective-permute-done.20 = bf16[592,256]{1,0:T(8,128)(2,1)S(1)} collective-permute-done((bf16[592,256]{1,0:T(8,128)(2,1)S(1)}, bf16[592,256]{1,0:T(8,128)(2,1)S(1)}, u32[]{:S(2)}, u32[]{:S(2)}) %collective-permute-start.20) | collective-permute-done | bytes 303136 | tf_op jit(solution)/shard_map/ppermute | solution.py:23
  95.2 7.4 %collective-permute-done.22 = bf16[592,256]{1,0:T(8,128)(2,1)S(1)} collective-permute-done((bf16[592,256]{1,0:T(8,128)(2,1)S(1)}, bf16[592,256]{1,0:T(8,128)(2,1)S(1)}, u32[]{:S(2)}, u32[]{:S(2)}) %collective-permute-start.22) | collective-permute-done | bytes 303136 | tf_op jit(solution)/shard_map/ppermute | solution.py:23
  103.1 5.8 %collective-permute-start.24 = (bf16[160,256]{1,0:T(8,128)(2,1)S(1)}, bf16[160,256]{1,0:T(8,128)(2,1)S(1)}, u32[]{:S(2)}, u32[]{:S(2)}) collective-permute-start(bf16[160,256]{1,0:T(8,128)(2,1)S(1)} %get-tuple-element.138), channel_id=1, source_target_pairs={{0,4},{4,8},{8,12},{12,0},{1,5},{5,9},{9,13},{13,1},{2,6},{6,10},{... | collective-permute-start | bytes 245768 | tf_op jit(solution)/shard_map/ppermute | solution.py:23
  108.9 2.2 %collective-permute-start.26 = (bf16[160,256]{1,0:T(8,128)(2,1)S(1)}, bf16[160,256]{1,0:T(8,128)(2,1)S(1)}, u32[]{:S(2)}, u32[]{:S(2)}) collective-permute-start(bf16[160,256]{1,0:T(8,128)(2,1)S(1)} %get-tuple-element.140), channel_id=1, source_target_pairs={{0,8},{4,12},{8,0},{12,4},{1,9},{5,13},{9,1},{13,5},{2,10},{6,14},... | collective-permute-start | bytes 245768 | tf_op jit(solution)/shard_map/ppermute | solution.py:23
  111.1 2.7 %collective-permute-start.28 = (bf16[288,576]{1,0:T(8,128)(2,1)S(1)}, bf16[288,576]{1,0:T(8,128)(2,1)S(1)}, u32[]{:S(2)}, u32[]{:S(2)}) collective-permute-start(bf16[288,576]{1,0:T(8,128)(2,1)S(1)} %convolution_convert_fusion.2), channel_id=1, source_target_pairs={{0,96},{32,0},{64,32},{96,64},{1,97},{33,1},{65,33},{97,65},{2,98}... | collective-permute-start | bytes 995336 | tf_op jit(solution)/shard_map/ppermute | solution.py:23
  113.9 5.1 %collective-permute-start.36 = (bf16[144,576]{1,0:T(8,128)(2,1)S(1)}, bf16[144,576]{1,0:T(8,128)(2,1)S(1)}, u32[]{:S(2)}, u32[]{:S(2)}) collective-permute-start(bf16[144,576]{1,0:T(8,128)(2,1)S(1)} %get-tuple-element.114), channel_id=1, source_target_pairs={{0,128},{128,0},{1,129},{129,1},{2,130},{130,2},{3,131},{131,3},{4... | collective-permute-start | bytes 497672 | tf_op jit(solution)/shard_map/ppermute | solution.py:23
  119.0 1.5 collective-permute-start.35
  120.9 4.8 %collective-permute-start.29 = (bf16[160,128]{1,0:T(8,128)(2,1)S(1)}, bf16[160,128]{1,0:T(8,128)(2,1)S(1)}, u32[]{:S(2)}, u32[]{:S(2)}) collective-permute-start(bf16[160,128]{1,0:T(8,128)(2,1)S(1)} %pad_maximum_fusion.10), channel_id=1, source_target_pairs={{0,128},{128,0},{1,129},{129,1},{2,130},{130,2},{3,131},{131,3},{4... | collective-permute-start | bytes 122888 | tf_op jit(solution)/shard_map/ppermute | solution.py:23
  126.2 17.0 %collective-permute-start.37 = (bf16[2,144,576]{2,1,0:T(8,128)(2,1)S(1)}, bf16[2,144,576]{2,1,0:T(8,128)(2,1)S(1)}, u32[]{:S(2)}, u32[]{:S(2)}) collective-permute-start(bf16[2,144,576]{2,1,0:T(8,128)(2,1)S(1)} %pad_maximum_fusion.6), channel_id=1, source_target_pairs={{0,16},{16,0},{1,17},{17,1},{2,18},{18,2},{3,19},{19,3},{4,20},{20... | collective-permute-start | bytes 995336 | tf_op jit(solution)/shard_map/ppermute | solution.py:23
  143.3 7.4 %collective-permute-start.30 = (f32[144]{0:T(256)S(1)}, f32[144]{0:T(256)S(1)}, u32[]{:S(2)}, u32[]{:S(2)}) collective-permute-start(f32[144]{0:T(256)S(1)} %slice_add_fusion.1), channel_id=1, source_target_pairs={{0,16},{16,0},{1,17},{17,1},{2,18},{18,2},{3,19},{19,3},{4,20},{20... | collective-permute-start | bytes 1736 | tf_op jit(solution)/shard_map/ppermute | solution.py:23
  151.5 2.7 %collective-permute-start.32 = (f32[144]{0:T(256)S(1)}, f32[144]{0:T(256)S(1)}, u32[]{:S(2)}, u32[]{:S(2)}) collective-permute-start(f32[144]{0:T(256)S(1)} %add.232), channel_id=1, source_target_pairs={{0,96},{32,0},{64,32},{96,64},{1,97},{33,1},{65,33},{97,65},{2,98}... | collective-permute-start | bytes 1736 | tf_op jit(solution)/shard_map/ppermute | solution.py:23
  155.1 3.0 %collective-permute-done.33 = f32[144]{0:T(256)S(1)} collective-permute-done((f32[144]{0:T(256)S(1)}, f32[144]{0:T(256)S(1)}, u32[]{:S(2)}, u32[]{:S(2)}) %collective-permute-start.33) | collective-permute-done | bytes 608 | tf_op jit(solution)/shard_map/ppermute | solution.py:23
  160.1 2.2 %join.1 = (bf16[144,1152]{1,0:T(8,128)(2,1)}, bf16[144,1152]{1,0:T(8,128)(2,1)}) custom-call(bf16[2,144,576]{2,1,0:T(8,128)(2,1)} %bitcast.133, bf16[144,576]{1,0:T(8,128)(2,1)} %copy-done.2, bf16[2,144,576]{2,1,0:T(8,128)(2,1)} %copy-done.1), custom_call_target="tpu_custom_call" | custom-call | tf_op jit(solution)/shard_map/join/pallas_call | solution.py:124
  (157 shorter events, 25.4 us)
Async XLA Ops:
  2.7 11.1 %collective-permute-start = (bf16[208,576]{1,0:T(8,128)(2,1)S(1)}, bf16[208,576]{1,0:T(8,128)(2,1)S(1)}, u32[]{:S(2)}, u32[]{:S(2)}) collective-permute-start(bf16[208,576]{1,0:T(8,128)(2,1)S(1)} %get-tuple-element.51), channel_id=1, source_target_pairs={{0,16},{16,0},{1,17},{17,1},{2,18},{18,2},{3,19},{19,3},{4,20},{20... | collective-permute-start | bytes 718856 | tf_op jit(solution)/shard_map/ppermute | solution.py:23
  8.0 22.8 %collective-permute-start.4 = (bf16[2,144,576]{2,1,0:T(8,128)(2,1)S(1)}, bf16[2,144,576]{2,1,0:T(8,128)(2,1)S(1)}, u32[]{:S(2)}, u32[]{:S(2)}) collective-permute-start(bf16[2,144,576]{2,1,0:T(8,128)(2,1)S(1)} %get-tuple-element.57), channel_id=1, source_target_pairs={{0,128},{128,0},{1,129},{129,1},{2,130},{130,2},{3,131},{131,3},{4... | collective-permute-start | bytes 995336 | tf_op jit(solution)/shard_map/ppermute | solution.py:23
  13.3 14.3 %collective-permute-start.1 = (bf16[576,128]{1,0:T(8,128)(2,1)}, bf16[576,128]{1,0:T(8,128)(2,1)S(1)}, u32[]{:S(2)}, u32[]{:S(2)}) collective-permute-start(bf16[576,128]{1,0:T(8,128)(2,1)} %bitcast.142), channel_id=1, source_target_pairs={{0,128},{128,0},{1,129},{129,1},{2,130},{130,2},{3,131},{131,3},{4... | collective-permute-start | bytes 442376 | tf_op jit(solution)/shard_map/ppermute | solution.py:23
  13.9 18.5 %collective-permute-start.2 = (bf16[2,144,576]{2,1,0:T(8,128)(2,1)S(1)}, bf16[2,144,576]{2,1,0:T(8,128)(2,1)S(1)}, u32[]{:S(2)}, u32[]{:S(2)}) collective-permute-start(bf16[2,144,576]{2,1,0:T(8,128)(2,1)S(1)} %maximum_select_fusion), channel_id=1, source_target_pairs={{0,32},{32,64},{64,96},{96,0},{1,33},{33,65},{65,97},{97,1},{2,34}... | collective-permute-start | bytes 995336 | tf_op jit(solution)/shard_map/ppermute | solution.py:23
  15.1 18.8 %collective-permute-start.3 = (bf16[2,144,576]{2,1,0:T(8,128)(2,1)S(1)}, bf16[2,144,576]{2,1,0:T(8,128)(2,1)S(1)}, u32[]{:S(2)}, u32[]{:S(2)}) collective-permute-start(bf16[2,144,576]{2,1,0:T(8,128)(2,1)S(1)} %maximum_select_fusion), channel_id=1, source_target_pairs={{0,96},{32,0},{64,32},{96,64},{1,97},{33,1},{65,33},{97,65},{2,98}... | collective-permute-start | bytes 995336 | tf_op jit(solution)/shard_map/ppermute | solution.py:23
  27.7 9.6 %collective-permute-start.6 = (bf16[576,256]{1,0:T(8,128)(2,1)S(1)}, bf16[576,256]{1,0:T(8,128)(2,1)S(1)}, u32[]{:S(2)}, u32[]{:S(2)}) collective-permute-start(bf16[576,256]{1,0:T(8,128)(2,1)S(1)} %constant_dynamic-update-slice_fusion), channel_id=1, source_target_pairs={{0,1},{1,2},{2,3},{3,0},{4,5},{5,6},{6,7},{7,4},{8,9},{9,10},{10,1... | collective-permute-start | bytes 884744 | tf_op jit(solution)/shard_map/ppermute | solution.py:23
  29.0 10.7 %collective-permute-start.7 = (bf16[576,256]{1,0:T(8,128)(2,1)S(1)}, bf16[576,256]{1,0:T(8,128)(2,1)S(1)}, u32[]{:S(2)}, u32[]{:S(2)}) collective-permute-start(bf16[576,256]{1,0:T(8,128)(2,1)S(1)} %constant_dynamic-update-slice_fusion), channel_id=1, source_target_pairs={{0,3},{1,0},{2,1},{3,2},{4,7},{5,4},{6,5},{7,6},{8,11},{9,8},{10,9... | collective-permute-start | bytes 884744 | tf_op jit(solution)/shard_map/ppermute | solution.py:23
  30.9 5.8 %collective-permute-start.5 = (bf16[144,576]{1,0:T(8,128)(2,1)S(1)}, bf16[144,576]{1,0:T(8,128)(2,1)S(1)}, u32[]{:S(2)}, u32[]{:S(2)}) collective-permute-start(bf16[144,576]{1,0:T(8,128)(2,1)S(1)} %get-tuple-element.117), channel_id=1, source_target_pairs={{0,16},{16,0},{1,17},{17,1},{2,18},{18,2},{3,19},{19,3},{4,20},{20... | collective-permute-start | bytes 497672 | tf_op jit(solution)/shard_map/ppermute | solution.py:23
  32.4 11.9 %collective-permute-start.8 = (bf16[576,256]{1,0:T(8,128)(2,1)S(1)}, bf16[576,256]{1,0:T(8,128)(2,1)S(1)}, u32[]{:S(2)}, u32[]{:S(2)}) collective-permute-start(bf16[576,256]{1,0:T(8,128)(2,1)S(1)} %constant_dynamic-update-slice_fusion), channel_id=1, source_target_pairs={{0,2},{1,3},{2,0},{3,1},{4,6},{5,7},{6,4},{7,5},{8,10},{9,11},{10,... | collective-permute-start | bytes 884744 | tf_op jit(solution)/shard_map/ppermute | solution.py:23
  33.9 25.1 %collective-permute-start.9 = (bf16[2,144,576]{2,1,0:T(8,128)(2,1)S(1)}, bf16[2,144,576]{2,1,0:T(8,128)(2,1)S(1)}, u32[]{:S(2)}, u32[]{:S(2)}) collective-permute-start(bf16[2,144,576]{2,1,0:T(8,128)(2,1)S(1)} %maximum_select_fusion), channel_id=1, source_target_pairs={{0,64},{32,96},{64,0},{96,32},{1,65},{33,97},{65,1},{97,33},{2,66}... | collective-permute-start | bytes 995336 | tf_op jit(solution)/shard_map/ppermute | solution.py:23
  36.7 20.4 %collective-permute-start.11 = (bf16[2,144,576]{2,1,0:T(8,128)(2,1)S(1)}, bf16[2,144,576]{2,1,0:T(8,128)(2,1)S(1)}, u32[]{:S(2)}, u32[]{:S(2)}) collective-permute-start(bf16[2,144,576]{2,1,0:T(8,128)(2,1)S(1)} %maximum_select_fusion.1), channel_id=1, source_target_pairs={{0,32},{32,64},{64,96},{96,0},{1,33},{33,65},{65,97},{97,1},{2,34}... | collective-permute-start | bytes 995336 | tf_op jit(solution)/shard_map/ppermute | solution.py:23
  37.2 23.9 %collective-permute-start.14 = (bf16[2,144,576]{2,1,0:T(8,128)(2,1)S(1)}, bf16[2,144,576]{2,1,0:T(8,128)(2,1)S(1)}, u32[]{:S(2)}, u32[]{:S(2)}) collective-permute-start(bf16[2,144,576]{2,1,0:T(8,128)(2,1)S(1)} %maximum_select_fusion.1), channel_id=1, source_target_pairs={{0,64},{32,96},{64,0},{96,32},{1,65},{33,97},{65,1},{97,33},{2,66}... | collective-permute-start | bytes 995336 | tf_op jit(solution)/shard_map/ppermute | solution.py:23
  39.6 21.8 %collective-permute-start.12 = (bf16[2,144,576]{2,1,0:T(8,128)(2,1)S(1)}, bf16[2,144,576]{2,1,0:T(8,128)(2,1)S(1)}, u32[]{:S(2)}, u32[]{:S(2)}) collective-permute-start(bf16[2,144,576]{2,1,0:T(8,128)(2,1)S(1)} %maximum_select_fusion.1), channel_id=1, source_target_pairs={{0,96},{32,0},{64,32},{96,64},{1,97},{33,1},{65,33},{97,65},{2,98}... | collective-permute-start | bytes 995336 | tf_op jit(solution)/shard_map/ppermute | solution.py:23
  45.1 16.3 %collective-permute-start.10 = (bf16[2,64,576]{2,1,0:T(8,128)(2,1)S(1)}, bf16[2,64,576]{2,1,0:T(8,128)(2,1)S(1)}, u32[]{:S(2)}, u32[]{:S(2)}) collective-permute-start(bf16[2,64,576]{2,1,0:T(8,128)(2,1)S(1)} %get-tuple-element.65), channel_id=1, source_target_pairs={{0,128},{128,0},{1,129},{129,1},{2,130},{130,2},{3,131},{131,3},{4... | collective-permute-start | bytes 442376 | tf_op jit(solution)/shard_map/ppermute | solution.py:23
  69.5 4.6 %collective-permute-start.16 = (bf16[2304,256]{1,0:T(8,128)(2,1)S(1)}, bf16[2304,256]{1,0:T(8,128)(2,1)S(1)}, u32[]{:S(2)}, u32[]{:S(2)}) collective-permute-start(bf16[2304,256]{1,0:T(8,128)(2,1)S(1)} %convolution_convert_fusion), channel_id=1, source_target_pairs={{0,16},{16,0},{1,17},{17,1},{2,18},{18,2},{3,19},{19,3},{4,20},{20... | collective-permute-start | bytes 3538952 | tf_op jit(solution)/shard_map/ppermute | solution.py:23
  71.3 10.3 %collective-permute-start.18 = (bf16[288,576]{1,0:T(8,128)(2,1)S(1)}, bf16[288,576]{1,0:T(8,128)(2,1)S(1)}, u32[]{:S(2)}, u32[]{:S(2)}) collective-permute-start(bf16[288,576]{1,0:T(8,128)(2,1)S(1)} %convolution_convert_fusion.5), channel_id=1, source_target_pairs={{0,96},{32,0},{64,32},{96,64},{1,97},{33,1},{65,33},{97,65},{2,98}... | collective-permute-start | bytes 995336 | tf_op jit(solution)/shard_map/ppermute | solution.py:23
  74.0 10.7 %collective-permute-start.17 = (bf16[288,576]{1,0:T(8,128)(2,1)S(1)}, bf16[288,576]{1,0:T(8,128)(2,1)S(1)}, u32[]{:S(2)}, u32[]{:S(2)}) collective-permute-start(bf16[288,576]{1,0:T(8,128)(2,1)S(1)} %convolution_convert_fusion.6), channel_id=1, source_target_pairs={{0,32},{32,64},{64,96},{96,0},{1,33},{33,65},{65,97},{97,1},{2,34}... | collective-permute-start | bytes 995336 | tf_op jit(solution)/shard_map/ppermute | solution.py:23
  84.7 10.5 %collective-permute-start.20 = (bf16[592,256]{1,0:T(8,128)(2,1)S(1)}, bf16[592,256]{1,0:T(8,128)(2,1)S(1)}, u32[]{:S(2)}, u32[]{:S(2)}) collective-permute-start(bf16[592,256]{1,0:T(8,128)(2,1)S(1)} %get-tuple-element.74), channel_id=1, source_target_pairs={{0,1},{1,2},{2,3},{3,0},{4,5},{5,6},{6,7},{7,4},{8,9},{9,10},{10,1... | collective-permute-start | bytes 909320 | tf_op jit(solution)/shard_map/ppermute | solution.py:23
  87.7 7.5 %collective-permute-start.21 = (bf16[592,256]{1,0:T(8,128)(2,1)S(1)}, bf16[592,256]{1,0:T(8,128)(2,1)S(1)}, u32[]{:S(2)}, u32[]{:S(2)}) collective-permute-start(bf16[592,256]{1,0:T(8,128)(2,1)S(1)} %get-tuple-element.75), channel_id=1, source_target_pairs={{0,3},{1,0},{2,1},{3,2},{4,7},{5,4},{6,5},{7,6},{8,11},{9,8},{10,9... | collective-permute-start | bytes 909320 | tf_op jit(solution)/shard_map/ppermute | solution.py:23
  89.2 13.4 %collective-permute-start.22 = (bf16[592,256]{1,0:T(8,128)(2,1)S(1)}, bf16[592,256]{1,0:T(8,128)(2,1)S(1)}, u32[]{:S(2)}, u32[]{:S(2)}) collective-permute-start(bf16[592,256]{1,0:T(8,128)(2,1)S(1)} %get-tuple-element.76), channel_id=1, source_target_pairs={{0,2},{1,3},{2,0},{3,1},{4,6},{5,7},{6,4},{7,5},{8,10},{9,11},{10,... | collective-permute-start | bytes 909320 | tf_op jit(solution)/shard_map/ppermute | solution.py:23
  90.8 12.0 %collective-permute-start.23 = (bf16[288,576]{1,0:T(8,128)(2,1)S(1)}, bf16[288,576]{1,0:T(8,128)(2,1)S(1)}, u32[]{:S(2)}, u32[]{:S(2)}) collective-permute-start(bf16[288,576]{1,0:T(8,128)(2,1)S(1)} %convolution_convert_fusion.4), channel_id=1, source_target_pairs={{0,64},{32,96},{64,0},{96,32},{1,65},{33,97},{65,1},{97,33},{2,66}... | collective-permute-start | bytes 995336 | tf_op jit(solution)/shard_map/ppermute | solution.py:23
  103.1 10.8 %collective-permute-start.24 = (bf16[160,256]{1,0:T(8,128)(2,1)S(1)}, bf16[160,256]{1,0:T(8,128)(2,1)S(1)}, u32[]{:S(2)}, u32[]{:S(2)}) collective-permute-start(bf16[160,256]{1,0:T(8,128)(2,1)S(1)} %get-tuple-element.138), channel_id=1, source_target_pairs={{0,4},{4,8},{8,12},{12,0},{1,5},{5,9},{9,13},{13,1},{2,6},{6,10},{... | collective-permute-start | bytes 245768 | tf_op jit(solution)/shard_map/ppermute | solution.py:23
  108.9 5.0 %collective-permute-start.25 = (bf16[160,256]{1,0:T(8,128)(2,1)S(1)}, bf16[160,256]{1,0:T(8,128)(2,1)S(1)}, u32[]{:S(2)}, u32[]{:S(2)}) collective-permute-start(bf16[160,256]{1,0:T(8,128)(2,1)S(1)} %get-tuple-element.139), channel_id=1, source_target_pairs={{0,12},{4,0},{8,4},{12,8},{1,13},{5,1},{9,5},{13,9},{2,14},{6,2},{... | collective-permute-start | bytes 245768 | tf_op jit(solution)/shard_map/ppermute | solution.py:23
  108.9 10.1 %collective-permute-start.26 = (bf16[160,256]{1,0:T(8,128)(2,1)S(1)}, bf16[160,256]{1,0:T(8,128)(2,1)S(1)}, u32[]{:S(2)}, u32[]{:S(2)}) collective-permute-start(bf16[160,256]{1,0:T(8,128)(2,1)S(1)} %get-tuple-element.140), channel_id=1, source_target_pairs={{0,8},{4,12},{8,0},{12,4},{1,9},{5,13},{9,1},{13,5},{2,10},{6,14},... | collective-permute-start | bytes 245768 | tf_op jit(solution)/shard_map/ppermute | solution.py:23
  111.1 9.8 %collective-permute-start.27 = (bf16[288,576]{1,0:T(8,128)(2,1)S(1)}, bf16[288,576]{1,0:T(8,128)(2,1)S(1)}, u32[]{:S(2)}, u32[]{:S(2)}) collective-permute-start(bf16[288,576]{1,0:T(8,128)(2,1)S(1)} %convolution_convert_fusion.3), channel_id=1, source_target_pairs={{0,32},{32,64},{64,96},{96,0},{1,33},{33,65},{65,97},{97,1},{2,34}... | collective-permute-start | bytes 995336 | tf_op jit(solution)/shard_map/ppermute | solution.py:23
  111.1 9.8 %collective-permute-start.28 = (bf16[288,576]{1,0:T(8,128)(2,1)S(1)}, bf16[288,576]{1,0:T(8,128)(2,1)S(1)}, u32[]{:S(2)}, u32[]{:S(2)}) collective-permute-start(bf16[288,576]{1,0:T(8,128)(2,1)S(1)} %convolution_convert_fusion.2), channel_id=1, source_target_pairs={{0,96},{32,0},{64,32},{96,64},{1,97},{33,1},{65,33},{97,65},{2,98}... | collective-permute-start | bytes 995336 | tf_op jit(solution)/shard_map/ppermute | solution.py:23
  113.8 11.9 %collective-permute-start.34 = (bf16[288,576]{1,0:T(8,128)(2,1)S(1)}, bf16[288,576]{1,0:T(8,128)(2,1)S(1)}, u32[]{:S(2)}, u32[]{:S(2)}) collective-permute-start(bf16[288,576]{1,0:T(8,128)(2,1)S(1)} %convolution_convert_fusion.1), channel_id=1, source_target_pairs={{0,64},{32,96},{64,0},{96,32},{1,65},{33,97},{65,1},{97,33},{2,66}... | collective-permute-start | bytes 995336 | tf_op jit(solution)/shard_map/ppermute | solution.py:23
  113.9 12.2 %collective-permute-start.36 = (bf16[144,576]{1,0:T(8,128)(2,1)S(1)}, bf16[144,576]{1,0:T(8,128)(2,1)S(1)}, u32[]{:S(2)}, u32[]{:S(2)}) collective-permute-start(bf16[144,576]{1,0:T(8,128)(2,1)S(1)} %get-tuple-element.114), channel_id=1, source_target_pairs={{0,128},{128,0},{1,129},{129,1},{2,130},{130,2},{3,131},{131,3},{4... | collective-permute-start | bytes 497672 | tf_op jit(solution)/shard_map/ppermute | solution.py:23
  119.0 39.6 %collective-permute-start.35 = (bf16[144,576]{1,0:T(8,128)(2,1)S(1)}, bf16[144,576]{1,0:T(8,128)(2,1)S(1)}, u32[]{:S(2)}, u32[]{:S(2)}) collective-permute-start(bf16[144,576]{1,0:T(8,128)(2,1)S(1)} %get-tuple-element.115), channel_id=1, source_target_pairs={{0,128},{128,0},{1,129},{129,1},{2,130},{130,2},{3,131},{131,3},{4... | collective-permute-start | bytes 497672 | tf_op jit(solution)/shard_map/ppermute | solution.py:23
  120.9 22.4 %collective-permute-start.29 = (bf16[160,128]{1,0:T(8,128)(2,1)S(1)}, bf16[160,128]{1,0:T(8,128)(2,1)S(1)}, u32[]{:S(2)}, u32[]{:S(2)}) collective-permute-start(bf16[160,128]{1,0:T(8,128)(2,1)S(1)} %pad_maximum_fusion.10), channel_id=1, source_target_pairs={{0,128},{128,0},{1,129},{129,1},{2,130},{130,2},{3,131},{131,3},{4... | collective-permute-start | bytes 122888 | tf_op jit(solution)/shard_map/ppermute | solution.py:23
  126.2 32.4 %collective-permute-start.37 = (bf16[2,144,576]{2,1,0:T(8,128)(2,1)S(1)}, bf16[2,144,576]{2,1,0:T(8,128)(2,1)S(1)}, u32[]{:S(2)}, u32[]{:S(2)}) collective-permute-start(bf16[2,144,576]{2,1,0:T(8,128)(2,1)S(1)} %pad_maximum_fusion.6), channel_id=1, source_target_pairs={{0,16},{16,0},{1,17},{17,1},{2,18},{18,2},{3,19},{19,3},{4,20},{20... | collective-permute-start | bytes 995336 | tf_op jit(solution)/shard_map/ppermute | solution.py:23
  143.3 8.2 %collective-permute-start.30 = (f32[144]{0:T(256)S(1)}, f32[144]{0:T(256)S(1)}, u32[]{:S(2)}, u32[]{:S(2)}) collective-permute-start(f32[144]{0:T(256)S(1)} %slice_add_fusion.1), channel_id=1, source_target_pairs={{0,16},{16,0},{1,17},{17,1},{2,18},{18,2},{3,19},{19,3},{4,20},{20... | collective-permute-start | bytes 1736 | tf_op jit(solution)/shard_map/ppermute | solution.py:23
  (11 other events, 84.5 us)

commit v3 on v0

--- a/solution.py
+++ b/solution.py
@@ -73,10 +73,8 @@
             thin = []
             for ref in (first, second):
                 tail = ref[:, pl.ds(4 * main, 4 * rest)]
-                pick = tail[:, :rest]
-                for k in range(1, 4):
-                    pick = jnp.where(q == k, tail[:, k * rest : (k + 1) * rest], pick)
-                thin.append(pick)
+                turn = pltpu.roll(tail.astype(F32), ((4 - q) & 3) * rest, 1)
+                thin.append(turn[:, :rest].astype(BF16))
             out[:, pl.ds(2 * main, 2 * rest)] = jnp.concatenate(thin, axis=1)
 
 
@@ -191,6 +189,7 @@
     sec_to = {by: (sec + by) & 3 for by in range(4)}
     tp_to = {by: (tp + by) & 3 for by in range(4)}
     offset = (tp * 4 + sec) * own_rows
+    tp_to, offset, hidden_grad = barrier((tp_to, offset, hidden_grad))
 
     own_t = tokens.T
     far_t = swapped(own_t, "zh")
@@ -207,6 +206,7 @@
     near_got = [turned(near, "x", by) for by in steps]
 
     both = jnp.concatenate([own_t, far_t], axis=1)
+    both, near_got[0], near_got[1] = barrier((both, near_got[0], near_got[1]))
     section_got = [turned(both, "sec", by) for by in steps]
 
     near_got[0], near_got[1], backs, late_first = barrier(
@@ -227,7 +227,8 @@
     inv_rms = lax.rsqrt(jnp.mean(wide * wide, axis=0) + EPS)
     normed = (wide * inv_rms * norm_gain[:, None]).astype(BF16)
     normed, away_got[0] = barrier((normed, away_got[0]))
-    normed = jnp.concatenate([normed, swapped(normed, "core")], axis=1)
+    normed_other, away_got[2] = barrier((swapped(normed, "core"), away_got[2]))
+    normed = jnp.concatenate([normed, normed_other], axis=1)
 
     backs, *away_got = barrier((backs, *away_got))
     full = jnp.zeros((2, 4, 2, rows, width // 2), BF16)
@@ -262,10 +263,11 @@
         return jnp.dot(as_block(by_rows, zplace, xplace), d_both, preferred_element_type=F32)
 
     away_parts = [part(far_zh, x_to[by]).astype(BF16) for by in steps]
-    near_parts = [part(zh, x_to[by]).astype(BF16) for by in steps]
-    away_got = [turned(away_parts[k], "x", steps[k]) for k in (0, 1)]
+    away_got = [turned(p, "x", by) for p, by in zip(away_parts, steps)]
 
     got = swapped(d_normed(d_both[2 * group :]).astype(BF16), "core")
+    got, late_zh = barrier((got, zh))
+    near_parts = [part(late_zh, x_to[by]).astype(BF16) for by in steps]
     row = row_part[: 2 * group] + swapped(row_part[2 * group :], "core")
     mine = d_normed(d_both[: 2 * group]) + got.astype(F32)
     mine = mine.reshape(4, 4, own_rows, 2 * group)
@@ -278,19 +280,16 @@
         return block.reshape(4 * own_rows, 2 * group)
 
     sends = [with_rows(section(sec_to[by]), row) for by in steps]
-    *away_got, away_parts[2], sends[0], sends[1], sends[2] = barrier(
-        (*away_got, away_parts[2], *sends)
-    )
-    away_got.append(turned(away_parts[2], "x", 2))
+    g_away = (part(far_zh, x) + sum(g.astype(F32) for g in away_got)).astype(BF16)
+    g_away, *rest = barrier((g_away, *sends, *near_parts))
+    sends, near_parts = rest[:3], rest[3:]
     got = [turned(s, "sec", by) for s, by in zip(sends, steps)]
-    away_got[2], *near_parts = barrier((away_got[2], *near_parts))
     near_got = [turned(p, "x", by) for p, by in zip(near_parts, steps)]
-    g_away = part(far_zh, x) + sum(g.astype(F32) for g in away_got)
-    g_away = g_away.astype(BF16).reshape(2, rows, -1)
-    late = {}
-    g_away, late[1], late[3], late[2] = barrier((g_away, *(tp_to[by] for by in steps)))
+    g_away = g_away.reshape(2, rows, -1)
     away_keep = swapped(as_block(g_away, core), "zh")
     away_give = swapped(as_block(g_away, other_core), "zh")
+    late = {}
+    away_give, late[1], late[3], late[2] = barrier((away_give, *(tp_to[by] for by in steps)))
 
     total = section(sec) + sum(block_of(g) for g in got)
     row = row + sum(row_of(g) for g in got)
@@ -306,7 +305,7 @@
     gain_part = jnp.sum(total * own_inputs * inv_rms, axis=1)
     gain_rows = jnp.pad(gain_part, (0, 2 * group - own_rows)).reshape(2, group)
     send = with_rows(total[:, group:], row[group:], gain_rows[0], gain_rows[1])
-    send, near_got[0], near_got[1], late_zh = barrier((send, near_got[0], near_got[1], zh))
+    send, near_got[0], late_zh = barrier((send, near_got[0], zh))
     got = swapped(send, "zh")
     g_near = part(late_zh, x) + sum(g.astype(F32) for g in near_got)
     g_near = g_near.astype(BF16).reshape(2, rows, -1)

time: 161 us -> 160 us (level)
  the two profiles are of different devices: /device:TPU:24 before, /device:TPU:1 now
where the time goes in v3:
time: 160 us
  starting transfers between devices  78.2 us (49%)
  waiting for transfers between devices  60.6 us (38%)
  matrix products  7.48 us (5%)
  Pallas kernels  4.93 us (3%)
  other arithmetic  4.44 us (3%)
  local copies, waits for them, and re-layouts  3.38 us (2%)
    ppermute x39, starting transfers between devices, turned(): return lax.ppermute(array, axis, [(i, (i + by) % n) for i in range(n)])  78.2 us
    ppermute x39, waiting for transfers between devices, turned(): return lax.ppermute(array, axis, [(i, (i + by) % n) for i in range(n)])  60.6 us
  transfers between devices with their start and end apart: 39, of which 16 were waited for; matrix products, arithmetic and copies ran while one was open for 4% of the time, Pallas kernels for 1%

profile of v3, /device:TPU:1, one launch (start us, length us, event | category | flops | bytes accessed | tf_op | source)
XLA Modules:
  0.0 160.3 jit_solution(9947622991875299780)
XLA Ops:
  2.0 3.3 %collective-permute-start = (bf16[208,576]{1,0:T(8,128)(2,1)S(1)}, bf16[208,576]{1,0:T(8,128)(2,1)S(1)}, u32[]{:S(2)}, u32[]{:S(2)}) collective-permute-start(bf16[208,576]{1,0:T(8,128)(2,1)S(1)} %get-tuple-element.61), channel_id=1, source_target_pairs={{0,16},{16,0},{1,17},{17,1},{2,18},{18,2},{3,19},{19,3},{4,20},{20... | collective-permute-start | bytes 718856 | tf_op jit(solution)/shard_map/ppermute | solution.py:23
  5.3 5.2 %collective-permute-start.1 = (bf16[576,128]{1,0:T(8,128)(2,1)}, bf16[576,128]{1,0:T(8,128)(2,1)S(1)}, u32[]{:S(2)}, u32[]{:S(2)}) collective-permute-start(bf16[576,128]{1,0:T(8,128)(2,1)} %bitcast.144), channel_id=1, source_target_pairs={{0,128},{128,0},{1,129},{129,1},{2,130},{130,2},{3,131},{131,3},{4... | collective-permute-start | bytes 442376 | tf_op jit(solution)/shard_map/ppermute | solution.py:23
  12.4 2.5 %collective-permute-done.1 = bf16[576,128]{1,0:T(8,128)(2,1)S(1)} collective-permute-done((bf16[576,128]{1,0:T(8,128)(2,1)}, bf16[576,128]{1,0:T(8,128)(2,1)S(1)}, u32[]{:S(2)}, u32[]{:S(2)}) %collective-permute-start.1) | collective-permute-done | bytes 147488 | tf_op jit(solution)/shard_map/ppermute | solution.py:23
  14.9 5.2 %collective-permute-start.5 = (bf16[144,576]{1,0:T(8,128)(2,1)S(1)}, bf16[144,576]{1,0:T(8,128)(2,1)S(1)}, u32[]{:S(2)}, u32[]{:S(2)}) collective-permute-start(bf16[144,576]{1,0:T(8,128)(2,1)S(1)} %get-tuple-element.73), channel_id=1, source_target_pairs={{0,128},{128,0},{1,129},{129,1},{2,130},{130,2},{3,131},{131,3},{4... | collective-permute-start | bytes 497672 | tf_op jit(solution)/shard_map/ppermute | solution.py:23
  24.8 10.1 %collective-permute-done.5 = bf16[144,576]{1,0:T(8,128)(2,1)S(1)} collective-permute-done((bf16[144,576]{1,0:T(8,128)(2,1)S(1)}, bf16[144,576]{1,0:T(8,128)(2,1)S(1)}, u32[]{:S(2)}, u32[]{:S(2)}) %collective-permute-start.5) | collective-permute-done | bytes 165920 | tf_op jit(solution)/shard_map/ppermute | solution.py:23
  39.1 1.6 collective-permute-start.9
  43.1 5.8 %collective-permute-start.15 = (bf16[2,144,576]{2,1,0:T(8,128)(2,1)S(1)}, bf16[2,144,576]{2,1,0:T(8,128)(2,1)S(1)}, u32[]{:S(2)}, u32[]{:S(2)}) collective-permute-start(bf16[2,144,576]{2,1,0:T(8,128)(2,1)S(1)} %maximum_select_fusion.1), channel_id=1, source_target_pairs={{0,64},{32,96},{64,0},{96,32},{1,65},{33,97},{65,1},{97,33},{2,66}... | collective-permute-start | bytes 995336 | tf_op jit(solution)/shard_map/ppermute | solution.py:23
  49.1 3.2 %collective-permute-done.9 = bf16[576,256]{1,0:T(8,128)(2,1)S(1)} collective-permute-done((bf16[576,256]{1,0:T(8,128)(2,1)S(1)}, bf16[576,256]{1,0:T(8,128)(2,1)S(1)}, u32[]{:S(2)}, u32[]{:S(2)}) %collective-permute-start.9) | collective-permute-done | bytes 294944 | tf_op jit(solution)/shard_map/ppermute | solution.py:23
  52.4 4.5 %collective-permute-start.11 = (bf16[2,64,576]{2,1,0:T(8,128)(2,1)S(1)}, bf16[2,64,576]{2,1,0:T(8,128)(2,1)S(1)}, u32[]{:S(2)}, u32[]{:S(2)}) collective-permute-start(bf16[2,64,576]{2,1,0:T(8,128)(2,1)S(1)} %get-tuple-element.82), channel_id=1, source_target_pairs={{0,128},{128,0},{1,129},{129,1},{2,130},{130,2},{3,131},{131,3},{4... | collective-permute-start | bytes 442376 | tf_op jit(solution)/shard_map/ppermute | solution.py:23
  57.7 2.4 %collective-permute-start.14 = (bf16[2304,256]{1,0:T(8,128)(2,1)S(1)}, bf16[2304,256]{1,0:T(8,128)(2,1)S(1)}, u32[]{:S(2)}, u32[]{:S(2)}) collective-permute-start(bf16[2304,256]{1,0:T(8,128)(2,1)S(1)} %multiply_convert_fusion), channel_id=1, source_target_pairs={{0,16},{16,0},{1,17},{17,1},{2,18},{18,2},{3,19},{19,3},{4,20},{20... | collective-permute-start | bytes 3538952 | tf_op jit(solution)/shard_map/ppermute | solution.py:23
  60.4 2.1 %collective-permute-done.14 = bf16[2304,256]{1,0:T(8,128)(2,1)S(1)} collective-permute-done((bf16[2304,256]{1,0:T(8,128)(2,1)S(1)}, bf16[2304,256]{1,0:T(8,128)(2,1)S(1)}, u32[]{:S(2)}, u32[]{:S(2)}) %collective-permute-start.14) | collective-permute-done | bytes 1179680 | tf_op jit(solution)/shard_map/ppermute | solution.py:23
  62.9 2.1 %fusion.84 = f32[512,576]{1,0:T(8,128)S(1)} fusion(bf16[2304,512]{1,0:T(8,128)(2,1)S(1)} %constant_dynamic-update-slice_fusion, bf16[2304,576]{1,0:T(8,128)(2,1)S(1)} %bitcast.118), kind=kOutput, calls=%fused_computation.191 | convolution fusion | flops 1358954496 | bytes 6193152 | tf_op jit(solution)/shard_map/dot_general | solution.py:248
  65.2 2.4 %collective-permute-start.16 = (bf16[64,576]{1,0:T(8,128)(2,1)S(1)}, bf16[64,576]{1,0:T(8,128)(2,1)S(1)}, u32[]{:S(2)}, u32[]{:S(2)}) collective-permute-start(bf16[64,576]{1,0:T(8,128)(2,1)S(1)} %get-tuple-element.142), channel_id=1, source_target_pairs={{0,16},{16,0},{1,17},{17,1},{2,18},{18,2},{3,19},{19,3},{4,20},{20... | collective-permute-start | bytes 221192 | tf_op jit(solution)/shard_map/ppermute | solution.py:23
  73.8 1.9 %collective-permute-start.18 = (bf16[288,576]{1,0:T(8,128)(2,1)S(1)}, bf16[288,576]{1,0:T(8,128)(2,1)S(1)}, u32[]{:S(2)}, u32[]{:S(2)}) collective-permute-start(bf16[288,576]{1,0:T(8,128)(2,1)S(1)} %convolution_convert_fusion.6), channel_id=1, source_target_pairs={{0,32},{32,64},{64,96},{96,0},{1,33},{33,65},{65,97},{97,1},{2,34}... | collective-permute-start | bytes 995336 | tf_op jit(solution)/shard_map/ppermute | solution.py:23
  76.5 2.8 %collective-permute-start.20 = (bf16[288,576]{1,0:T(8,128)(2,1)S(1)}, bf16[288,576]{1,0:T(8,128)(2,1)S(1)}, u32[]{:S(2)}, u32[]{:S(2)}) collective-permute-start(bf16[288,576]{1,0:T(8,128)(2,1)S(1)} %convolution_convert_fusion.4), channel_id=1, source_target_pairs={{0,64},{32,96},{64,0},{96,32},{1,65},{33,97},{65,1},{97,33},{2,66}... | collective-permute-start | bytes 995336 | tf_op jit(solution)/shard_map/ppermute | solution.py:23
  79.4 5.5 %collective-permute-done.18 = bf16[288,576]{1,0:T(8,128)(2,1)S(1)} collective-permute-done((bf16[288,576]{1,0:T(8,128)(2,1)S(1)}, bf16[288,576]{1,0:T(8,128)(2,1)S(1)}, u32[]{:S(2)}, u32[]{:S(2)}) %collective-permute-start.18) | collective-permute-done | bytes 331808 | tf_op jit(solution)/shard_map/ppermute | solution.py:23
  85.9 8.5 %collective-permute-done.20 = bf16[288,576]{1,0:T(8,128)(2,1)S(1)} collective-permute-done((bf16[288,576]{1,0:T(8,128)(2,1)S(1)}, bf16[288,576]{1,0:T(8,128)(2,1)S(1)}, u32[]{:S(2)}, u32[]{:S(2)}) %collective-permute-start.20) | collective-permute-done | bytes 331808 | tf_op jit(solution)/shard_map/ppermute | solution.py:23
  97.5 2.8 %collective-permute-start.23 = (bf16[592,256]{1,0:T(8,128)(2,1)S(1)}, bf16[592,256]{1,0:T(8,128)(2,1)S(1)}, u32[]{:S(2)}, u32[]{:S(2)}) collective-permute-start(bf16[592,256]{1,0:T(8,128)(2,1)S(1)} %get-tuple-element.94), channel_id=1, source_target_pairs={{0,3},{1,0},{2,1},{3,2},{4,7},{5,4},{6,5},{7,6},{8,11},{9,8},{10,9... | collective-permute-start | bytes 909320 | tf_op jit(solution)/shard_map/ppermute | solution.py:23
  100.3 1.8 %collective-permute-start.24 = (bf16[592,256]{1,0:T(8,128)(2,1)S(1)}, bf16[592,256]{1,0:T(8,128)(2,1)S(1)}, u32[]{:S(2)}, u32[]{:S(2)}) collective-permute-start(bf16[592,256]{1,0:T(8,128)(2,1)S(1)} %get-tuple-element.95), channel_id=1, source_target_pairs={{0,2},{1,3},{2,0},{3,1},{4,6},{5,7},{6,4},{7,5},{8,10},{9,11},{10,... | collective-permute-start | bytes 909320 | tf_op jit(solution)/shard_map/ppermute | solution.py:23
  102.2 1.9 %collective-permute-start.25 = (bf16[144,576]{1,0:T(8,128)(2,1)S(1)}, bf16[144,576]{1,0:T(8,128)(2,1)S(1)}, u32[]{:S(2)}, u32[]{:S(2)}) collective-permute-start(bf16[144,576]{1,0:T(8,128)(2,1)S(1)} %get-tuple-element.133), channel_id=1, source_target_pairs={{0,128},{128,0},{1,129},{129,1},{2,130},{130,2},{3,131},{131,3},{4... | collective-permute-start | bytes 497672 | tf_op jit(solution)/shard_map/ppermute | solution.py:23
  104.2 11.4 %collective-permute-done.25 = bf16[144,576]{1,0:T(8,128)(2,1)S(1)} collective-permute-done((bf16[144,576]{1,0:T(8,128)(2,1)S(1)}, bf16[144,576]{1,0:T(8,128)(2,1)S(1)}, u32[]{:S(2)}, u32[]{:S(2)}) %collective-permute-start.25) | collective-permute-done | bytes 165920 | tf_op jit(solution)/shard_map/ppermute | solution.py:23
  116.2 3.1 %collective-permute-start.27 = (bf16[160,256]{1,0:T(8,128)(2,1)S(1)}, bf16[160,256]{1,0:T(8,128)(2,1)S(1)}, u32[]{:S(2)}, u32[]{:S(2)}) collective-permute-start(bf16[160,256]{1,0:T(8,128)(2,1)S(1)} %get-tuple-element.155), channel_id=1, source_target_pairs={{0,12},{4,0},{8,4},{12,8},{1,13},{5,1},{9,5},{13,9},{2,14},{6,2},{... | collective-permute-start | bytes 245768 | tf_op jit(solution)/shard_map/ppermute | solution.py:23
  120.2 1.9 %collective-permute-start.35 = (bf16[288,576]{1,0:T(8,128)(2,1)S(1)}, bf16[288,576]{1,0:T(8,128)(2,1)S(1)}, u32[]{:S(2)}, u32[]{:S(2)}) collective-permute-start(bf16[288,576]{1,0:T(8,128)(2,1)S(1)} %convolution_convert_fusion.2), channel_id=1, source_target_pairs={{0,96},{32,0},{64,32},{96,64},{1,97},{33,1},{65,33},{97,65},{2,98}... | collective-permute-start | bytes 995336 | tf_op jit(solution)/shard_map/ppermute | solution.py:23
  122.8 2.0 %collective-permute-done.28 = bf16[160,256]{1,0:T(8,128)(2,1)S(1)} collective-permute-done((bf16[160,256]{1,0:T(8,128)(2,1)S(1)}, bf16[160,256]{1,0:T(8,128)(2,1)S(1)}, u32[]{:S(2)}, u32[]{:S(2)}) %collective-permute-start.28) | collective-permute-done | bytes 81952 | tf_op jit(solution)/shard_map/ppermute | solution.py:23
  125.1 6.0 %collective-permute-done.29 = bf16[288,576]{1,0:T(8,128)(2,1)S(1)} collective-permute-done((bf16[288,576]{1,0:T(8,128)(2,1)S(1)}, bf16[288,576]{1,0:T(8,128)(2,1)S(1)}, u32[]{:S(2)}, u32[]{:S(2)}) %collective-permute-start.29) | collective-permute-done | bytes 331808 | tf_op jit(solution)/shard_map/ppermute | solution.py:23
  131.1 3.1 %collective-permute-done.36 = bf16[288,576]{1,0:T(8,128)(2,1)S(1)} collective-permute-done((bf16[288,576]{1,0:T(8,128)(2,1)S(1)}, bf16[288,576]{1,0:T(8,128)(2,1)S(1)}, u32[]{:S(2)}, u32[]{:S(2)}) %collective-permute-start.36) | collective-permute-done | bytes 331808 | tf_op jit(solution)/shard_map/ppermute | solution.py:23
  134.6 2.4 %collective-permute-start.30 = (bf16[160,128]{1,0:T(8,128)(2,1)S(1)}, bf16[160,128]{1,0:T(8,128)(2,1)S(1)}, u32[]{:S(2)}, u32[]{:S(2)}) collective-permute-start(bf16[160,128]{1,0:T(8,128)(2,1)S(1)} %pad_maximum_fusion.11), channel_id=1, source_target_pairs={{0,128},{128,0},{1,129},{129,1},{2,130},{130,2},{3,131},{131,3},{4... | collective-permute-start | bytes 122888 | tf_op jit(solution)/shard_map/ppermute | solution.py:23
  137.1 4.0 %collective-permute-start.38 = (bf16[2,144,576]{2,1,0:T(8,128)(2,1)S(1)}, bf16[2,144,576]{2,1,0:T(8,128)(2,1)S(1)}, u32[]{:S(2)}, u32[]{:S(2)}) collective-permute-start(bf16[2,144,576]{2,1,0:T(8,128)(2,1)S(1)} %pad_maximum_fusion.6), channel_id=1, source_target_pairs={{0,16},{16,0},{1,17},{17,1},{2,18},{18,2},{3,19},{19,3},{4,20},{20... | collective-permute-start | bytes 995336 | tf_op jit(solution)/shard_map/ppermute | solution.py:23
  141.5 6.6 %collective-permute-start.31 = (f32[144]{0:T(256)S(1)}, f32[144]{0:T(256)S(1)}, u32[]{:S(2)}, u32[]{:S(2)}) collective-permute-start(f32[144]{0:T(256)S(1)} %slice_add_fusion.1), channel_id=1, source_target_pairs={{0,16},{16,0},{1,17},{17,1},{2,18},{18,2},{3,19},{19,3},{4,20},{20... | collective-permute-start | bytes 1736 | tf_op jit(solution)/shard_map/ppermute | solution.py:23
  149.5 2.6 %collective-permute-start.33 = (f32[144]{0:T(256)S(1)}, f32[144]{0:T(256)S(1)}, u32[]{:S(2)}, u32[]{:S(2)}) collective-permute-start(f32[144]{0:T(256)S(1)} %add.232), channel_id=1, source_target_pairs={{0,96},{32,0},{64,32},{96,64},{1,97},{33,1},{65,33},{97,65},{2,98}... | collective-permute-start | bytes 1736 | tf_op jit(solution)/shard_map/ppermute | solution.py:23
  154.0 2.0 %collective-permute-done.34 = f32[144]{0:T(256)S(1)} collective-permute-done((f32[144]{0:T(256)S(1)}, f32[144]{0:T(256)S(1)}, u32[]{:S(2)}, u32[]{:S(2)}) %collective-permute-start.34) | collective-permute-done | bytes 608 | tf_op jit(solution)/shard_map/ppermute | solution.py:23
  158.0 2.2 %join.1 = (bf16[144,1152]{1,0:T(8,128)(2,1)}, bf16[144,1152]{1,0:T(8,128)(2,1)}) custom-call(bf16[2,144,576]{2,1,0:T(8,128)(2,1)} %bitcast.134, bf16[144,576]{1,0:T(8,128)(2,1)} %copy-done.2, bf16[2,144,576]{2,1,0:T(8,128)(2,1)} %copy-done.1), custom_call_target="tpu_custom_call" | custom-call | tf_op jit(solution)/shard_map/join/pallas_call | solution.py:122
  (157 shorter events, 35.9 us)
Async XLA Ops:
  2.0 18.1 %collective-permute-start = (bf16[208,576]{1,0:T(8,128)(2,1)S(1)}, bf16[208,576]{1,0:T(8,128)(2,1)S(1)}, u32[]{:S(2)}, u32[]{:S(2)}) collective-permute-start(bf16[208,576]{1,0:T(8,128)(2,1)S(1)} %get-tuple-element.61), channel_id=1, source_target_pairs={{0,16},{16,0},{1,17},{17,1},{2,18},{18,2},{3,19},{19,3},{4,20},{20... | collective-permute-start | bytes 718856 | tf_op jit(solution)/shard_map/ppermute | solution.py:23
  5.3 9.5 %collective-permute-start.1 = (bf16[576,128]{1,0:T(8,128)(2,1)}, bf16[576,128]{1,0:T(8,128)(2,1)S(1)}, u32[]{:S(2)}, u32[]{:S(2)}) collective-permute-start(bf16[576,128]{1,0:T(8,128)(2,1)} %bitcast.144), channel_id=1, source_target_pairs={{0,128},{128,0},{1,129},{129,1},{2,130},{130,2},{3,131},{131,3},{4... | collective-permute-start | bytes 442376 | tf_op jit(solution)/shard_map/ppermute | solution.py:23
  11.9 27.2 %collective-permute-start.4 = (bf16[144,576]{1,0:T(8,128)(2,1)S(1)}, bf16[144,576]{1,0:T(8,128)(2,1)S(1)}, u32[]{:S(2)}, u32[]{:S(2)}) collective-permute-start(bf16[144,576]{1,0:T(8,128)(2,1)S(1)} %get-tuple-element.72), channel_id=1, source_target_pairs={{0,128},{128,0},{1,129},{129,1},{2,130},{130,2},{3,131},{131,3},{4... | collective-permute-start | bytes 497672 | tf_op jit(solution)/shard_map/ppermute | solution.py:23
  14.9 20.0 %collective-permute-start.5 = (bf16[144,576]{1,0:T(8,128)(2,1)S(1)}, bf16[144,576]{1,0:T(8,128)(2,1)S(1)}, u32[]{:S(2)}, u32[]{:S(2)}) collective-permute-start(bf16[144,576]{1,0:T(8,128)(2,1)S(1)} %get-tuple-element.73), channel_id=1, source_target_pairs={{0,128},{128,0},{1,129},{129,1},{2,130},{130,2},{3,131},{131,3},{4... | collective-permute-start | bytes 497672 | tf_op jit(solution)/shard_map/ppermute | solution.py:23
  20.2 16.0 %collective-permute-start.2 = (bf16[2,144,576]{2,1,0:T(8,128)(2,1)S(1)}, bf16[2,144,576]{2,1,0:T(8,128)(2,1)S(1)}, u32[]{:S(2)}, u32[]{:S(2)}) collective-permute-start(bf16[2,144,576]{2,1,0:T(8,128)(2,1)S(1)} %maximum_select_fusion), channel_id=1, source_target_pairs={{0,32},{32,64},{64,96},{96,0},{1,33},{33,65},{65,97},{97,1},{2,34}... | collective-permute-start | bytes 995336 | tf_op jit(solution)/shard_map/ppermute | solution.py:23
  21.5 14.8 %collective-permute-start.3 = (bf16[2,144,576]{2,1,0:T(8,128)(2,1)S(1)}, bf16[2,144,576]{2,1,0:T(8,128)(2,1)S(1)}, u32[]{:S(2)}, u32[]{:S(2)}) collective-permute-start(bf16[2,144,576]{2,1,0:T(8,128)(2,1)S(1)} %maximum_select_fusion), channel_id=1, source_target_pairs={{0,96},{32,0},{64,32},{96,64},{1,97},{33,1},{65,33},{97,65},{2,98}... | collective-permute-start | bytes 995336 | tf_op jit(solution)/shard_map/ppermute | solution.py:23
  23.0 37.2 %collective-permute-start.10 = (bf16[2,144,576]{2,1,0:T(8,128)(2,1)S(1)}, bf16[2,144,576]{2,1,0:T(8,128)(2,1)S(1)}, u32[]{:S(2)}, u32[]{:S(2)}) collective-permute-start(bf16[2,144,576]{2,1,0:T(8,128)(2,1)S(1)} %maximum_select_fusion), channel_id=1, source_target_pairs={{0,64},{32,96},{64,0},{96,32},{1,65},{33,97},{65,1},{97,33},{2,66}... | collective-permute-start | bytes 995336 | tf_op jit(solution)/shard_map/ppermute | solution.py:23
  36.3 6.9 %collective-permute-start.7 = (bf16[576,256]{1,0:T(8,128)(2,1)S(1)}, bf16[576,256]{1,0:T(8,128)(2,1)S(1)}, u32[]{:S(2)}, u32[]{:S(2)}) collective-permute-start(bf16[576,256]{1,0:T(8,128)(2,1)S(1)} %pad_maximum_fusion.7), channel_id=1, source_target_pairs={{0,1},{1,2},{2,3},{3,0},{4,5},{5,6},{6,7},{7,4},{8,9},{9,10},{10,1... | collective-permute-start | bytes 884744 | tf_op jit(solution)/shard_map/ppermute | solution.py:23
  37.5 11.5 %collective-permute-start.8 = (bf16[576,256]{1,0:T(8,128)(2,1)S(1)}, bf16[576,256]{1,0:T(8,128)(2,1)S(1)}, u32[]{:S(2)}, u32[]{:S(2)}) collective-permute-start(bf16[576,256]{1,0:T(8,128)(2,1)S(1)} %pad_maximum_fusion.7), channel_id=1, source_target_pairs={{0,3},{1,0},{2,1},{3,2},{4,7},{5,4},{6,5},{7,6},{8,11},{9,8},{10,9... | collective-permute-start | bytes 884744 | tf_op jit(solution)/shard_map/ppermute | solution.py:23
  39.1 13.3 %collective-permute-start.9 = (bf16[576,256]{1,0:T(8,128)(2,1)S(1)}, bf16[576,256]{1,0:T(8,128)(2,1)S(1)}, u32[]{:S(2)}, u32[]{:S(2)}) collective-permute-start(bf16[576,256]{1,0:T(8,128)(2,1)S(1)} %pad_maximum_fusion.7), channel_id=1, source_target_pairs={{0,2},{1,3},{2,0},{3,1},{4,6},{5,7},{6,4},{7,5},{8,10},{9,11},{10,... | collective-permute-start | bytes 884744 | tf_op jit(solution)/shard_map/ppermute | solution.py:23
  40.7 16.9 %collective-permute-start.12 = (bf16[2,144,576]{2,1,0:T(8,128)(2,1)S(1)}, bf16[2,144,576]{2,1,0:T(8,128)(2,1)S(1)}, u32[]{:S(2)}, u32[]{:S(2)}) collective-permute-start(bf16[2,144,576]{2,1,0:T(8,128)(2,1)S(1)} %maximum_select_fusion.1), channel_id=1, source_target_pairs={{0,32},{32,64},{64,96},{96,0},{1,33},{33,65},{65,97},{97,1},{2,34}... | collective-permute-start | bytes 995336 | tf_op jit(solution)/shard_map/ppermute | solution.py:23
  43.1 17.3 %collective-permute-start.15 = (bf16[2,144,576]{2,1,0:T(8,128)(2,1)S(1)}, bf16[2,144,576]{2,1,0:T(8,128)(2,1)S(1)}, u32[]{:S(2)}, u32[]{:S(2)}) collective-permute-start(bf16[2,144,576]{2,1,0:T(8,128)(2,1)S(1)} %maximum_select_fusion.1), channel_id=1, source_target_pairs={{0,64},{32,96},{64,0},{96,32},{1,65},{33,97},{65,1},{97,33},{2,66}... | collective-permute-start | bytes 995336 | tf_op jit(solution)/shard_map/ppermute | solution.py:23
  49.0 13.6 %collective-permute-start.13 = (bf16[2,144,576]{2,1,0:T(8,128)(2,1)S(1)}, bf16[2,144,576]{2,1,0:T(8,128)(2,1)S(1)}, u32[]{:S(2)}, u32[]{:S(2)}) collective-permute-start(bf16[2,144,576]{2,1,0:T(8,128)(2,1)S(1)} %maximum_select_fusion.1), channel_id=1, source_target_pairs={{0,96},{32,0},{64,32},{96,64},{1,97},{33,1},{65,33},{97,65},{2,98}... | collective-permute-start | bytes 995336 | tf_op jit(solution)/shard_map/ppermute | solution.py:23
  52.4 10.2 %collective-permute-start.11 = (bf16[2,64,576]{2,1,0:T(8,128)(2,1)S(1)}, bf16[2,64,576]{2,1,0:T(8,128)(2,1)S(1)}, u32[]{:S(2)}, u32[]{:S(2)}) collective-permute-start(bf16[2,64,576]{2,1,0:T(8,128)(2,1)S(1)} %get-tuple-element.82), channel_id=1, source_target_pairs={{0,128},{128,0},{1,129},{129,1},{2,130},{130,2},{3,131},{131,3},{4... | collective-permute-start | bytes 442376 | tf_op jit(solution)/shard_map/ppermute | solution.py:23
  72.0 22.9 %collective-permute-start.17 = (bf16[2304,256]{1,0:T(8,128)(2,1)S(1)}, bf16[2304,256]{1,0:T(8,128)(2,1)S(1)}, u32[]{:S(2)}, u32[]{:S(2)}) collective-permute-start(bf16[2304,256]{1,0:T(8,128)(2,1)S(1)} %convolution_convert_fusion), channel_id=1, source_target_pairs={{0,16},{16,0},{1,17},{17,1},{2,18},{18,2},{3,19},{19,3},{4,20},{20... | collective-permute-start | bytes 3538952 | tf_op jit(solution)/shard_map/ppermute | solution.py:23
  72.4 6.9 %collective-permute-start.21 = (f32[256]{0:T(256)S(1)}, f32[256]{0:T(256)S(1)}, u32[]{:S(2)}, u32[]{:S(2)}) collective-permute-start(f32[256]{0:T(256)S(1)} %slice.244), channel_id=1, source_target_pairs={{0,16},{16,0},{1,17},{17,1},{2,18},{18,2},{3,19},{19,3},{4,20},{20... | collective-permute-start | bytes 3080 | tf_op jit(solution)/shard_map/ppermute | solution.py:23
  73.8 11.1 %collective-permute-start.18 = (bf16[288,576]{1,0:T(8,128)(2,1)S(1)}, bf16[288,576]{1,0:T(8,128)(2,1)S(1)}, u32[]{:S(2)}, u32[]{:S(2)}) collective-permute-start(bf16[288,576]{1,0:T(8,128)(2,1)S(1)} %convolution_convert_fusion.6), channel_id=1, source_target_pairs={{0,32},{32,64},{64,96},{96,0},{1,33},{33,65},{65,97},{97,1},{2,34}... | collective-permute-start | bytes 995336 | tf_op jit(solution)/shard_map/ppermute | solution.py:23
  75.7 10.2 %collective-permute-start.19 = (bf16[288,576]{1,0:T(8,128)(2,1)S(1)}, bf16[288,576]{1,0:T(8,128)(2,1)S(1)}, u32[]{:S(2)}, u32[]{:S(2)}) collective-permute-start(bf16[288,576]{1,0:T(8,128)(2,1)S(1)} %convolution_convert_fusion.5), channel_id=1, source_target_pairs={{0,96},{32,0},{64,32},{96,64},{1,97},{33,1},{65,33},{97,65},{2,98}... | collective-permute-start | bytes 995336 | tf_op jit(solution)/shard_map/ppermute | solution.py:23
  76.5 17.9 %collective-permute-start.20 = (bf16[288,576]{1,0:T(8,128)(2,1)S(1)}, bf16[288,576]{1,0:T(8,128)(2,1)S(1)}, u32[]{:S(2)}, u32[]{:S(2)}) collective-permute-start(bf16[288,576]{1,0:T(8,128)(2,1)S(1)} %convolution_convert_fusion.4), channel_id=1, source_target_pairs={{0,64},{32,96},{64,0},{96,32},{1,65},{33,97},{65,1},{97,33},{2,66}... | collective-permute-start | bytes 995336 | tf_op jit(solution)/shard_map/ppermute | solution.py:23
  96.5 19.1 %collective-permute-start.22 = (bf16[592,256]{1,0:T(8,128)(2,1)S(1)}, bf16[592,256]{1,0:T(8,128)(2,1)S(1)}, u32[]{:S(2)}, u32[]{:S(2)}) collective-permute-start(bf16[592,256]{1,0:T(8,128)(2,1)S(1)} %get-tuple-element.93), channel_id=1, source_target_pairs={{0,1},{1,2},{2,3},{3,0},{4,5},{5,6},{6,7},{7,4},{8,9},{9,10},{10,1... | collective-permute-start | bytes 909320 | tf_op jit(solution)/shard_map/ppermute | solution.py:23
  97.5 18.1 %collective-permute-start.23 = (bf16[592,256]{1,0:T(8,128)(2,1)S(1)}, bf16[592,256]{1,0:T(8,128)(2,1)S(1)}, u32[]{:S(2)}, u32[]{:S(2)}) collective-permute-start(bf16[592,256]{1,0:T(8,128)(2,1)S(1)} %get-tuple-element.94), channel_id=1, source_target_pairs={{0,3},{1,0},{2,1},{3,2},{4,7},{5,4},{6,5},{7,6},{8,11},{9,8},{10,9... | collective-permute-start | bytes 909320 | tf_op jit(solution)/shard_map/ppermute | solution.py:23
  100.3 15.3 %collective-permute-start.24 = (bf16[592,256]{1,0:T(8,128)(2,1)S(1)}, bf16[592,256]{1,0:T(8,128)(2,1)S(1)}, u32[]{:S(2)}, u32[]{:S(2)}) collective-permute-start(bf16[592,256]{1,0:T(8,128)(2,1)S(1)} %get-tuple-element.95), channel_id=1, source_target_pairs={{0,2},{1,3},{2,0},{3,1},{4,6},{5,7},{6,4},{7,5},{8,10},{9,11},{10,... | collective-permute-start | bytes 909320 | tf_op jit(solution)/shard_map/ppermute | solution.py:23
  102.2 13.5 %collective-permute-start.25 = (bf16[144,576]{1,0:T(8,128)(2,1)S(1)}, bf16[144,576]{1,0:T(8,128)(2,1)S(1)}, u32[]{:S(2)}, u32[]{:S(2)}) collective-permute-start(bf16[144,576]{1,0:T(8,128)(2,1)S(1)} %get-tuple-element.133), channel_id=1, source_target_pairs={{0,128},{128,0},{1,129},{129,1},{2,130},{130,2},{3,131},{131,3},{4... | collective-permute-start | bytes 497672 | tf_op jit(solution)/shard_map/ppermute | solution.py:23
  115.9 6.1 %collective-permute-start.26 = (bf16[160,256]{1,0:T(8,128)(2,1)S(1)}, bf16[160,256]{1,0:T(8,128)(2,1)S(1)}, u32[]{:S(2)}, u32[]{:S(2)}) collective-permute-start(bf16[160,256]{1,0:T(8,128)(2,1)S(1)} %get-tuple-element.154), channel_id=1, source_target_pairs={{0,4},{4,8},{8,12},{12,0},{1,5},{5,9},{9,13},{13,1},{2,6},{6,10},{... | collective-permute-start | bytes 245768 | tf_op jit(solution)/shard_map/ppermute | solution.py:23
  116.2 6.0 %collective-permute-start.27 = (bf16[160,256]{1,0:T(8,128)(2,1)S(1)}, bf16[160,256]{1,0:T(8,128)(2,1)S(1)}, u32[]{:S(2)}, u32[]{:S(2)}) collective-permute-start(bf16[160,256]{1,0:T(8,128)(2,1)S(1)} %get-tuple-element.155), channel_id=1, source_target_pairs={{0,12},{4,0},{8,4},{12,8},{1,13},{5,1},{9,5},{13,9},{2,14},{6,2},{... | collective-permute-start | bytes 245768 | tf_op jit(solution)/shard_map/ppermute | solution.py:23
  119.3 11.8 %collective-permute-start.29 = (bf16[288,576]{1,0:T(8,128)(2,1)S(1)}, bf16[288,576]{1,0:T(8,128)(2,1)S(1)}, u32[]{:S(2)}, u32[]{:S(2)}) collective-permute-start(bf16[288,576]{1,0:T(8,128)(2,1)S(1)} %convolution_convert_fusion.3), channel_id=1, source_target_pairs={{0,32},{32,64},{64,96},{96,0},{1,33},{33,65},{65,97},{97,1},{2,34}... | collective-permute-start | bytes 995336 | tf_op jit(solution)/shard_map/ppermute | solution.py:23
  120.2 10.9 %collective-permute-start.35 = (bf16[288,576]{1,0:T(8,128)(2,1)S(1)}, bf16[288,576]{1,0:T(8,128)(2,1)S(1)}, u32[]{:S(2)}, u32[]{:S(2)}) collective-permute-start(bf16[288,576]{1,0:T(8,128)(2,1)S(1)} %convolution_convert_fusion.2), channel_id=1, source_target_pairs={{0,96},{32,0},{64,32},{96,64},{1,97},{33,1},{65,33},{97,65},{2,98}... | collective-permute-start | bytes 995336 | tf_op jit(solution)/shard_map/ppermute | solution.py:23
  122.1 12.1 %collective-permute-start.36 = (bf16[288,576]{1,0:T(8,128)(2,1)S(1)}, bf16[288,576]{1,0:T(8,128)(2,1)S(1)}, u32[]{:S(2)}, u32[]{:S(2)}) collective-permute-start(bf16[288,576]{1,0:T(8,128)(2,1)S(1)} %convolution_convert_fusion.1), channel_id=1, source_target_pairs={{0,64},{32,96},{64,0},{96,32},{1,65},{33,97},{65,1},{97,33},{2,66}... | collective-permute-start | bytes 995336 | tf_op jit(solution)/shard_map/ppermute | solution.py:23
  122.2 34.5 %collective-permute-start.37 = (bf16[144,576]{1,0:T(8,128)(2,1)S(1)}, bf16[144,576]{1,0:T(8,128)(2,1)S(1)}, u32[]{:S(2)}, u32[]{:S(2)}) collective-permute-start(bf16[144,576]{1,0:T(8,128)(2,1)S(1)} %get-tuple-element.132), channel_id=1, source_target_pairs={{0,128},{128,0},{1,129},{129,1},{2,130},{130,2},{3,131},{131,3},{4... | collective-permute-start | bytes 497672 | tf_op jit(solution)/shard_map/ppermute | solution.py:23
  134.6 6.9 %collective-permute-start.30 = (bf16[160,128]{1,0:T(8,128)(2,1)S(1)}, bf16[160,128]{1,0:T(8,128)(2,1)S(1)}, u32[]{:S(2)}, u32[]{:S(2)}) collective-permute-start(bf16[160,128]{1,0:T(8,128)(2,1)S(1)} %pad_maximum_fusion.11), channel_id=1, source_target_pairs={{0,128},{128,0},{1,129},{129,1},{2,130},{130,2},{3,131},{131,3},{4... | collective-permute-start | bytes 122888 | tf_op jit(solution)/shard_map/ppermute | solution.py:23
  137.1 19.5 %collective-permute-start.38 = (bf16[2,144,576]{2,1,0:T(8,128)(2,1)S(1)}, bf16[2,144,576]{2,1,0:T(8,128)(2,1)S(1)}, u32[]{:S(2)}, u32[]{:S(2)}) collective-permute-start(bf16[2,144,576]{2,1,0:T(8,128)(2,1)S(1)} %pad_maximum_fusion.6), channel_id=1, source_target_pairs={{0,16},{16,0},{1,17},{17,1},{2,18},{18,2},{3,19},{19,3},{4,20},{20... | collective-permute-start | bytes 995336 | tf_op jit(solution)/shard_map/ppermute | solution.py:23
  141.5 7.4 %collective-permute-start.31 = (f32[144]{0:T(256)S(1)}, f32[144]{0:T(256)S(1)}, u32[]{:S(2)}, u32[]{:S(2)}) collective-permute-start(f32[144]{0:T(256)S(1)} %slice_add_fusion.1), channel_id=1, source_target_pairs={{0,16},{16,0},{1,17},{17,1},{2,18},{18,2},{3,19},{19,3},{4,20},{20... | collective-permute-start | bytes 1736 | tf_op jit(solution)/shard_map/ppermute | solution.py:23
  (12 other events, 88.9 us)

commit v4 on v0

--- a/solution.py
+++ b/solution.py
@@ -73,10 +73,8 @@
             thin = []
             for ref in (first, second):
                 tail = ref[:, pl.ds(4 * main, 4 * rest)]
-                pick = tail[:, :rest]
-                for k in range(1, 4):
-                    pick = jnp.where(q == k, tail[:, k * rest : (k + 1) * rest], pick)
-                thin.append(pick)
+                turn = pltpu.roll(tail.astype(F32), ((4 - q) & 3) * rest, 1)
+                thin.append(turn[:, :rest].astype(BF16))
             out[:, pl.ds(2 * main, 2 * rest)] = jnp.concatenate(thin, axis=1)
 
 
@@ -191,6 +189,7 @@
     sec_to = {by: (sec + by) & 3 for by in range(4)}
     tp_to = {by: (tp + by) & 3 for by in range(4)}
     offset = (tp * 4 + sec) * own_rows
+    tp_to, offset, hidden_grad = barrier((tp_to, offset, hidden_grad))
 
     own_t = tokens.T
     far_t = swapped(own_t, "zh")
@@ -207,6 +206,7 @@
     near_got = [turned(near, "x", by) for by in steps]
 
     both = jnp.concatenate([own_t, far_t], axis=1)
+    both, near_got[0], near_got[1] = barrier((both, near_got[0], near_got[1]))
     section_got = [turned(both, "sec", by) for by in steps]
 
     near_got[0], near_got[1], backs, late_first = barrier(
@@ -227,7 +227,8 @@
     inv_rms = lax.rsqrt(jnp.mean(wide * wide, axis=0) + EPS)
     normed = (wide * inv_rms * norm_gain[:, None]).astype(BF16)
     normed, away_got[0] = barrier((normed, away_got[0]))
-    normed = jnp.concatenate([normed, swapped(normed, "core")], axis=1)
+    normed_other, away_got[2] = barrier((swapped(normed, "core"), away_got[2]))
+    normed = jnp.concatenate([normed, normed_other], axis=1)
 
     backs, *away_got = barrier((backs, *away_got))
     full = jnp.zeros((2, 4, 2, rows, width // 2), BF16)

time: 161 us -> 152 us (0.944)
  the two profiles are of different devices: /device:TPU:24 before, /device:TPU:1 now
where the time goes in v4:
time: 152 us
  starting transfers between devices  82.8 us (54%)
  waiting for transfers between devices  47.5 us (31%)
  matrix products  7.46 us (5%)
  Pallas kernels  4.93 us (3%)
  other arithmetic  4.32 us (3%)
  local copies, waits for them, and re-layouts  3.37 us (2%)
    ppermute x39, starting transfers between devices, turned(): return lax.ppermute(array, axis, [(i, (i + by) % n) for i in range(n)])  82.8 us
    ppermute x39, waiting for transfers between devices, turned(): return lax.ppermute(array, axis, [(i, (i + by) % n) for i in range(n)])  47.5 us
    dot_general x8, matrix products, part(): jnp.dot(as_block(by_rows, zplace, xplace), d_both, preferred_element_type...  3.15 us
  transfers between devices with their start and end apart: 39, of which 15 were waited for; matrix products, arithmetic and copies ran while one was open for 5% of the time, Pallas kernels for 1%

profile of v4, /device:TPU:1, one launch (start us, length us, event | category | flops | bytes accessed | tf_op | source)
XLA Modules:
  0.0 151.7 jit_solution(6414996505742693957)
XLA Ops:
  2.0 3.3 %collective-permute-start = (bf16[208,576]{1,0:T(8,128)(2,1)S(1)}, bf16[208,576]{1,0:T(8,128)(2,1)S(1)}, u32[]{:S(2)}, u32[]{:S(2)}) collective-permute-start(bf16[208,576]{1,0:T(8,128)(2,1)S(1)} %get-tuple-element.63), channel_id=1, source_target_pairs={{0,16},{16,0},{1,17},{17,1},{2,18},{18,2},{3,19},{19,3},{4,20},{20... | collective-permute-start | bytes 718856 | tf_op jit(solution)/shard_map/ppermute | solution.py:23
  5.3 5.2 %collective-permute-start.1 = (bf16[576,128]{1,0:T(8,128)(2,1)}, bf16[576,128]{1,0:T(8,128)(2,1)S(1)}, u32[]{:S(2)}, u32[]{:S(2)}) collective-permute-start(bf16[576,128]{1,0:T(8,128)(2,1)} %bitcast.142), channel_id=1, source_target_pairs={{0,128},{128,0},{1,129},{129,1},{2,130},{130,2},{3,131},{131,3},{4... | collective-permute-start | bytes 442376 | tf_op jit(solution)/shard_map/ppermute | solution.py:23
  12.5 2.4 %collective-permute-done.1 = bf16[576,128]{1,0:T(8,128)(2,1)S(1)} collective-permute-done((bf16[576,128]{1,0:T(8,128)(2,1)}, bf16[576,128]{1,0:T(8,128)(2,1)S(1)}, u32[]{:S(2)}, u32[]{:S(2)}) %collective-permute-start.1) | collective-permute-done | bytes 147488 | tf_op jit(solution)/shard_map/ppermute | solution.py:23
  14.9 5.2 %collective-permute-start.5 = (bf16[144,576]{1,0:T(8,128)(2,1)S(1)}, bf16[144,576]{1,0:T(8,128)(2,1)S(1)}, u32[]{:S(2)}, u32[]{:S(2)}) collective-permute-start(bf16[144,576]{1,0:T(8,128)(2,1)S(1)} %get-tuple-element.75), channel_id=1, source_target_pairs={{0,128},{128,0},{1,129},{129,1},{2,130},{130,2},{3,131},{131,3},{4... | collective-permute-start | bytes 497672 | tf_op jit(solution)/shard_map/ppermute | solution.py:23
  24.8 10.1 %collective-permute-done.5 = bf16[144,576]{1,0:T(8,128)(2,1)S(1)} collective-permute-done((bf16[144,576]{1,0:T(8,128)(2,1)S(1)}, bf16[144,576]{1,0:T(8,128)(2,1)S(1)}, u32[]{:S(2)}, u32[]{:S(2)}) %collective-permute-start.5) | collective-permute-done | bytes 165920 | tf_op jit(solution)/shard_map/ppermute | solution.py:23
  37.6 1.5 %collective-permute-start.8 = (bf16[576,256]{1,0:T(8,128)(2,1)S(1)}, bf16[576,256]{1,0:T(8,128)(2,1)S(1)}, u32[]{:S(2)}, u32[]{:S(2)}) collective-permute-start(bf16[576,256]{1,0:T(8,128)(2,1)S(1)} %pad_maximum_fusion.7), channel_id=1, source_target_pairs={{0,3},{1,0},{2,1},{3,2},{4,7},{5,4},{6,5},{7,6},{8,11},{9,8},{10,9... | collective-permute-start | bytes 884744 | tf_op jit(solution)/shard_map/ppermute | solution.py:23
  39.1 1.6 %collective-permute-start.9 = (bf16[576,256]{1,0:T(8,128)(2,1)S(1)}, bf16[576,256]{1,0:T(8,128)(2,1)S(1)}, u32[]{:S(2)}, u32[]{:S(2)}) collective-permute-start(bf16[576,256]{1,0:T(8,128)(2,1)S(1)} %pad_maximum_fusion.7), channel_id=1, source_target_pairs={{0,2},{1,3},{2,0},{3,1},{4,6},{5,7},{6,4},{7,5},{8,10},{9,11},{10,... | collective-permute-start | bytes 884744 | tf_op jit(solution)/shard_map/ppermute | solution.py:23
  43.2 5.8 %collective-permute-start.15 = (bf16[2,144,576]{2,1,0:T(8,128)(2,1)S(1)}, bf16[2,144,576]{2,1,0:T(8,128)(2,1)S(1)}, u32[]{:S(2)}, u32[]{:S(2)}) collective-permute-start(bf16[2,144,576]{2,1,0:T(8,128)(2,1)S(1)} %maximum_select_fusion.1), channel_id=1, source_target_pairs={{0,64},{32,96},{64,0},{96,32},{1,65},{33,97},{65,1},{97,33},{2,66}... | collective-permute-start | bytes 995336 | tf_op jit(solution)/shard_map/ppermute | solution.py:23
  49.2 3.2 %collective-permute-done.9 = bf16[576,256]{1,0:T(8,128)(2,1)S(1)} collective-permute-done((bf16[576,256]{1,0:T(8,128)(2,1)S(1)}, bf16[576,256]{1,0:T(8,128)(2,1)S(1)}, u32[]{:S(2)}, u32[]{:S(2)}) %collective-permute-start.9) | collective-permute-done | bytes 294944 | tf_op jit(solution)/shard_map/ppermute | solution.py:23
  52.4 4.5 %collective-permute-start.11 = (bf16[2,64,576]{2,1,0:T(8,128)(2,1)S(1)}, bf16[2,64,576]{2,1,0:T(8,128)(2,1)S(1)}, u32[]{:S(2)}, u32[]{:S(2)}) collective-permute-start(bf16[2,64,576]{2,1,0:T(8,128)(2,1)S(1)} %get-tuple-element.84), channel_id=1, source_target_pairs={{0,128},{128,0},{1,129},{129,1},{2,130},{130,2},{3,131},{131,3},{4... | collective-permute-start | bytes 442376 | tf_op jit(solution)/shard_map/ppermute | solution.py:23
  57.7 2.4 %collective-permute-start.14 = (bf16[2304,256]{1,0:T(8,128)(2,1)S(1)}, bf16[2304,256]{1,0:T(8,128)(2,1)S(1)}, u32[]{:S(2)}, u32[]{:S(2)}) collective-permute-start(bf16[2304,256]{1,0:T(8,128)(2,1)S(1)} %multiply_convert_fusion), channel_id=1, source_target_pairs={{0,16},{16,0},{1,17},{17,1},{2,18},{18,2},{3,19},{19,3},{4,20},{20... | collective-permute-start | bytes 3538952 | tf_op jit(solution)/shard_map/ppermute | solution.py:23
  60.4 2.2 %collective-permute-done.14 = bf16[2304,256]{1,0:T(8,128)(2,1)S(1)} collective-permute-done((bf16[2304,256]{1,0:T(8,128)(2,1)S(1)}, bf16[2304,256]{1,0:T(8,128)(2,1)S(1)}, u32[]{:S(2)}, u32[]{:S(2)}) %collective-permute-start.14) | collective-permute-done | bytes 1179680 | tf_op jit(solution)/shard_map/ppermute | solution.py:23
  63.0 2.1 %fusion.84 = f32[512,576]{1,0:T(8,128)S(1)} fusion(bf16[2304,512]{1,0:T(8,128)(2,1)S(1)} %constant_dynamic-update-slice_fusion, bf16[2304,576]{1,0:T(8,128)(2,1)S(1)} %bitcast.116), kind=kOutput, calls=%fused_computation.191 | convolution fusion | flops 1358954496 | bytes 6193152 | tf_op jit(solution)/shard_map/dot_general | solution.py:248
  65.2 2.4 %collective-permute-start.16 = (bf16[64,576]{1,0:T(8,128)(2,1)S(1)}, bf16[64,576]{1,0:T(8,128)(2,1)S(1)}, u32[]{:S(2)}, u32[]{:S(2)}) collective-permute-start(bf16[64,576]{1,0:T(8,128)(2,1)S(1)} %get-tuple-element.146), channel_id=1, source_target_pairs={{0,16},{16,0},{1,17},{17,1},{2,18},{18,2},{3,19},{19,3},{4,20},{20... | collective-permute-start | bytes 221192 | tf_op jit(solution)/shard_map/ppermute | solution.py:23
  73.9 2.0 %collective-permute-start.19 = (bf16[288,576]{1,0:T(8,128)(2,1)S(1)}, bf16[288,576]{1,0:T(8,128)(2,1)S(1)}, u32[]{:S(2)}, u32[]{:S(2)}) collective-permute-start(bf16[288,576]{1,0:T(8,128)(2,1)S(1)} %convolution_convert_fusion.5), channel_id=1, source_target_pairs={{0,96},{32,0},{64,32},{96,64},{1,97},{33,1},{65,33},{97,65},{2,98}... | collective-permute-start | bytes 995336 | tf_op jit(solution)/shard_map/ppermute | solution.py:23
  77.3 7.2 %collective-permute-done.19 = bf16[288,576]{1,0:T(8,128)(2,1)S(1)} collective-permute-done((bf16[288,576]{1,0:T(8,128)(2,1)S(1)}, bf16[288,576]{1,0:T(8,128)(2,1)S(1)}, u32[]{:S(2)}, u32[]{:S(2)}) %collective-permute-start.19) | collective-permute-done | bytes 331808 | tf_op jit(solution)/shard_map/ppermute | solution.py:23
  84.4 2.1 %collective-permute-done.18 = bf16[288,576]{1,0:T(8,128)(2,1)S(1)} collective-permute-done((bf16[288,576]{1,0:T(8,128)(2,1)S(1)}, bf16[288,576]{1,0:T(8,128)(2,1)S(1)}, u32[]{:S(2)}, u32[]{:S(2)}) %collective-permute-start.18) | collective-permute-done | bytes 331808 | tf_op jit(solution)/shard_map/ppermute | solution.py:23
  87.0 3.2 %collective-permute-start.22 = (bf16[592,256]{1,0:T(8,128)(2,1)S(1)}, bf16[592,256]{1,0:T(8,128)(2,1)S(1)}, u32[]{:S(2)}, u32[]{:S(2)}) collective-permute-start(bf16[592,256]{1,0:T(8,128)(2,1)S(1)} %get-tuple-element.94), channel_id=1, source_target_pairs={{0,3},{1,0},{2,1},{3,2},{4,7},{5,4},{6,5},{7,6},{8,11},{9,8},{10,9... | collective-permute-start | bytes 909320 | tf_op jit(solution)/shard_map/ppermute | solution.py:23
  90.2 1.7 %collective-permute-start.23 = (bf16[592,256]{1,0:T(8,128)(2,1)S(1)}, bf16[592,256]{1,0:T(8,128)(2,1)S(1)}, u32[]{:S(2)}, u32[]{:S(2)}) collective-permute-start(bf16[592,256]{1,0:T(8,128)(2,1)S(1)} %get-tuple-element.95), channel_id=1, source_target_pairs={{0,2},{1,3},{2,0},{3,1},{4,6},{5,7},{6,4},{7,5},{8,10},{9,11},{10,... | collective-permute-start | bytes 909320 | tf_op jit(solution)/shard_map/ppermute | solution.py:23
  93.3 3.0 %collective-permute-done.21 = bf16[592,256]{1,0:T(8,128)(2,1)S(1)} collective-permute-done((bf16[592,256]{1,0:T(8,128)(2,1)S(1)}, bf16[592,256]{1,0:T(8,128)(2,1)S(1)}, u32[]{:S(2)}, u32[]{:S(2)}) %collective-permute-start.21) | collective-permute-done | bytes 303136 | tf_op jit(solution)/shard_map/ppermute | solution.py:23
  96.2 7.4 %collective-permute-done.23 = bf16[592,256]{1,0:T(8,128)(2,1)S(1)} collective-permute-done((bf16[592,256]{1,0:T(8,128)(2,1)S(1)}, bf16[592,256]{1,0:T(8,128)(2,1)S(1)}, u32[]{:S(2)}, u32[]{:S(2)}) %collective-permute-start.23) | collective-permute-done | bytes 303136 | tf_op jit(solution)/shard_map/ppermute | solution.py:23
  104.1 1.9 %collective-permute-start.25 = (bf16[160,256]{1,0:T(8,128)(2,1)S(1)}, bf16[160,256]{1,0:T(8,128)(2,1)S(1)}, u32[]{:S(2)}, u32[]{:S(2)}) collective-permute-start(bf16[160,256]{1,0:T(8,128)(2,1)S(1)} %get-tuple-element.158), channel_id=1, source_target_pairs={{0,4},{4,8},{8,12},{12,0},{1,5},{5,9},{9,13},{13,1},{2,6},{6,10},{... | collective-permute-start | bytes 245768 | tf_op jit(solution)/shard_map/ppermute | solution.py:23
  107.5 2.7 %collective-permute-start.29 = (bf16[288,576]{1,0:T(8,128)(2,1)S(1)}, bf16[288,576]{1,0:T(8,128)(2,1)S(1)}, u32[]{:S(2)}, u32[]{:S(2)}) collective-permute-start(bf16[288,576]{1,0:T(8,128)(2,1)S(1)} %convolution_convert_fusion.2), channel_id=1, source_target_pairs={{0,96},{32,0},{64,32},{96,64},{1,97},{33,1},{65,33},{97,65},{2,98}... | collective-permute-start | bytes 995336 | tf_op jit(solution)/shard_map/ppermute | solution.py:23
  110.3 2.1 %collective-permute-start.37 = (bf16[144,576]{1,0:T(8,128)(2,1)S(1)}, bf16[144,576]{1,0:T(8,128)(2,1)S(1)}, u32[]{:S(2)}, u32[]{:S(2)}) collective-permute-start(bf16[144,576]{1,0:T(8,128)(2,1)S(1)} %get-tuple-element.136), channel_id=1, source_target_pairs={{0,128},{128,0},{1,129},{129,1},{2,130},{130,2},{3,131},{131,3},{4... | collective-permute-start | bytes 497672 | tf_op jit(solution)/shard_map/ppermute | solution.py:23
  112.4 2.7 %collective-permute-done.27 = bf16[160,256]{1,0:T(8,128)(2,1)S(1)} collective-permute-done((bf16[160,256]{1,0:T(8,128)(2,1)S(1)}, bf16[160,256]{1,0:T(8,128)(2,1)S(1)}, u32[]{:S(2)}, u32[]{:S(2)}) %collective-permute-start.27) | collective-permute-done | bytes 81952 | tf_op jit(solution)/shard_map/ppermute | solution.py:23
  116.9 4.1 %collective-permute-start.30 = (bf16[160,128]{1,0:T(8,128)(2,1)S(1)}, bf16[160,128]{1,0:T(8,128)(2,1)S(1)}, u32[]{:S(2)}, u32[]{:S(2)}) collective-permute-start(bf16[160,128]{1,0:T(8,128)(2,1)S(1)} %pad_maximum_fusion.11), channel_id=1, source_target_pairs={{0,128},{128,0},{1,129},{129,1},{2,130},{130,2},{3,131},{131,3},{4... | collective-permute-start | bytes 122888 | tf_op jit(solution)/shard_map/ppermute | solution.py:23
  121.0 2.2 %collective-permute-done.35 = bf16[288,576]{1,0:T(8,128)(2,1)S(1)} collective-permute-done((bf16[288,576]{1,0:T(8,128)(2,1)S(1)}, bf16[288,576]{1,0:T(8,128)(2,1)S(1)}, u32[]{:S(2)}, u32[]{:S(2)}) %collective-permute-start.35) | collective-permute-done | bytes 331808 | tf_op jit(solution)/shard_map/ppermute | solution.py:23
  123.7 10.3 %collective-permute-start.38 = (bf16[2,144,576]{2,1,0:T(8,128)(2,1)S(1)}, bf16[2,144,576]{2,1,0:T(8,128)(2,1)S(1)}, u32[]{:S(2)}, u32[]{:S(2)}) collective-permute-start(bf16[2,144,576]{2,1,0:T(8,128)(2,1)S(1)} %pad_maximum_fusion.6), channel_id=1, source_target_pairs={{0,16},{16,0},{1,17},{17,1},{2,18},{18,2},{3,19},{19,3},{4,20},{20... | collective-permute-start | bytes 995336 | tf_op jit(solution)/shard_map/ppermute | solution.py:23
  134.3 2.6 %collective-permute-start.31 = (f32[144]{0:T(256)S(1)}, f32[144]{0:T(256)S(1)}, u32[]{:S(2)}, u32[]{:S(2)}) collective-permute-start(f32[144]{0:T(256)S(1)} %slice_add_fusion.1), channel_id=1, source_target_pairs={{0,16},{16,0},{1,17},{17,1},{2,18},{18,2},{3,19},{19,3},{4,20},{20... | collective-permute-start | bytes 1736 | tf_op jit(solution)/shard_map/ppermute | solution.py:23
  137.7 4.6 %collective-permute-start.32 = (f32[144]{0:T(256)S(1)}, f32[144]{0:T(256)S(1)}, u32[]{:S(2)}, u32[]{:S(2)}) collective-permute-start(f32[144]{0:T(256)S(1)} %add.232), channel_id=1, source_target_pairs={{0,32},{32,64},{64,96},{96,0},{1,33},{33,65},{65,97},{97,1},{2,34}... | collective-permute-start | bytes 1736 | tf_op jit(solution)/shard_map/ppermute | solution.py:23
  145.4 2.0 %collective-permute-done.34 = f32[144]{0:T(256)S(1)} collective-permute-done((f32[144]{0:T(256)S(1)}, f32[144]{0:T(256)S(1)}, u32[]{:S(2)}, u32[]{:S(2)}) %collective-permute-start.34) | collective-permute-done | bytes 608 | tf_op jit(solution)/shard_map/ppermute | solution.py:23
  149.4 2.2 %join.1 = (bf16[144,1152]{1,0:T(8,128)(2,1)}, bf16[144,1152]{1,0:T(8,128)(2,1)}) custom-call(bf16[2,144,576]{2,1,0:T(8,128)(2,1)} %bitcast.132, bf16[144,576]{1,0:T(8,128)(2,1)} %copy-done.2, bf16[2,144,576]{2,1,0:T(8,128)(2,1)} %copy-done.1), custom_call_target="tpu_custom_call" | custom-call | tf_op jit(solution)/shard_map/join/pallas_call | solution.py:122
  (157 shorter events, 34.4 us)
Async XLA Ops:
  2.0 18.1 %collective-permute-start = (bf16[208,576]{1,0:T(8,128)(2,1)S(1)}, bf16[208,576]{1,0:T(8,128)(2,1)S(1)}, u32[]{:S(2)}, u32[]{:S(2)}) collective-permute-start(bf16[208,576]{1,0:T(8,128)(2,1)S(1)} %get-tuple-element.63), channel_id=1, source_target_pairs={{0,16},{16,0},{1,17},{17,1},{2,18},{18,2},{3,19},{19,3},{4,20},{20... | collective-permute-start | bytes 718856 | tf_op jit(solution)/shard_map/ppermute | solution.py:23
  5.3 9.5 %collective-permute-start.1 = (bf16[576,128]{1,0:T(8,128)(2,1)}, bf16[576,128]{1,0:T(8,128)(2,1)S(1)}, u32[]{:S(2)}, u32[]{:S(2)}) collective-permute-start(bf16[576,128]{1,0:T(8,128)(2,1)} %bitcast.142), channel_id=1, source_target_pairs={{0,128},{128,0},{1,129},{129,1},{2,130},{130,2},{3,131},{131,3},{4... | collective-permute-start | bytes 442376 | tf_op jit(solution)/shard_map/ppermute | solution.py:23
  11.9 27.2 %collective-permute-start.4 = (bf16[144,576]{1,0:T(8,128)(2,1)S(1)}, bf16[144,576]{1,0:T(8,128)(2,1)S(1)}, u32[]{:S(2)}, u32[]{:S(2)}) collective-permute-start(bf16[144,576]{1,0:T(8,128)(2,1)S(1)} %get-tuple-element.74), channel_id=1, source_target_pairs={{0,128},{128,0},{1,129},{129,1},{2,130},{130,2},{3,131},{131,3},{4... | collective-permute-start | bytes 497672 | tf_op jit(solution)/shard_map/ppermute | solution.py:23
  14.9 20.0 %collective-permute-start.5 = (bf16[144,576]{1,0:T(8,128)(2,1)S(1)}, bf16[144,576]{1,0:T(8,128)(2,1)S(1)}, u32[]{:S(2)}, u32[]{:S(2)}) collective-permute-start(bf16[144,576]{1,0:T(8,128)(2,1)S(1)} %get-tuple-element.75), channel_id=1, source_target_pairs={{0,128},{128,0},{1,129},{129,1},{2,130},{130,2},{3,131},{131,3},{4... | collective-permute-start | bytes 497672 | tf_op jit(solution)/shard_map/ppermute | solution.py:23
  20.2 16.0 %collective-permute-start.2 = (bf16[2,144,576]{2,1,0:T(8,128)(2,1)S(1)}, bf16[2,144,576]{2,1,0:T(8,128)(2,1)S(1)}, u32[]{:S(2)}, u32[]{:S(2)}) collective-permute-start(bf16[2,144,576]{2,1,0:T(8,128)(2,1)S(1)} %maximum_select_fusion), channel_id=1, source_target_pairs={{0,32},{32,64},{64,96},{96,0},{1,33},{33,65},{65,97},{97,1},{2,34}... | collective-permute-start | bytes 995336 | tf_op jit(solution)/shard_map/ppermute | solution.py:23
  21.5 14.8 %collective-permute-start.3 = (bf16[2,144,576]{2,1,0:T(8,128)(2,1)S(1)}, bf16[2,144,576]{2,1,0:T(8,128)(2,1)S(1)}, u32[]{:S(2)}, u32[]{:S(2)}) collective-permute-start(bf16[2,144,576]{2,1,0:T(8,128)(2,1)S(1)} %maximum_select_fusion), channel_id=1, source_target_pairs={{0,96},{32,0},{64,32},{96,64},{1,97},{33,1},{65,33},{97,65},{2,98}... | collective-permute-start | bytes 995336 | tf_op jit(solution)/shard_map/ppermute | solution.py:23
  23.0 37.1 %collective-permute-start.10 = (bf16[2,144,576]{2,1,0:T(8,128)(2,1)S(1)}, bf16[2,144,576]{2,1,0:T(8,128)(2,1)S(1)}, u32[]{:S(2)}, u32[]{:S(2)}) collective-permute-start(bf16[2,144,576]{2,1,0:T(8,128)(2,1)S(1)} %maximum_select_fusion), channel_id=1, source_target_pairs={{0,64},{32,96},{64,0},{96,32},{1,65},{33,97},{65,1},{97,33},{2,66}... | collective-permute-start | bytes 995336 | tf_op jit(solution)/shard_map/ppermute | solution.py:23
  34.9 5.7 %collective-permute-start.6 = (bf16[144,576]{1,0:T(8,128)(2,1)S(1)}, bf16[144,576]{1,0:T(8,128)(2,1)S(1)}, u32[]{:S(2)}, u32[]{:S(2)}) collective-permute-start(bf16[144,576]{1,0:T(8,128)(2,1)S(1)} %collective-permute-done.5), channel_id=1, source_target_pairs={{0,16},{16,0},{1,17},{17,1},{2,18},{18,2},{3,19},{19,3},{4,20},{20... | collective-permute-start | bytes 497672 | tf_op jit(solution)/shard_map/ppermute | solution.py:23
  36.3 6.9 %collective-permute-start.7 = (bf16[576,256]{1,0:T(8,128)(2,1)S(1)}, bf16[576,256]{1,0:T(8,128)(2,1)S(1)}, u32[]{:S(2)}, u32[]{:S(2)}) collective-permute-start(bf16[576,256]{1,0:T(8,128)(2,1)S(1)} %pad_maximum_fusion.7), channel_id=1, source_target_pairs={{0,1},{1,2},{2,3},{3,0},{4,5},{5,6},{6,7},{7,4},{8,9},{9,10},{10,1... | collective-permute-start | bytes 884744 | tf_op jit(solution)/shard_map/ppermute | solution.py:23
  37.6 11.5 %collective-permute-start.8 = (bf16[576,256]{1,0:T(8,128)(2,1)S(1)}, bf16[576,256]{1,0:T(8,128)(2,1)S(1)}, u32[]{:S(2)}, u32[]{:S(2)}) collective-permute-start(bf16[576,256]{1,0:T(8,128)(2,1)S(1)} %pad_maximum_fusion.7), channel_id=1, source_target_pairs={{0,3},{1,0},{2,1},{3,2},{4,7},{5,4},{6,5},{7,6},{8,11},{9,8},{10,9... | collective-permute-start | bytes 884744 | tf_op jit(solution)/shard_map/ppermute | solution.py:23
  39.1 13.3 %collective-permute-start.9 = (bf16[576,256]{1,0:T(8,128)(2,1)S(1)}, bf16[576,256]{1,0:T(8,128)(2,1)S(1)}, u32[]{:S(2)}, u32[]{:S(2)}) collective-permute-start(bf16[576,256]{1,0:T(8,128)(2,1)S(1)} %pad_maximum_fusion.7), channel_id=1, source_target_pairs={{0,2},{1,3},{2,0},{3,1},{4,6},{5,7},{6,4},{7,5},{8,10},{9,11},{10,... | collective-permute-start | bytes 884744 | tf_op jit(solution)/shard_map/ppermute | solution.py:23
  40.7 16.9 %collective-permute-start.12 = (bf16[2,144,576]{2,1,0:T(8,128)(2,1)S(1)}, bf16[2,144,576]{2,1,0:T(8,128)(2,1)S(1)}, u32[]{:S(2)}, u32[]{:S(2)}) collective-permute-start(bf16[2,144,576]{2,1,0:T(8,128)(2,1)S(1)} %maximum_select_fusion.1), channel_id=1, source_target_pairs={{0,32},{32,64},{64,96},{96,0},{1,33},{33,65},{65,97},{97,1},{2,34}... | collective-permute-start | bytes 995336 | tf_op jit(solution)/shard_map/ppermute | solution.py:23
  43.2 17.2 %collective-permute-start.15 = (bf16[2,144,576]{2,1,0:T(8,128)(2,1)S(1)}, bf16[2,144,576]{2,1,0:T(8,128)(2,1)S(1)}, u32[]{:S(2)}, u32[]{:S(2)}) collective-permute-start(bf16[2,144,576]{2,1,0:T(8,128)(2,1)S(1)} %maximum_select_fusion.1), channel_id=1, source_target_pairs={{0,64},{32,96},{64,0},{96,32},{1,65},{33,97},{65,1},{97,33},{2,66}... | collective-permute-start | bytes 995336 | tf_op jit(solution)/shard_map/ppermute | solution.py:23
  49.0 13.5 %collective-permute-start.13 = (bf16[2,144,576]{2,1,0:T(8,128)(2,1)S(1)}, bf16[2,144,576]{2,1,0:T(8,128)(2,1)S(1)}, u32[]{:S(2)}, u32[]{:S(2)}) collective-permute-start(bf16[2,144,576]{2,1,0:T(8,128)(2,1)S(1)} %maximum_select_fusion.1), channel_id=1, source_target_pairs={{0,96},{32,0},{64,32},{96,64},{1,97},{33,1},{65,33},{97,65},{2,98}... | collective-permute-start | bytes 995336 | tf_op jit(solution)/shard_map/ppermute | solution.py:23
  52.4 10.2 %collective-permute-start.11 = (bf16[2,64,576]{2,1,0:T(8,128)(2,1)S(1)}, bf16[2,64,576]{2,1,0:T(8,128)(2,1)S(1)}, u32[]{:S(2)}, u32[]{:S(2)}) collective-permute-start(bf16[2,64,576]{2,1,0:T(8,128)(2,1)S(1)} %get-tuple-element.84), channel_id=1, source_target_pairs={{0,128},{128,0},{1,129},{129,1},{2,130},{130,2},{3,131},{131,3},{4... | collective-permute-start | bytes 442376 | tf_op jit(solution)/shard_map/ppermute | solution.py:23
  57.7 4.9 %collective-permute-start.14 = (bf16[2304,256]{1,0:T(8,128)(2,1)S(1)}, bf16[2304,256]{1,0:T(8,128)(2,1)S(1)}, u32[]{:S(2)}, u32[]{:S(2)}) collective-permute-start(bf16[2304,256]{1,0:T(8,128)(2,1)S(1)} %multiply_convert_fusion), channel_id=1, source_target_pairs={{0,16},{16,0},{1,17},{17,1},{2,18},{18,2},{3,19},{19,3},{4,20},{20... | collective-permute-start | bytes 3538952 | tf_op jit(solution)/shard_map/ppermute | solution.py:23
  73.9 10.6 %collective-permute-start.19 = (bf16[288,576]{1,0:T(8,128)(2,1)S(1)}, bf16[288,576]{1,0:T(8,128)(2,1)S(1)}, u32[]{:S(2)}, u32[]{:S(2)}) collective-permute-start(bf16[288,576]{1,0:T(8,128)(2,1)S(1)} %convolution_convert_fusion.5), channel_id=1, source_target_pairs={{0,96},{32,0},{64,32},{96,64},{1,97},{33,1},{65,33},{97,65},{2,98}... | collective-permute-start | bytes 995336 | tf_op jit(solution)/shard_map/ppermute | solution.py:23
  75.8 10.7 %collective-permute-start.18 = (bf16[288,576]{1,0:T(8,128)(2,1)S(1)}, bf16[288,576]{1,0:T(8,128)(2,1)S(1)}, u32[]{:S(2)}, u32[]{:S(2)}) collective-permute-start(bf16[288,576]{1,0:T(8,128)(2,1)S(1)} %convolution_convert_fusion.6), channel_id=1, source_target_pairs={{0,32},{32,64},{64,96},{96,0},{1,33},{33,65},{65,97},{97,1},{2,34}... | collective-permute-start | bytes 995336 | tf_op jit(solution)/shard_map/ppermute | solution.py:23
  86.5 9.7 %collective-permute-start.21 = (bf16[592,256]{1,0:T(8,128)(2,1)S(1)}, bf16[592,256]{1,0:T(8,128)(2,1)S(1)}, u32[]{:S(2)}, u32[]{:S(2)}) collective-permute-start(bf16[592,256]{1,0:T(8,128)(2,1)S(1)} %get-tuple-element.93), channel_id=1, source_target_pairs={{0,1},{1,2},{2,3},{3,0},{4,5},{5,6},{6,7},{7,4},{8,9},{9,10},{10,1... | collective-permute-start | bytes 909320 | tf_op jit(solution)/shard_map/ppermute | solution.py:23
  87.0 9.2 %collective-permute-start.22 = (bf16[592,256]{1,0:T(8,128)(2,1)S(1)}, bf16[592,256]{1,0:T(8,128)(2,1)S(1)}, u32[]{:S(2)}, u32[]{:S(2)}) collective-permute-start(bf16[592,256]{1,0:T(8,128)(2,1)S(1)} %get-tuple-element.94), channel_id=1, source_target_pairs={{0,3},{1,0},{2,1},{3,2},{4,7},{5,4},{6,5},{7,6},{8,11},{9,8},{10,9... | collective-permute-start | bytes 909320 | tf_op jit(solution)/shard_map/ppermute | solution.py:23
  90.2 13.4 %collective-permute-start.23 = (bf16[592,256]{1,0:T(8,128)(2,1)S(1)}, bf16[592,256]{1,0:T(8,128)(2,1)S(1)}, u32[]{:S(2)}, u32[]{:S(2)}) collective-permute-start(bf16[592,256]{1,0:T(8,128)(2,1)S(1)} %get-tuple-element.95), channel_id=1, source_target_pairs={{0,2},{1,3},{2,0},{3,1},{4,6},{5,7},{6,4},{7,5},{8,10},{9,11},{10,... | collective-permute-start | bytes 909320 | tf_op jit(solution)/shard_map/ppermute | solution.py:23
  92.4 11.5 %collective-permute-start.24 = (bf16[288,576]{1,0:T(8,128)(2,1)S(1)}, bf16[288,576]{1,0:T(8,128)(2,1)S(1)}, u32[]{:S(2)}, u32[]{:S(2)}) collective-permute-start(bf16[288,576]{1,0:T(8,128)(2,1)S(1)} %convolution_convert_fusion.4), channel_id=1, source_target_pairs={{0,64},{32,96},{64,0},{96,32},{1,65},{33,97},{65,1},{97,33},{2,66}... | collective-permute-start | bytes 995336 | tf_op jit(solution)/shard_map/ppermute | solution.py:23
  104.1 6.1 %collective-permute-start.25 = (bf16[160,256]{1,0:T(8,128)(2,1)S(1)}, bf16[160,256]{1,0:T(8,128)(2,1)S(1)}, u32[]{:S(2)}, u32[]{:S(2)}) collective-permute-start(bf16[160,256]{1,0:T(8,128)(2,1)S(1)} %get-tuple-element.158), channel_id=1, source_target_pairs={{0,4},{4,8},{8,12},{12,0},{1,5},{5,9},{9,13},{13,1},{2,6},{6,10},{... | collective-permute-start | bytes 245768 | tf_op jit(solution)/shard_map/ppermute | solution.py:23
  107.5 7.7 %collective-permute-start.27 = (bf16[160,256]{1,0:T(8,128)(2,1)S(1)}, bf16[160,256]{1,0:T(8,128)(2,1)S(1)}, u32[]{:S(2)}, u32[]{:S(2)}) collective-permute-start(bf16[160,256]{1,0:T(8,128)(2,1)S(1)} %get-tuple-element.160), channel_id=1, source_target_pairs={{0,8},{4,12},{8,0},{12,4},{1,9},{5,13},{9,1},{13,5},{2,10},{6,14},... | collective-permute-start | bytes 245768 | tf_op jit(solution)/shard_map/ppermute | solution.py:23
  107.5 9.4 %collective-permute-start.28 = (bf16[288,576]{1,0:T(8,128)(2,1)S(1)}, bf16[288,576]{1,0:T(8,128)(2,1)S(1)}, u32[]{:S(2)}, u32[]{:S(2)}) collective-permute-start(bf16[288,576]{1,0:T(8,128)(2,1)S(1)} %convolution_convert_fusion.3), channel_id=1, source_target_pairs={{0,32},{32,64},{64,96},{96,0},{1,33},{33,65},{65,97},{97,1},{2,34}... | collective-permute-start | bytes 995336 | tf_op jit(solution)/shard_map/ppermute | solution.py:23
  107.5 9.4 %collective-permute-start.29 = (bf16[288,576]{1,0:T(8,128)(2,1)S(1)}, bf16[288,576]{1,0:T(8,128)(2,1)S(1)}, u32[]{:S(2)}, u32[]{:S(2)}) collective-permute-start(bf16[288,576]{1,0:T(8,128)(2,1)S(1)} %convolution_convert_fusion.2), channel_id=1, source_target_pairs={{0,96},{32,0},{64,32},{96,64},{1,97},{33,1},{65,33},{97,65},{2,98}... | collective-permute-start | bytes 995336 | tf_op jit(solution)/shard_map/ppermute | solution.py:23
  110.2 13.0 %collective-permute-start.35 = (bf16[288,576]{1,0:T(8,128)(2,1)S(1)}, bf16[288,576]{1,0:T(8,128)(2,1)S(1)}, u32[]{:S(2)}, u32[]{:S(2)}) collective-permute-start(bf16[288,576]{1,0:T(8,128)(2,1)S(1)} %convolution_convert_fusion.1), channel_id=1, source_target_pairs={{0,64},{32,96},{64,0},{96,32},{1,65},{33,97},{65,1},{97,33},{2,66}... | collective-permute-start | bytes 995336 | tf_op jit(solution)/shard_map/ppermute | solution.py:23
  110.3 13.3 %collective-permute-start.37 = (bf16[144,576]{1,0:T(8,128)(2,1)S(1)}, bf16[144,576]{1,0:T(8,128)(2,1)S(1)}, u32[]{:S(2)}, u32[]{:S(2)}) collective-permute-start(bf16[144,576]{1,0:T(8,128)(2,1)S(1)} %get-tuple-element.136), channel_id=1, source_target_pairs={{0,128},{128,0},{1,129},{129,1},{2,130},{130,2},{3,131},{131,3},{4... | collective-permute-start | bytes 497672 | tf_op jit(solution)/shard_map/ppermute | solution.py:23
  115.2 32.8 %collective-permute-start.36 = (bf16[144,576]{1,0:T(8,128)(2,1)S(1)}, bf16[144,576]{1,0:T(8,128)(2,1)S(1)}, u32[]{:S(2)}, u32[]{:S(2)}) collective-permute-start(bf16[144,576]{1,0:T(8,128)(2,1)S(1)} %get-tuple-element.137), channel_id=1, source_target_pairs={{0,128},{128,0},{1,129},{129,1},{2,130},{130,2},{3,131},{131,3},{4... | collective-permute-start | bytes 497672 | tf_op jit(solution)/shard_map/ppermute | solution.py:23
  116.9 17.4 %collective-permute-start.30 = (bf16[160,128]{1,0:T(8,128)(2,1)S(1)}, bf16[160,128]{1,0:T(8,128)(2,1)S(1)}, u32[]{:S(2)}, u32[]{:S(2)}) collective-permute-start(bf16[160,128]{1,0:T(8,128)(2,1)S(1)} %pad_maximum_fusion.11), channel_id=1, source_target_pairs={{0,128},{128,0},{1,129},{129,1},{2,130},{130,2},{3,131},{131,3},{4... | collective-permute-start | bytes 122888 | tf_op jit(solution)/shard_map/ppermute | solution.py:23
  123.7 24.3 %collective-permute-start.38 = (bf16[2,144,576]{2,1,0:T(8,128)(2,1)S(1)}, bf16[2,144,576]{2,1,0:T(8,128)(2,1)S(1)}, u32[]{:S(2)}, u32[]{:S(2)}) collective-permute-start(bf16[2,144,576]{2,1,0:T(8,128)(2,1)S(1)} %pad_maximum_fusion.6), channel_id=1, source_target_pairs={{0,16},{16,0},{1,17},{17,1},{2,18},{18,2},{3,19},{19,3},{4,20},{20... | collective-permute-start | bytes 995336 | tf_op jit(solution)/shard_map/ppermute | solution.py:23
  137.7 7.7 %collective-permute-start.32 = (f32[144]{0:T(256)S(1)}, f32[144]{0:T(256)S(1)}, u32[]{:S(2)}, u32[]{:S(2)}) collective-permute-start(f32[144]{0:T(256)S(1)} %add.232), channel_id=1, source_target_pairs={{0,32},{32,64},{64,96},{96,0},{1,33},{33,65},{65,97},{97,1},{2,34}... | collective-permute-start | bytes 1736 | tf_op jit(solution)/shard_map/ppermute | solution.py:23
  (12 other events, 78.9 us)

commit v5 on v4

--- a/solution.py
+++ b/solution.py
@@ -27,6 +27,10 @@
     return turned(array, axis, 1)
 
 
+def crossed(array):
+    return lax.ppermute(array, ("zh", "core"), [(i, 3 - i) for i in range(4)])
+
+
 def unsigned(index):
     return index.astype(jnp.uint32)
 
@@ -55,7 +59,7 @@
     zh, core = lax.axis_index("zh"), lax.axis_index("core")
     rows = gate_ref.shape[0]
     if aways:
-        weights, backs = outs[:2], [outs[2].at[0], outs[2].at[1]]
+        weights, backs = outs[:2], outs[2:]
     else:
         weights = [out.at[pl.ds(0, rows)] for out in outs]
         backs = [out.at[pl.ds(rows, half)] for out in outs]
@@ -83,7 +87,7 @@
     main, rest = parts_of(width)
     half = hidden_grad.shape[0] // 2
     if aways:
-        outs = [(rows, width // 2), (rows, width // 2), (2, half, width // 2)]
+        outs = [(rows, width // 2), (rows, width // 2), *[(half, width // 2)] * 2]
     else:
         outs = [(rows + half, width // 2)] * 2
     return pl.pallas_call(
@@ -196,7 +200,7 @@
 
     near_own, near_other = packed(0, w_gate, w_up, hidden_grad)
     hidden_grad, near_own = barrier((hidden_grad, near_own))
-    away_own, away_other, backs = packed(1, w_gate, w_up, hidden_grad)
+    away_own, away_other, back_same, back_cross = packed(1, w_gate, w_up, hidden_grad)
     near_other = swapped(near_other, "core")
     away_other, far_t = barrier((away_other, far_t))
     away_own, away_other = swapped(away_own, "zh"), swapped(away_other, "zh")
@@ -209,11 +213,11 @@
     both, near_got[0], near_got[1] = barrier((both, near_got[0], near_got[1]))
     section_got = [turned(both, "sec", by) for by in steps]
 
-    near_got[0], near_got[1], backs, late_first = barrier(
-        (near_got[0], near_got[1], backs, first_core)
+    near_got[0], near_got[1], back_same, back_cross, late_first = barrier(
+        (near_got[0], near_got[1], back_same, back_cross, first_core)
     )
     away_other = swapped(away_other, "core")
-    backs = swapped(backs, "zh")
+    back_same, back_cross = swapped(back_same, "zh"), crossed(back_cross)
     away = ordered(away_own, away_other, late_first)
     late = {}
     away, late[0], late[1], late[2], late[3] = barrier((away, *(sec_to[by] for by in range(4))))
@@ -230,7 +234,7 @@
     normed_other, away_got[2] = barrier((swapped(normed, "core"), away_got[2]))
     normed = jnp.concatenate([normed, normed_other], axis=1)
 
-    backs, *away_got = barrier((backs, *away_got))
+    back_same, back_cross, *away_got = barrier((back_same, back_cross, *away_got))
     full = jnp.zeros((2, 4, 2, rows, width // 2), BF16)
     for pieces, place in (((near, *near_got), zh), ((away, *away_got), far_zh)):
         for by, piece in zip((0, 3, 1, 2), pieces):
@@ -239,7 +243,7 @@
     back = jnp.concatenate(
         [
             half
-            for block in (near_own[rows:], backs[0], near_other[rows:], swapped(backs[1], "core"))
+            for block in (near_own[rows:], back_same, near_other[rows:], back_cross)
             for half in split_pair(block)
         ],
         axis=0,
@@ -311,9 +315,10 @@
     got = swapped(send, "zh")
     g_near = part(late_zh, x) + sum(g.astype(F32) for g in near_got)
     g_near = g_near.astype(BF16).reshape(2, rows, -1)
-    give = swapped(jnp.stack([as_block(g_near, other_core), away_give]), "core")
     grad_gain = gain_part + jnp.concatenate([row_of(got, 1), row_of(got, 2)])[:own_rows]
     grad_gain = grad_gain + swapped(grad_gain, "core")
+    late_core, grad_gain = barrier((other_core, grad_gain))
+    give = swapped(jnp.stack([as_block(g_near, late_core), away_give]), "core")
     grad_gain = grad_gain + sum(turned(grad_gain, "x", by) for by in steps)
     d_own, row_sum = total[:, :group] + block_of(got), row[:group] + row_of(got)
     inv = inv_rms[:group]

time: 152 us -> 152 us (level); the launches traced: 152 us -> 150 us
  starting transfers between devices: 82.8 us -> 69.3 us
  waiting for transfers between devices: 47.5 us -> 59.2 us
    ppermute x39 -> x38, starting transfers between devices: 82.8 us -> 67.1 us  [turned(): return lax.ppermute(array, axis, [(i, (i + by) % n) for i in range(n)])]
    ppermute x39 -> x38, waiting for transfers between devices: 47.5 us -> 53.6 us  [turned(): return lax.ppermute(array, axis, [(i, (i + by) % n) for i in range(n)])]
    ppermute x0 -> x1, waiting for transfers between devices: none -> 5.65 us  [crossed(): return lax.ppermute(array, ('zh', 'core'), [(i, 3 - i) for i in range(4)])]
    ppermute x0 -> x1, starting transfers between devices: none -> 2.15 us  [crossed(): return lax.ppermute(array, ('zh', 'core'), [(i, 3 - i) for i in range(4)])]
where the time goes in v5:
time: 152 us; the launch traced here: 150 us
  starting transfers between devices  69.3 us (46%)
  waiting for transfers between devices  59.2 us (39%)
  matrix products  7.46 us (5%)
  Pallas kernels  4.93 us (3%)
  other arithmetic  4.32 us (3%)
  local copies, waits for them, and re-layouts  3.25 us (2%)
    ppermute x38, starting transfers between devices, turned(): return lax.ppermute(array, axis, [(i, (i + by) % n) for i in range(n)])  67.1 us
    ppermute x38, waiting for transfers between devices, turned(): return lax.ppermute(array, axis, [(i, (i + by) % n) for i in range(n)])  53.6 us
    ppermute x1, waiting for transfers between devices, crossed(): return lax.ppermute(array, ('zh', 'core'), [(i, 3 - i) for i in range(4)])  5.65 us
    dot_general x8, matrix products, part(): jnp.dot(as_block(by_rows, zplace, xplace), d_both, preferred_element_type...  3.15 us
  transfers between devices with their start and end apart: 39, of which 15 were waited for; matrix products, arithmetic and copies ran while one was open for 5% of the time, Pallas kernels for 1%

profile of v5, /device:TPU:1, one launch (start us, length us, event | category | flops | bytes accessed | tf_op | source)
XLA Modules:
  0.0 149.8 jit_solution(7004020667293142055)
XLA Ops:
  2.0 3.3 %collective-permute-start = (bf16[208,576]{1,0:T(8,128)(2,1)S(1)}, bf16[208,576]{1,0:T(8,128)(2,1)S(1)}, u32[]{:S(2)}, u32[]{:S(2)}) collective-permute-start(bf16[208,576]{1,0:T(8,128)(2,1)S(1)} %get-tuple-element.68), channel_id=1, source_target_pairs={{0,16},{16,0},{1,17},{17,1},{2,18},{18,2},{3,19},{19,3},{4,20},{20... | collective-permute-start | bytes 718856 | tf_op jit(solution)/shard_map/ppermute | solution.py:23
  5.3 5.2 %collective-permute-start.1 = (bf16[576,128]{1,0:T(8,128)(2,1)}, bf16[576,128]{1,0:T(8,128)(2,1)S(1)}, u32[]{:S(2)}, u32[]{:S(2)}) collective-permute-start(bf16[576,128]{1,0:T(8,128)(2,1)} %bitcast.138), channel_id=1, source_target_pairs={{0,128},{128,0},{1,129},{129,1},{2,130},{130,2},{3,131},{131,3},{4... | collective-permute-start | bytes 442376 | tf_op jit(solution)/shard_map/ppermute | solution.py:23
  12.5 2.4 %collective-permute-done.1 = bf16[576,128]{1,0:T(8,128)(2,1)S(1)} collective-permute-done((bf16[576,128]{1,0:T(8,128)(2,1)}, bf16[576,128]{1,0:T(8,128)(2,1)S(1)}, u32[]{:S(2)}, u32[]{:S(2)}) %collective-permute-start.1) | collective-permute-done | bytes 147488 | tf_op jit(solution)/shard_map/ppermute | solution.py:23
  14.9 5.2 %collective-permute-start.5 = (bf16[144,576]{1,0:T(8,128)(2,1)S(1)}, bf16[144,576]{1,0:T(8,128)(2,1)S(1)}, u32[]{:S(2)}, u32[]{:S(2)}) collective-permute-start(bf16[144,576]{1,0:T(8,128)(2,1)S(1)} %get-tuple-element.81), channel_id=1, source_target_pairs={{0,128},{128,0},{1,129},{129,1},{2,130},{130,2},{3,131},{131,3},{4... | collective-permute-start | bytes 497672 | tf_op jit(solution)/shard_map/ppermute | solution.py:23
  21.5 1.5 %collective-permute-start.3 = (bf16[2,144,576]{2,1,0:T(8,128)(2,1)S(1)}, bf16[2,144,576]{2,1,0:T(8,128)(2,1)S(1)}, u32[]{:S(2)}, u32[]{:S(2)}) collective-permute-start(bf16[2,144,576]{2,1,0:T(8,128)(2,1)S(1)} %maximum_select_fusion), channel_id=1, source_target_pairs={{0,96},{32,0},{64,32},{96,64},{1,97},{33,1},{65,33},{97,65},{2,98}... | collective-permute-start | bytes 995336 | tf_op jit(solution)/shard_map/ppermute | solution.py:23
  24.8 10.1 %collective-permute-done.5 = bf16[144,576]{1,0:T(8,128)(2,1)S(1)} collective-permute-done((bf16[144,576]{1,0:T(8,128)(2,1)S(1)}, bf16[144,576]{1,0:T(8,128)(2,1)S(1)}, u32[]{:S(2)}, u32[]{:S(2)}) %collective-permute-start.5) | collective-permute-done | bytes 165920 | tf_op jit(solution)/shard_map/ppermute | solution.py:23
  37.6 1.5 %collective-permute-start.8 = (bf16[576,256]{1,0:T(8,128)(2,1)S(1)}, bf16[576,256]{1,0:T(8,128)(2,1)S(1)}, u32[]{:S(2)}, u32[]{:S(2)}) collective-permute-start(bf16[576,256]{1,0:T(8,128)(2,1)S(1)} %pad_maximum_fusion.7), channel_id=1, source_target_pairs={{0,3},{1,0},{2,1},{3,2},{4,7},{5,4},{6,5},{7,6},{8,11},{9,8},{10,9... | collective-permute-start | bytes 884744 | tf_op jit(solution)/shard_map/ppermute | solution.py:23
  39.1 1.6 %collective-permute-start.9 = (bf16[576,256]{1,0:T(8,128)(2,1)S(1)}, bf16[576,256]{1,0:T(8,128)(2,1)S(1)}, u32[]{:S(2)}, u32[]{:S(2)}) collective-permute-start(bf16[576,256]{1,0:T(8,128)(2,1)S(1)} %pad_maximum_fusion.7), channel_id=1, source_target_pairs={{0,2},{1,3},{2,0},{3,1},{4,6},{5,7},{6,4},{7,5},{8,10},{9,11},{10,... | collective-permute-start | bytes 884744 | tf_op jit(solution)/shard_map/ppermute | solution.py:23
  43.2 5.8 %collective-permute-start.16 = (bf16[2,144,576]{2,1,0:T(8,128)(2,1)S(1)}, bf16[2,144,576]{2,1,0:T(8,128)(2,1)S(1)}, u32[]{:S(2)}, u32[]{:S(2)}) collective-permute-start(bf16[2,144,576]{2,1,0:T(8,128)(2,1)S(1)} %maximum_select_fusion.1), channel_id=1, source_target_pairs={{0,64},{32,96},{64,0},{96,32},{1,65},{33,97},{65,1},{97,33},{2,66}... | collective-permute-start | bytes 995336 | tf_op jit(solution)/shard_map/ppermute | solution.py:23
  49.2 3.2 %collective-permute-done.9 = bf16[576,256]{1,0:T(8,128)(2,1)S(1)} collective-permute-done((bf16[576,256]{1,0:T(8,128)(2,1)S(1)}, bf16[576,256]{1,0:T(8,128)(2,1)S(1)}, u32[]{:S(2)}, u32[]{:S(2)}) %collective-permute-start.9) | collective-permute-done | bytes 294944 | tf_op jit(solution)/shard_map/ppermute | solution.py:23
  52.4 4.5 %collective-permute-start.11 = (bf16[64,576]{1,0:T(8,128)(2,1)S(1)}, bf16[64,576]{1,0:T(8,128)(2,1)S(1)}, u32[]{:S(2)}, u32[]{:S(2)}) collective-permute-start(bf16[64,576]{1,0:T(8,128)(2,1)S(1)} %get-tuple-element.90), channel_id=1, source_target_pairs={{0,128},{128,0},{1,129},{129,1},{2,130},{130,2},{3,131},{131,3},{4... | collective-permute-start | bytes 221192 | tf_op jit(solution)/shard_map/ppermute | solution.py:23
  57.7 2.4 %collective-permute-start.15 = (bf16[2304,256]{1,0:T(8,128)(2,1)S(1)}, bf16[2304,256]{1,0:T(8,128)(2,1)S(1)}, u32[]{:S(2)}, u32[]{:S(2)}) collective-permute-start(bf16[2304,256]{1,0:T(8,128)(2,1)S(1)} %multiply_convert_fusion), channel_id=1, source_target_pairs={{0,16},{16,0},{1,17},{17,1},{2,18},{18,2},{3,19},{19,3},{4,20},{20... | collective-permute-start | bytes 3538952 | tf_op jit(solution)/shard_map/ppermute | solution.py:23
  60.2 2.2 %collective-permute-start.12 = (bf16[64,576]{1,0:T(8,128)(2,1)S(1)}, bf16[64,576]{1,0:T(8,128)(2,1)S(1)}, u32[]{:S(2)}, u32[]{:S(2)}) collective-permute-start(bf16[64,576]{1,0:T(8,128)(2,1)S(1)} %get-tuple-element.91), channel_id=1, source_target_pairs={{0,144},{16,128},{128,16},{144,0},{1,145},{17,129},{129,17},{145,1... | collective-permute-start | bytes 221192 | tf_op jit(solution)/shard_map/ppermute | solution.py:31
  62.6 5.7 %collective-permute-done.12 = bf16[64,576]{1,0:T(8,128)(2,1)S(1)} collective-permute-done((bf16[64,576]{1,0:T(8,128)(2,1)S(1)}, bf16[64,576]{1,0:T(8,128)(2,1)S(1)}, u32[]{:S(2)}, u32[]{:S(2)}) %collective-permute-start.12) | collective-permute-done | bytes 73760 | tf_op jit(solution)/shard_map/ppermute | solution.py:31
  68.6 2.1 %fusion.84 = f32[512,576]{1,0:T(8,128)S(1)} fusion(bf16[2304,512]{1,0:T(8,128)(2,1)S(1)} %constant_dynamic-update-slice_fusion, bf16[2304,576]{1,0:T(8,128)(2,1)S(1)} %bitcast.112), kind=kOutput, calls=%fused_computation.189 | convolution fusion | flops 1358954496 | bytes 6193152 | tf_op jit(solution)/shard_map/dot_general | solution.py:252
  79.2 7.3 %collective-permute-done.19 = bf16[288,576]{1,0:T(8,128)(2,1)S(1)} collective-permute-done((bf16[288,576]{1,0:T(8,128)(2,1)S(1)}, bf16[288,576]{1,0:T(8,128)(2,1)S(1)}, u32[]{:S(2)}, u32[]{:S(2)}) %collective-permute-start.19) | collective-permute-done | bytes 331808 | tf_op jit(solution)/shard_map/ppermute | solution.py:23
  86.4 2.3 %collective-permute-done.18 = bf16[288,576]{1,0:T(8,128)(2,1)S(1)} collective-permute-done((bf16[288,576]{1,0:T(8,128)(2,1)S(1)}, bf16[288,576]{1,0:T(8,128)(2,1)S(1)}, u32[]{:S(2)}, u32[]{:S(2)}) %collective-permute-start.18) | collective-permute-done | bytes 331808 | tf_op jit(solution)/shard_map/ppermute | solution.py:23
  89.6 1.8 %collective-permute-start.22 = (bf16[592,256]{1,0:T(8,128)(2,1)S(1)}, bf16[592,256]{1,0:T(8,128)(2,1)S(1)}, u32[]{:S(2)}, u32[]{:S(2)}) collective-permute-start(bf16[592,256]{1,0:T(8,128)(2,1)S(1)} %get-tuple-element.102), channel_id=1, source_target_pairs={{0,3},{1,0},{2,1},{3,2},{4,7},{5,4},{6,5},{7,6},{8,11},{9,8},{10,9... | collective-permute-start | bytes 909320 | tf_op jit(solution)/shard_map/ppermute | solution.py:23
  91.4 2.8 %collective-permute-start.23 = (bf16[592,256]{1,0:T(8,128)(2,1)S(1)}, bf16[592,256]{1,0:T(8,128)(2,1)S(1)}, u32[]{:S(2)}, u32[]{:S(2)}) collective-permute-start(bf16[592,256]{1,0:T(8,128)(2,1)S(1)} %get-tuple-element.103), channel_id=1, source_target_pairs={{0,2},{1,3},{2,0},{3,1},{4,6},{5,7},{6,4},{7,5},{8,10},{9,11},{10,... | collective-permute-start | bytes 909320 | tf_op jit(solution)/shard_map/ppermute | solution.py:23
  95.1 2.3 %collective-permute-done.21 = bf16[592,256]{1,0:T(8,128)(2,1)S(1)} collective-permute-done((bf16[592,256]{1,0:T(8,128)(2,1)S(1)}, bf16[592,256]{1,0:T(8,128)(2,1)S(1)}, u32[]{:S(2)}, u32[]{:S(2)}) %collective-permute-start.21) | collective-permute-done | bytes 303136 | tf_op jit(solution)/shard_map/ppermute | solution.py:23
  98.4 7.1 %collective-permute-done.23 = bf16[592,256]{1,0:T(8,128)(2,1)S(1)} collective-permute-done((bf16[592,256]{1,0:T(8,128)(2,1)S(1)}, bf16[592,256]{1,0:T(8,128)(2,1)S(1)}, u32[]{:S(2)}, u32[]{:S(2)}) %collective-permute-start.23) | collective-permute-done | bytes 303136 | tf_op jit(solution)/shard_map/ppermute | solution.py:23
  106.9 2.5 %collective-permute-start.26 = (bf16[160,256]{1,0:T(8,128)(2,1)S(1)}, bf16[160,256]{1,0:T(8,128)(2,1)S(1)}, u32[]{:S(2)}, u32[]{:S(2)}) collective-permute-start(bf16[160,256]{1,0:T(8,128)(2,1)S(1)} %get-tuple-element.167), channel_id=1, source_target_pairs={{0,12},{4,0},{8,4},{12,8},{1,13},{5,1},{9,5},{13,9},{2,14},{6,2},{... | collective-permute-start | bytes 245768 | tf_op jit(solution)/shard_map/ppermute | solution.py:23
  109.4 2.7 %collective-permute-start.29 = (bf16[288,576]{1,0:T(8,128)(2,1)S(1)}, bf16[288,576]{1,0:T(8,128)(2,1)S(1)}, u32[]{:S(2)}, u32[]{:S(2)}) collective-permute-start(bf16[288,576]{1,0:T(8,128)(2,1)S(1)} %convolution_convert_fusion.2), channel_id=1, source_target_pairs={{0,96},{32,0},{64,32},{96,64},{1,97},{33,1},{65,33},{97,65},{2,98}... | collective-permute-start | bytes 995336 | tf_op jit(solution)/shard_map/ppermute | solution.py:23
  112.2 3.4 %collective-permute-start.37 = (bf16[144,576]{1,0:T(8,128)(2,1)S(1)}, bf16[144,576]{1,0:T(8,128)(2,1)S(1)}, u32[]{:S(2)}, u32[]{:S(2)}) collective-permute-start(bf16[144,576]{1,0:T(8,128)(2,1)S(1)} %get-tuple-element.146), channel_id=1, source_target_pairs={{0,128},{128,0},{1,129},{129,1},{2,130},{130,2},{3,131},{131,3},{4... | collective-permute-start | bytes 497672 | tf_op jit(solution)/shard_map/ppermute | solution.py:23
  116.6 3.5 %collective-permute-start.36 = (bf16[144,576]{1,0:T(8,128)(2,1)S(1)}, bf16[144,576]{1,0:T(8,128)(2,1)S(1)}, u32[]{:S(2)}, u32[]{:S(2)}) collective-permute-start(bf16[144,576]{1,0:T(8,128)(2,1)S(1)} %get-tuple-element.147), channel_id=1, source_target_pairs={{0,128},{128,0},{1,129},{129,1},{2,130},{130,2},{3,131},{131,3},{4... | collective-permute-start | bytes 497672 | tf_op jit(solution)/shard_map/ppermute | solution.py:23
  120.4 2.0 %collective-permute-start.30 = (bf16[160,128]{1,0:T(8,128)(2,1)S(1)}, bf16[160,128]{1,0:T(8,128)(2,1)S(1)}, u32[]{:S(2)}, u32[]{:S(2)}) collective-permute-start(bf16[160,128]{1,0:T(8,128)(2,1)S(1)} %pad_maximum_fusion.11), channel_id=1, source_target_pairs={{0,128},{128,0},{1,129},{129,1},{2,130},{130,2},{3,131},{131,3},{4... | collective-permute-start | bytes 122888 | tf_op jit(solution)/shard_map/ppermute | solution.py:23
  122.4 2.2 %collective-permute-done.35 = bf16[288,576]{1,0:T(8,128)(2,1)S(1)} collective-permute-done((bf16[288,576]{1,0:T(8,128)(2,1)S(1)}, bf16[288,576]{1,0:T(8,128)(2,1)S(1)}, u32[]{:S(2)}, u32[]{:S(2)}) %collective-permute-start.35) | collective-permute-done | bytes 331808 | tf_op jit(solution)/shard_map/ppermute | solution.py:23
  125.1 11.2 %collective-permute-done.30 = bf16[160,128]{1,0:T(8,128)(2,1)S(1)} collective-permute-done((bf16[160,128]{1,0:T(8,128)(2,1)S(1)}, bf16[160,128]{1,0:T(8,128)(2,1)S(1)}, u32[]{:S(2)}, u32[]{:S(2)}) %collective-permute-start.30) | collective-permute-done | bytes 40992 | tf_op jit(solution)/shard_map/ppermute | solution.py:23
  136.3 1.8 %collective-permute-start.31 = (f32[144]{0:T(256)S(1)}, f32[144]{0:T(256)S(1)}, u32[]{:S(2)}, u32[]{:S(2)}) collective-permute-start(f32[144]{0:T(256)S(1)} %slice_add_fusion.1), channel_id=1, source_target_pairs={{0,16},{16,0},{1,17},{17,1},{2,18},{18,2},{3,19},{19,3},{4,20},{20... | collective-permute-start | bytes 1736 | tf_op jit(solution)/shard_map/ppermute | solution.py:23
  139.8 1.8 %collective-permute-start.33 = (f32[144]{0:T(256)S(1)}, f32[144]{0:T(256)S(1)}, u32[]{:S(2)}, u32[]{:S(2)}) collective-permute-start(f32[144]{0:T(256)S(1)} %add.232), channel_id=1, source_target_pairs={{0,96},{32,0},{64,32},{96,64},{1,97},{33,1},{65,33},{97,65},{2,98}... | collective-permute-start | bytes 1736 | tf_op jit(solution)/shard_map/ppermute | solution.py:23
  144.0 1.6 %collective-permute-done.34 = f32[144]{0:T(256)S(1)} collective-permute-done((f32[144]{0:T(256)S(1)}, f32[144]{0:T(256)S(1)}, u32[]{:S(2)}, u32[]{:S(2)}) %collective-permute-start.34) | collective-permute-done | bytes 608 | tf_op jit(solution)/shard_map/ppermute | solution.py:23
  147.6 2.2 %join.1 = (bf16[144,1152]{1,0:T(8,128)(2,1)}, bf16[144,1152]{1,0:T(8,128)(2,1)}) custom-call(bf16[2,144,576]{2,1,0:T(8,128)(2,1)} %bitcast.128, bf16[144,576]{1,0:T(8,128)(2,1)} %copy-done.2, bf16[2,144,576]{2,1,0:T(8,128)(2,1)} %copy-done.1), custom_call_target="tpu_custom_call" | custom-call | tf_op jit(solution)/shard_map/join/pallas_call | solution.py:126
  (154 shorter events, 33.2 us)
Async XLA Ops:
  2.0 18.1 %collective-permute-start = (bf16[208,576]{1,0:T(8,128)(2,1)S(1)}, bf16[208,576]{1,0:T(8,128)(2,1)S(1)}, u32[]{:S(2)}, u32[]{:S(2)}) collective-permute-start(bf16[208,576]{1,0:T(8,128)(2,1)S(1)} %get-tuple-element.68), channel_id=1, source_target_pairs={{0,16},{16,0},{1,17},{17,1},{2,18},{18,2},{3,19},{19,3},{4,20},{20... | collective-permute-start | bytes 718856 | tf_op jit(solution)/shard_map/ppermute | solution.py:23
  5.3 9.5 %collective-permute-start.1 = (bf16[576,128]{1,0:T(8,128)(2,1)}, bf16[576,128]{1,0:T(8,128)(2,1)S(1)}, u32[]{:S(2)}, u32[]{:S(2)}) collective-permute-start(bf16[576,128]{1,0:T(8,128)(2,1)} %bitcast.138), channel_id=1, source_target_pairs={{0,128},{128,0},{1,129},{129,1},{2,130},{130,2},{3,131},{131,3},{4... | collective-permute-start | bytes 442376 | tf_op jit(solution)/shard_map/ppermute | solution.py:23
  11.9 27.2 %collective-permute-start.4 = (bf16[144,576]{1,0:T(8,128)(2,1)S(1)}, bf16[144,576]{1,0:T(8,128)(2,1)S(1)}, u32[]{:S(2)}, u32[]{:S(2)}) collective-permute-start(bf16[144,576]{1,0:T(8,128)(2,1)S(1)} %get-tuple-element.80), channel_id=1, source_target_pairs={{0,128},{128,0},{1,129},{129,1},{2,130},{130,2},{3,131},{131,3},{4... | collective-permute-start | bytes 497672 | tf_op jit(solution)/shard_map/ppermute | solution.py:23
  14.9 20.0 %collective-permute-start.5 = (bf16[144,576]{1,0:T(8,128)(2,1)S(1)}, bf16[144,576]{1,0:T(8,128)(2,1)S(1)}, u32[]{:S(2)}, u32[]{:S(2)}) collective-permute-start(bf16[144,576]{1,0:T(8,128)(2,1)S(1)} %get-tuple-element.81), channel_id=1, source_target_pairs={{0,128},{128,0},{1,129},{129,1},{2,130},{130,2},{3,131},{131,3},{4... | collective-permute-start | bytes 497672 | tf_op jit(solution)/shard_map/ppermute | solution.py:23
  20.2 16.0 %collective-permute-start.2 = (bf16[2,144,576]{2,1,0:T(8,128)(2,1)S(1)}, bf16[2,144,576]{2,1,0:T(8,128)(2,1)S(1)}, u32[]{:S(2)}, u32[]{:S(2)}) collective-permute-start(bf16[2,144,576]{2,1,0:T(8,128)(2,1)S(1)} %maximum_select_fusion), channel_id=1, source_target_pairs={{0,32},{32,64},{64,96},{96,0},{1,33},{33,65},{65,97},{97,1},{2,34}... | collective-permute-start | bytes 995336 | tf_op jit(solution)/shard_map/ppermute | solution.py:23
  21.5 14.8 %collective-permute-start.3 = (bf16[2,144,576]{2,1,0:T(8,128)(2,1)S(1)}, bf16[2,144,576]{2,1,0:T(8,128)(2,1)S(1)}, u32[]{:S(2)}, u32[]{:S(2)}) collective-permute-start(bf16[2,144,576]{2,1,0:T(8,128)(2,1)S(1)} %maximum_select_fusion), channel_id=1, source_target_pairs={{0,96},{32,0},{64,32},{96,64},{1,97},{33,1},{65,33},{97,65},{2,98}... | collective-permute-start | bytes 995336 | tf_op jit(solution)/shard_map/ppermute | solution.py:23
  23.0 37.1 %collective-permute-start.10 = (bf16[2,144,576]{2,1,0:T(8,128)(2,1)S(1)}, bf16[2,144,576]{2,1,0:T(8,128)(2,1)S(1)}, u32[]{:S(2)}, u32[]{:S(2)}) collective-permute-start(bf16[2,144,576]{2,1,0:T(8,128)(2,1)S(1)} %maximum_select_fusion), channel_id=1, source_target_pairs={{0,64},{32,96},{64,0},{96,32},{1,65},{33,97},{65,1},{97,33},{2,66}... | collective-permute-start | bytes 995336 | tf_op jit(solution)/shard_map/ppermute | solution.py:23
  34.9 5.7 %collective-permute-start.6 = (bf16[144,576]{1,0:T(8,128)(2,1)S(1)}, bf16[144,576]{1,0:T(8,128)(2,1)S(1)}, u32[]{:S(2)}, u32[]{:S(2)}) collective-permute-start(bf16[144,576]{1,0:T(8,128)(2,1)S(1)} %collective-permute-done.5), channel_id=1, source_target_pairs={{0,16},{16,0},{1,17},{17,1},{2,18},{18,2},{3,19},{19,3},{4,20},{20... | collective-permute-start | bytes 497672 | tf_op jit(solution)/shard_map/ppermute | solution.py:23
  36.3 6.9 %collective-permute-start.7 = (bf16[576,256]{1,0:T(8,128)(2,1)S(1)}, bf16[576,256]{1,0:T(8,128)(2,1)S(1)}, u32[]{:S(2)}, u32[]{:S(2)}) collective-permute-start(bf16[576,256]{1,0:T(8,128)(2,1)S(1)} %pad_maximum_fusion.7), channel_id=1, source_target_pairs={{0,1},{1,2},{2,3},{3,0},{4,5},{5,6},{6,7},{7,4},{8,9},{9,10},{10,1... | collective-permute-start | bytes 884744 | tf_op jit(solution)/shard_map/ppermute | solution.py:23
  37.6 11.5 %collective-permute-start.8 = (bf16[576,256]{1,0:T(8,128)(2,1)S(1)}, bf16[576,256]{1,0:T(8,128)(2,1)S(1)}, u32[]{:S(2)}, u32[]{:S(2)}) collective-permute-start(bf16[576,256]{1,0:T(8,128)(2,1)S(1)} %pad_maximum_fusion.7), channel_id=1, source_target_pairs={{0,3},{1,0},{2,1},{3,2},{4,7},{5,4},{6,5},{7,6},{8,11},{9,8},{10,9... | collective-permute-start | bytes 884744 | tf_op jit(solution)/shard_map/ppermute | solution.py:23
  39.1 13.3 %collective-permute-start.9 = (bf16[576,256]{1,0:T(8,128)(2,1)S(1)}, bf16[576,256]{1,0:T(8,128)(2,1)S(1)}, u32[]{:S(2)}, u32[]{:S(2)}) collective-permute-start(bf16[576,256]{1,0:T(8,128)(2,1)S(1)} %pad_maximum_fusion.7), channel_id=1, source_target_pairs={{0,2},{1,3},{2,0},{3,1},{4,6},{5,7},{6,4},{7,5},{8,10},{9,11},{10,... | collective-permute-start | bytes 884744 | tf_op jit(solution)/shard_map/ppermute | solution.py:23
  40.7 16.9 %collective-permute-start.13 = (bf16[2,144,576]{2,1,0:T(8,128)(2,1)S(1)}, bf16[2,144,576]{2,1,0:T(8,128)(2,1)S(1)}, u32[]{:S(2)}, u32[]{:S(2)}) collective-permute-start(bf16[2,144,576]{2,1,0:T(8,128)(2,1)S(1)} %maximum_select_fusion.1), channel_id=1, source_target_pairs={{0,32},{32,64},{64,96},{96,0},{1,33},{33,65},{65,97},{97,1},{2,34}... | collective-permute-start | bytes 995336 | tf_op jit(solution)/shard_map/ppermute | solution.py:23
  43.2 19.4 %collective-permute-start.16 = (bf16[2,144,576]{2,1,0:T(8,128)(2,1)S(1)}, bf16[2,144,576]{2,1,0:T(8,128)(2,1)S(1)}, u32[]{:S(2)}, u32[]{:S(2)}) collective-permute-start(bf16[2,144,576]{2,1,0:T(8,128)(2,1)S(1)} %maximum_select_fusion.1), channel_id=1, source_target_pairs={{0,64},{32,96},{64,0},{96,32},{1,65},{33,97},{65,1},{97,33},{2,66}... | collective-permute-start | bytes 995336 | tf_op jit(solution)/shard_map/ppermute | solution.py:23
  49.0 19.2 %collective-permute-start.14 = (bf16[2,144,576]{2,1,0:T(8,128)(2,1)S(1)}, bf16[2,144,576]{2,1,0:T(8,128)(2,1)S(1)}, u32[]{:S(2)}, u32[]{:S(2)}) collective-permute-start(bf16[2,144,576]{2,1,0:T(8,128)(2,1)S(1)} %maximum_select_fusion.1), channel_id=1, source_target_pairs={{0,96},{32,0},{64,32},{96,64},{1,97},{33,1},{65,33},{97,65},{2,98}... | collective-permute-start | bytes 995336 | tf_op jit(solution)/shard_map/ppermute | solution.py:23
  52.4 10.2 %collective-permute-start.11 = (bf16[64,576]{1,0:T(8,128)(2,1)S(1)}, bf16[64,576]{1,0:T(8,128)(2,1)S(1)}, u32[]{:S(2)}, u32[]{:S(2)}) collective-permute-start(bf16[64,576]{1,0:T(8,128)(2,1)S(1)} %get-tuple-element.90), channel_id=1, source_target_pairs={{0,128},{128,0},{1,129},{129,1},{2,130},{130,2},{3,131},{131,3},{4... | collective-permute-start | bytes 221192 | tf_op jit(solution)/shard_map/ppermute | solution.py:23
  60.2 8.1 %collective-permute-start.12 = (bf16[64,576]{1,0:T(8,128)(2,1)S(1)}, bf16[64,576]{1,0:T(8,128)(2,1)S(1)}, u32[]{:S(2)}, u32[]{:S(2)}) collective-permute-start(bf16[64,576]{1,0:T(8,128)(2,1)S(1)} %get-tuple-element.91), channel_id=1, source_target_pairs={{0,144},{16,128},{128,16},{144,0},{1,145},{17,129},{129,17},{145,1... | collective-permute-start | bytes 221192 | tf_op jit(solution)/shard_map/ppermute | solution.py:31
  76.2 10.2 %collective-permute-start.19 = (bf16[288,576]{1,0:T(8,128)(2,1)S(1)}, bf16[288,576]{1,0:T(8,128)(2,1)S(1)}, u32[]{:S(2)}, u32[]{:S(2)}) collective-permute-start(bf16[288,576]{1,0:T(8,128)(2,1)S(1)} %convolution_convert_fusion.5), channel_id=1, source_target_pairs={{0,96},{32,0},{64,32},{96,64},{1,97},{33,1},{65,33},{97,65},{2,98}... | collective-permute-start | bytes 995336 | tf_op jit(solution)/shard_map/ppermute | solution.py:23
  77.7 11.0 %collective-permute-start.18 = (bf16[288,576]{1,0:T(8,128)(2,1)S(1)}, bf16[288,576]{1,0:T(8,128)(2,1)S(1)}, u32[]{:S(2)}, u32[]{:S(2)}) collective-permute-start(bf16[288,576]{1,0:T(8,128)(2,1)S(1)} %convolution_convert_fusion.6), channel_id=1, source_target_pairs={{0,32},{32,64},{64,96},{96,0},{1,33},{33,65},{65,97},{97,1},{2,34}... | collective-permute-start | bytes 995336 | tf_op jit(solution)/shard_map/ppermute | solution.py:23
  88.7 8.7 %collective-permute-start.21 = (bf16[592,256]{1,0:T(8,128)(2,1)S(1)}, bf16[592,256]{1,0:T(8,128)(2,1)S(1)}, u32[]{:S(2)}, u32[]{:S(2)}) collective-permute-start(bf16[592,256]{1,0:T(8,128)(2,1)S(1)} %get-tuple-element.101), channel_id=1, source_target_pairs={{0,1},{1,2},{2,3},{3,0},{4,5},{5,6},{6,7},{7,4},{8,9},{9,10},{10,1... | collective-permute-start | bytes 909320 | tf_op jit(solution)/shard_map/ppermute | solution.py:23
  89.6 8.9 %collective-permute-start.22 = (bf16[592,256]{1,0:T(8,128)(2,1)S(1)}, bf16[592,256]{1,0:T(8,128)(2,1)S(1)}, u32[]{:S(2)}, u32[]{:S(2)}) collective-permute-start(bf16[592,256]{1,0:T(8,128)(2,1)S(1)} %get-tuple-element.102), channel_id=1, source_target_pairs={{0,3},{1,0},{2,1},{3,2},{4,7},{5,4},{6,5},{7,6},{8,11},{9,8},{10,9... | collective-permute-start | bytes 909320 | tf_op jit(solution)/shard_map/ppermute | solution.py:23
  91.4 14.2 %collective-permute-start.23 = (bf16[592,256]{1,0:T(8,128)(2,1)S(1)}, bf16[592,256]{1,0:T(8,128)(2,1)S(1)}, u32[]{:S(2)}, u32[]{:S(2)}) collective-permute-start(bf16[592,256]{1,0:T(8,128)(2,1)S(1)} %get-tuple-element.103), channel_id=1, source_target_pairs={{0,2},{1,3},{2,0},{3,1},{4,6},{5,7},{6,4},{7,5},{8,10},{9,11},{10,... | collective-permute-start | bytes 909320 | tf_op jit(solution)/shard_map/ppermute | solution.py:23
  94.6 11.1 %collective-permute-start.24 = (bf16[288,576]{1,0:T(8,128)(2,1)S(1)}, bf16[288,576]{1,0:T(8,128)(2,1)S(1)}, u32[]{:S(2)}, u32[]{:S(2)}) collective-permute-start(bf16[288,576]{1,0:T(8,128)(2,1)S(1)} %convolution_convert_fusion.4), channel_id=1, source_target_pairs={{0,64},{32,96},{64,0},{96,32},{1,65},{33,97},{65,1},{97,33},{2,66}... | collective-permute-start | bytes 995336 | tf_op jit(solution)/shard_map/ppermute | solution.py:23
  106.1 6.1 %collective-permute-start.25 = (bf16[160,256]{1,0:T(8,128)(2,1)S(1)}, bf16[160,256]{1,0:T(8,128)(2,1)S(1)}, u32[]{:S(2)}, u32[]{:S(2)}) collective-permute-start(bf16[160,256]{1,0:T(8,128)(2,1)S(1)} %get-tuple-element.166), channel_id=1, source_target_pairs={{0,4},{4,8},{8,12},{12,0},{1,5},{5,9},{9,13},{13,1},{2,6},{6,10},{... | collective-permute-start | bytes 245768 | tf_op jit(solution)/shard_map/ppermute | solution.py:23
  106.9 5.3 %collective-permute-start.26 = (bf16[160,256]{1,0:T(8,128)(2,1)S(1)}, bf16[160,256]{1,0:T(8,128)(2,1)S(1)}, u32[]{:S(2)}, u32[]{:S(2)}) collective-permute-start(bf16[160,256]{1,0:T(8,128)(2,1)S(1)} %get-tuple-element.167), channel_id=1, source_target_pairs={{0,12},{4,0},{8,4},{12,8},{1,13},{5,1},{9,5},{13,9},{2,14},{6,2},{... | collective-permute-start | bytes 245768 | tf_op jit(solution)/shard_map/ppermute | solution.py:23
  109.4 7.2 %collective-permute-start.27 = (bf16[160,256]{1,0:T(8,128)(2,1)S(1)}, bf16[160,256]{1,0:T(8,128)(2,1)S(1)}, u32[]{:S(2)}, u32[]{:S(2)}) collective-permute-start(bf16[160,256]{1,0:T(8,128)(2,1)S(1)} %get-tuple-element.168), channel_id=1, source_target_pairs={{0,8},{4,12},{8,0},{12,4},{1,9},{5,13},{9,1},{13,5},{2,10},{6,14},... | collective-permute-start | bytes 245768 | tf_op jit(solution)/shard_map/ppermute | solution.py:23
  109.4 11.0 %collective-permute-start.28 = (bf16[288,576]{1,0:T(8,128)(2,1)S(1)}, bf16[288,576]{1,0:T(8,128)(2,1)S(1)}, u32[]{:S(2)}, u32[]{:S(2)}) collective-permute-start(bf16[288,576]{1,0:T(8,128)(2,1)S(1)} %convolution_convert_fusion.3), channel_id=1, source_target_pairs={{0,32},{32,64},{64,96},{96,0},{1,33},{33,65},{65,97},{97,1},{2,34}... | collective-permute-start | bytes 995336 | tf_op jit(solution)/shard_map/ppermute | solution.py:23
  109.4 11.0 %collective-permute-start.29 = (bf16[288,576]{1,0:T(8,128)(2,1)S(1)}, bf16[288,576]{1,0:T(8,128)(2,1)S(1)}, u32[]{:S(2)}, u32[]{:S(2)}) collective-permute-start(bf16[288,576]{1,0:T(8,128)(2,1)S(1)} %convolution_convert_fusion.2), channel_id=1, source_target_pairs={{0,96},{32,0},{64,32},{96,64},{1,97},{33,1},{65,33},{97,65},{2,98}... | collective-permute-start | bytes 995336 | tf_op jit(solution)/shard_map/ppermute | solution.py:23
  112.1 12.5 %collective-permute-start.35 = (bf16[288,576]{1,0:T(8,128)(2,1)S(1)}, bf16[288,576]{1,0:T(8,128)(2,1)S(1)}, u32[]{:S(2)}, u32[]{:S(2)}) collective-permute-start(bf16[288,576]{1,0:T(8,128)(2,1)S(1)} %convolution_convert_fusion.1), channel_id=1, source_target_pairs={{0,64},{32,96},{64,0},{96,32},{1,65},{33,97},{65,1},{97,33},{2,66}... | collective-permute-start | bytes 995336 | tf_op jit(solution)/shard_map/ppermute | solution.py:23
  112.2 30.0 %collective-permute-start.37 = (bf16[144,576]{1,0:T(8,128)(2,1)S(1)}, bf16[144,576]{1,0:T(8,128)(2,1)S(1)}, u32[]{:S(2)}, u32[]{:S(2)}) collective-permute-start(bf16[144,576]{1,0:T(8,128)(2,1)S(1)} %get-tuple-element.146), channel_id=1, source_target_pairs={{0,128},{128,0},{1,129},{129,1},{2,130},{130,2},{3,131},{131,3},{4... | collective-permute-start | bytes 497672 | tf_op jit(solution)/shard_map/ppermute | solution.py:23
  116.6 29.5 %collective-permute-start.36 = (bf16[144,576]{1,0:T(8,128)(2,1)S(1)}, bf16[144,576]{1,0:T(8,128)(2,1)S(1)}, u32[]{:S(2)}, u32[]{:S(2)}) collective-permute-start(bf16[144,576]{1,0:T(8,128)(2,1)S(1)} %get-tuple-element.147), channel_id=1, source_target_pairs={{0,128},{128,0},{1,129},{129,1},{2,130},{130,2},{3,131},{131,3},{4... | collective-permute-start | bytes 497672 | tf_op jit(solution)/shard_map/ppermute | solution.py:23
  120.4 15.8 %collective-permute-start.30 = (bf16[160,128]{1,0:T(8,128)(2,1)S(1)}, bf16[160,128]{1,0:T(8,128)(2,1)S(1)}, u32[]{:S(2)}, u32[]{:S(2)}) collective-permute-start(bf16[160,128]{1,0:T(8,128)(2,1)S(1)} %pad_maximum_fusion.11), channel_id=1, source_target_pairs={{0,128},{128,0},{1,129},{129,1},{2,130},{130,2},{3,131},{131,3},{4... | collective-permute-start | bytes 122888 | tf_op jit(solution)/shard_map/ppermute | solution.py:23
  139.0 5.0 %collective-permute-start.32 = (f32[144]{0:T(256)S(1)}, f32[144]{0:T(256)S(1)}, u32[]{:S(2)}, u32[]{:S(2)}) collective-permute-start(f32[144]{0:T(256)S(1)} %add.232), channel_id=1, source_target_pairs={{0,32},{32,64},{64,96},{96,0},{1,33},{33,65},{65,97},{97,1},{2,34}... | collective-permute-start | bytes 1736 | tf_op jit(solution)/shard_map/ppermute | solution.py:23
  (12 other events, 76.5 us)

commit v6 on v4

--- a/solution.py
+++ b/solution.py
@@ -230,7 +230,8 @@
     normed_other, away_got[2] = barrier((swapped(normed, "core"), away_got[2]))
     normed = jnp.concatenate([normed, normed_other], axis=1)
 
-    backs, *away_got = barrier((backs, *away_got))
+    backs, away_got[0], away_got[2] = barrier((backs, away_got[0], away_got[2]))
+    back_other, away_got[1] = barrier((swapped(backs[1], "core"), away_got[1]))
     full = jnp.zeros((2, 4, 2, rows, width // 2), BF16)
     for pieces, place in (((near, *near_got), zh), ((away, *away_got), far_zh)):
         for by, piece in zip((0, 3, 1, 2), pieces):
@@ -239,7 +240,7 @@
     back = jnp.concatenate(
         [
             half
-            for block in (near_own[rows:], backs[0], near_other[rows:], swapped(backs[1], "core"))
+            for block in (near_own[rows:], backs[0], near_other[rows:], back_other)
             for half in split_pair(block)
         ],
         axis=0,

time: 152 us -> 155 us (1.020)
  starting transfers between devices: 82.8 us -> 85 us
    ppermute x39, starting transfers between devices: 82.8 us -> 85 us  [turned(): return lax.ppermute(array, axis, [(i, (i + by) % n) for i in range(n)])]
  transfers between devices with their start and end apart: 39 -> 39, of which waited for: 15 -> 16; matrix products, arithmetic and copies ran while one was open for 5% -> 5% of each run, Pallas kernels for 1% -> 1%
where the time goes in v6:
time: 155 us
  starting transfers between devices  85 us (55%)
  waiting for transfers between devices  48.8 us (31%)
  matrix products  7.46 us (5%)
  Pallas kernels  4.93 us (3%)
  other arithmetic  4.32 us (3%)
  local copies, waits for them, and re-layouts  3.36 us (2%)
    ppermute x39, starting transfers between devices, turned(): return lax.ppermute(array, axis, [(i, (i + by) % n) for i in range(n)])  85 us
    ppermute x39, waiting for transfers between devices, turned(): return lax.ppermute(array, axis, [(i, (i + by) % n) for i in range(n)])  48.8 us
    dot_general x8, matrix products, part(): jnp.dot(as_block(by_rows, zplace, xplace), d_both, preferred_element_type...  3.15 us
  transfers between devices with their start and end apart: 39, of which 16 were waited for; matrix products, arithmetic and copies ran while one was open for 5% of the time, Pallas kernels for 1%

profile of v6, /device:TPU:1, one launch (start us, length us, event | category | flops | bytes accessed | tf_op | source)
XLA Modules:
  0.0 155.2 jit_solution(17402951649538772374)
XLA Ops:
  2.0 3.3 %collective-permute-start = (bf16[208,576]{1,0:T(8,128)(2,1)S(1)}, bf16[208,576]{1,0:T(8,128)(2,1)S(1)}, u32[]{:S(2)}, u32[]{:S(2)}) collective-permute-start(bf16[208,576]{1,0:T(8,128)(2,1)S(1)} %get-tuple-element.64), channel_id=1, source_target_pairs={{0,16},{16,0},{1,17},{17,1},{2,18},{18,2},{3,19},{19,3},{4,20},{20... | collective-permute-start | bytes 718856 | tf_op jit(solution)/shard_map/ppermute | solution.py:23
  5.3 5.2 %collective-permute-start.1 = (bf16[576,128]{1,0:T(8,128)(2,1)}, bf16[576,128]{1,0:T(8,128)(2,1)S(1)}, u32[]{:S(2)}, u32[]{:S(2)}) collective-permute-start(bf16[576,128]{1,0:T(8,128)(2,1)} %bitcast.142), channel_id=1, source_target_pairs={{0,128},{128,0},{1,129},{129,1},{2,130},{130,2},{3,131},{131,3},{4... | collective-permute-start | bytes 442376 | tf_op jit(solution)/shard_map/ppermute | solution.py:23
  12.5 2.4 %collective-permute-done.1 = bf16[576,128]{1,0:T(8,128)(2,1)S(1)} collective-permute-done((bf16[576,128]{1,0:T(8,128)(2,1)}, bf16[576,128]{1,0:T(8,128)(2,1)S(1)}, u32[]{:S(2)}, u32[]{:S(2)}) %collective-permute-start.1) | collective-permute-done | bytes 147488 | tf_op jit(solution)/shard_map/ppermute | solution.py:23
  14.9 5.2 %collective-permute-start.5 = (bf16[144,576]{1,0:T(8,128)(2,1)S(1)}, bf16[144,576]{1,0:T(8,128)(2,1)S(1)}, u32[]{:S(2)}, u32[]{:S(2)}) collective-permute-start(bf16[144,576]{1,0:T(8,128)(2,1)S(1)} %get-tuple-element.76), channel_id=1, source_target_pairs={{0,128},{128,0},{1,129},{129,1},{2,130},{130,2},{3,131},{131,3},{4... | collective-permute-start | bytes 497672 | tf_op jit(solution)/shard_map/ppermute | solution.py:23
  21.5 1.5 collective-permute-start.3
  24.8 10.1 %collective-permute-done.5 = bf16[144,576]{1,0:T(8,128)(2,1)S(1)} collective-permute-done((bf16[144,576]{1,0:T(8,128)(2,1)S(1)}, bf16[144,576]{1,0:T(8,128)(2,1)S(1)}, u32[]{:S(2)}, u32[]{:S(2)}) %collective-permute-start.5) | collective-permute-done | bytes 165920 | tf_op jit(solution)/shard_map/ppermute | solution.py:23
  37.6 1.5 collective-permute-start.8
  39.1 1.6 %collective-permute-start.9 = (bf16[576,256]{1,0:T(8,128)(2,1)S(1)}, bf16[576,256]{1,0:T(8,128)(2,1)S(1)}, u32[]{:S(2)}, u32[]{:S(2)}) collective-permute-start(bf16[576,256]{1,0:T(8,128)(2,1)S(1)} %pad_maximum_fusion.7), channel_id=1, source_target_pairs={{0,2},{1,3},{2,0},{3,1},{4,6},{5,7},{6,4},{7,5},{8,10},{9,11},{10,... | collective-permute-start | bytes 884744 | tf_op jit(solution)/shard_map/ppermute | solution.py:23
  43.2 5.8 %collective-permute-start.14 = (bf16[2,144,576]{2,1,0:T(8,128)(2,1)S(1)}, bf16[2,144,576]{2,1,0:T(8,128)(2,1)S(1)}, u32[]{:S(2)}, u32[]{:S(2)}) collective-permute-start(bf16[2,144,576]{2,1,0:T(8,128)(2,1)S(1)} %maximum_select_fusion.1), channel_id=1, source_target_pairs={{0,64},{32,96},{64,0},{96,32},{1,65},{33,97},{65,1},{97,33},{2,66}... | collective-permute-start | bytes 995336 | tf_op jit(solution)/shard_map/ppermute | solution.py:23
  49.2 3.2 %collective-permute-done.9 = bf16[576,256]{1,0:T(8,128)(2,1)S(1)} collective-permute-done((bf16[576,256]{1,0:T(8,128)(2,1)S(1)}, bf16[576,256]{1,0:T(8,128)(2,1)S(1)}, u32[]{:S(2)}, u32[]{:S(2)}) %collective-permute-start.9) | collective-permute-done | bytes 294944 | tf_op jit(solution)/shard_map/ppermute | solution.py:23
  52.4 4.5 %collective-permute-start.11 = (bf16[2,64,576]{2,1,0:T(8,128)(2,1)S(1)}, bf16[2,64,576]{2,1,0:T(8,128)(2,1)S(1)}, u32[]{:S(2)}, u32[]{:S(2)}) collective-permute-start(bf16[2,64,576]{2,1,0:T(8,128)(2,1)S(1)} %get-tuple-element.85), channel_id=1, source_target_pairs={{0,128},{128,0},{1,129},{129,1},{2,130},{130,2},{3,131},{131,3},{4... | collective-permute-start | bytes 442376 | tf_op jit(solution)/shard_map/ppermute | solution.py:23
  57.7 2.4 %collective-permute-start.13 = (bf16[2304,256]{1,0:T(8,128)(2,1)S(1)}, bf16[2304,256]{1,0:T(8,128)(2,1)S(1)}, u32[]{:S(2)}, u32[]{:S(2)}) collective-permute-start(bf16[2304,256]{1,0:T(8,128)(2,1)S(1)} %multiply_convert_fusion), channel_id=1, source_target_pairs={{0,16},{16,0},{1,17},{17,1},{2,18},{18,2},{3,19},{19,3},{4,20},{20... | collective-permute-start | bytes 3538952 | tf_op jit(solution)/shard_map/ppermute | solution.py:23
  60.4 2.2 %collective-permute-done.13 = bf16[2304,256]{1,0:T(8,128)(2,1)S(1)} collective-permute-done((bf16[2304,256]{1,0:T(8,128)(2,1)S(1)}, bf16[2304,256]{1,0:T(8,128)(2,1)S(1)}, u32[]{:S(2)}, u32[]{:S(2)}) %collective-permute-start.13) | collective-permute-done | bytes 1179680 | tf_op jit(solution)/shard_map/ppermute | solution.py:23
  62.7 2.3 %collective-permute-start.15 = (bf16[64,576]{1,0:T(8,128)(2,1)S(1)}, bf16[64,576]{1,0:T(8,128)(2,1)S(1)}, u32[]{:S(2)}, u32[]{:S(2)}) collective-permute-start(bf16[64,576]{1,0:T(8,128)(2,1)S(1)} %get-tuple-element.148), channel_id=1, source_target_pairs={{0,16},{16,0},{1,17},{17,1},{2,18},{18,2},{3,19},{19,3},{4,20},{20... | collective-permute-start | bytes 221192 | tf_op jit(solution)/shard_map/ppermute | solution.py:23
  66.1 2.1 %fusion.84 = f32[512,576]{1,0:T(8,128)S(1)} fusion(bf16[2304,512]{1,0:T(8,128)(2,1)S(1)} %constant_dynamic-update-slice_fusion, bf16[2304,576]{1,0:T(8,128)(2,1)S(1)} %bitcast.116), kind=kOutput, calls=%fused_computation.191 | convolution fusion | flops 1358954496 | bytes 6193152 | tf_op jit(solution)/shard_map/dot_general | solution.py:249
  77.0 7.2 %collective-permute-done.19 = bf16[288,576]{1,0:T(8,128)(2,1)S(1)} collective-permute-done((bf16[288,576]{1,0:T(8,128)(2,1)S(1)}, bf16[288,576]{1,0:T(8,128)(2,1)S(1)}, u32[]{:S(2)}, u32[]{:S(2)}) %collective-permute-start.19) | collective-permute-done | bytes 331808 | tf_op jit(solution)/shard_map/ppermute | solution.py:23
  84.2 2.0 %collective-permute-done.18 = bf16[288,576]{1,0:T(8,128)(2,1)S(1)} collective-permute-done((bf16[288,576]{1,0:T(8,128)(2,1)S(1)}, bf16[288,576]{1,0:T(8,128)(2,1)S(1)}, u32[]{:S(2)}, u32[]{:S(2)}) %collective-permute-start.18) | collective-permute-done | bytes 331808 | tf_op jit(solution)/shard_map/ppermute | solution.py:23
  86.8 3.2 %collective-permute-start.22 = (bf16[592,256]{1,0:T(8,128)(2,1)S(1)}, bf16[592,256]{1,0:T(8,128)(2,1)S(1)}, u32[]{:S(2)}, u32[]{:S(2)}) collective-permute-start(bf16[592,256]{1,0:T(8,128)(2,1)S(1)} %get-tuple-element.96), channel_id=1, source_target_pairs={{0,3},{1,0},{2,1},{3,2},{4,7},{5,4},{6,5},{7,6},{8,11},{9,8},{10,9... | collective-permute-start | bytes 909320 | tf_op jit(solution)/shard_map/ppermute | solution.py:23
  90.0 1.7 %collective-permute-start.23 = (bf16[592,256]{1,0:T(8,128)(2,1)S(1)}, bf16[592,256]{1,0:T(8,128)(2,1)S(1)}, u32[]{:S(2)}, u32[]{:S(2)}) collective-permute-start(bf16[592,256]{1,0:T(8,128)(2,1)S(1)} %get-tuple-element.97), channel_id=1, source_target_pairs={{0,2},{1,3},{2,0},{3,1},{4,6},{5,7},{6,4},{7,5},{8,10},{9,11},{10,... | collective-permute-start | bytes 909320 | tf_op jit(solution)/shard_map/ppermute | solution.py:23
  93.1 3.0 %collective-permute-done.21 = bf16[592,256]{1,0:T(8,128)(2,1)S(1)} collective-permute-done((bf16[592,256]{1,0:T(8,128)(2,1)S(1)}, bf16[592,256]{1,0:T(8,128)(2,1)S(1)}, u32[]{:S(2)}, u32[]{:S(2)}) %collective-permute-start.21) | collective-permute-done | bytes 303136 | tf_op jit(solution)/shard_map/ppermute | solution.py:23
  96.0 7.4 %collective-permute-done.23 = bf16[592,256]{1,0:T(8,128)(2,1)S(1)} collective-permute-done((bf16[592,256]{1,0:T(8,128)(2,1)S(1)}, bf16[592,256]{1,0:T(8,128)(2,1)S(1)}, u32[]{:S(2)}, u32[]{:S(2)}) %collective-permute-start.23) | collective-permute-done | bytes 303136 | tf_op jit(solution)/shard_map/ppermute | solution.py:23
  103.9 1.9 %collective-permute-start.25 = (bf16[160,256]{1,0:T(8,128)(2,1)S(1)}, bf16[160,256]{1,0:T(8,128)(2,1)S(1)}, u32[]{:S(2)}, u32[]{:S(2)}) collective-permute-start(bf16[160,256]{1,0:T(8,128)(2,1)S(1)} %get-tuple-element.160), channel_id=1, source_target_pairs={{0,4},{4,8},{8,12},{12,0},{1,5},{5,9},{9,13},{13,1},{2,6},{6,10},{... | collective-permute-start | bytes 245768 | tf_op jit(solution)/shard_map/ppermute | solution.py:23
  107.3 2.7 %collective-permute-start.29 = (bf16[288,576]{1,0:T(8,128)(2,1)S(1)}, bf16[288,576]{1,0:T(8,128)(2,1)S(1)}, u32[]{:S(2)}, u32[]{:S(2)}) collective-permute-start(bf16[288,576]{1,0:T(8,128)(2,1)S(1)} %convolution_convert_fusion.2), channel_id=1, source_target_pairs={{0,96},{32,0},{64,32},{96,64},{1,97},{33,1},{65,33},{97,65},{2,98}... | collective-permute-start | bytes 995336 | tf_op jit(solution)/shard_map/ppermute | solution.py:23
  110.1 1.7 %collective-permute-start.37 = (bf16[144,576]{1,0:T(8,128)(2,1)S(1)}, bf16[144,576]{1,0:T(8,128)(2,1)S(1)}, u32[]{:S(2)}, u32[]{:S(2)}) collective-permute-start(bf16[144,576]{1,0:T(8,128)(2,1)S(1)} %get-tuple-element.138), channel_id=1, source_target_pairs={{0,128},{128,0},{1,129},{129,1},{2,130},{130,2},{3,131},{131,3},{4... | collective-permute-start | bytes 497672 | tf_op jit(solution)/shard_map/ppermute | solution.py:23
  111.8 3.1 %collective-permute-done.27 = bf16[160,256]{1,0:T(8,128)(2,1)S(1)} collective-permute-done((bf16[160,256]{1,0:T(8,128)(2,1)S(1)}, bf16[160,256]{1,0:T(8,128)(2,1)S(1)}, u32[]{:S(2)}, u32[]{:S(2)}) %collective-permute-start.27) | collective-permute-done | bytes 81952 | tf_op jit(solution)/shard_map/ppermute | solution.py:23
  116.1 4.7 %collective-permute-start.30 = (bf16[160,128]{1,0:T(8,128)(2,1)S(1)}, bf16[160,128]{1,0:T(8,128)(2,1)S(1)}, u32[]{:S(2)}, u32[]{:S(2)}) collective-permute-start(bf16[160,128]{1,0:T(8,128)(2,1)S(1)} %pad_maximum_fusion.11), channel_id=1, source_target_pairs={{0,128},{128,0},{1,129},{129,1},{2,130},{130,2},{3,131},{131,3},{4... | collective-permute-start | bytes 122888 | tf_op jit(solution)/shard_map/ppermute | solution.py:23
  120.8 2.2 %collective-permute-done.35 = bf16[288,576]{1,0:T(8,128)(2,1)S(1)} collective-permute-done((bf16[288,576]{1,0:T(8,128)(2,1)S(1)}, bf16[288,576]{1,0:T(8,128)(2,1)S(1)}, u32[]{:S(2)}, u32[]{:S(2)}) %collective-permute-start.35) | collective-permute-done | bytes 331808 | tf_op jit(solution)/shard_map/ppermute | solution.py:23
  123.5 17.0 %collective-permute-start.38 = (bf16[2,144,576]{2,1,0:T(8,128)(2,1)S(1)}, bf16[2,144,576]{2,1,0:T(8,128)(2,1)S(1)}, u32[]{:S(2)}, u32[]{:S(2)}) collective-permute-start(bf16[2,144,576]{2,1,0:T(8,128)(2,1)S(1)} %pad_maximum_fusion.6), channel_id=1, source_target_pairs={{0,16},{16,0},{1,17},{17,1},{2,18},{18,2},{3,19},{19,3},{4,20},{20... | collective-permute-start | bytes 995336 | tf_op jit(solution)/shard_map/ppermute | solution.py:23
  140.5 3.0 %collective-permute-start.31 = (f32[144]{0:T(256)S(1)}, f32[144]{0:T(256)S(1)}, u32[]{:S(2)}, u32[]{:S(2)}) collective-permute-start(f32[144]{0:T(256)S(1)} %slice_add_fusion.1), channel_id=1, source_target_pairs={{0,16},{16,0},{1,17},{17,1},{2,18},{18,2},{3,19},{19,3},{4,20},{20... | collective-permute-start | bytes 1736 | tf_op jit(solution)/shard_map/ppermute | solution.py:23
  144.3 2.7 %collective-permute-start.33 = (f32[144]{0:T(256)S(1)}, f32[144]{0:T(256)S(1)}, u32[]{:S(2)}, u32[]{:S(2)}) collective-permute-start(f32[144]{0:T(256)S(1)} %add.232), channel_id=1, source_target_pairs={{0,96},{32,0},{64,32},{96,64},{1,97},{33,1},{65,33},{97,65},{2,98}... | collective-permute-start | bytes 1736 | tf_op jit(solution)/shard_map/ppermute | solution.py:23
  148.0 3.0 %collective-permute-done.34 = f32[144]{0:T(256)S(1)} collective-permute-done((f32[144]{0:T(256)S(1)}, f32[144]{0:T(256)S(1)}, u32[]{:S(2)}, u32[]{:S(2)}) %collective-permute-start.34) | collective-permute-done | bytes 608 | tf_op jit(solution)/shard_map/ppermute | solution.py:23
  152.9 2.2 %join.1 = (bf16[144,1152]{1,0:T(8,128)(2,1)}, bf16[144,1152]{1,0:T(8,128)(2,1)}) custom-call(bf16[2,144,576]{2,1,0:T(8,128)(2,1)} %bitcast.132, bf16[144,576]{1,0:T(8,128)(2,1)} %copy-done.2, bf16[2,144,576]{2,1,0:T(8,128)(2,1)} %copy-done.1), custom_call_target="tpu_custom_call" | custom-call | tf_op jit(solution)/shard_map/join/pallas_call | solution.py:122
  (157 shorter events, 31.8 us)
Async XLA Ops:
  2.0 18.1 %collective-permute-start = (bf16[208,576]{1,0:T(8,128)(2,1)S(1)}, bf16[208,576]{1,0:T(8,128)(2,1)S(1)}, u32[]{:S(2)}, u32[]{:S(2)}) collective-permute-start(bf16[208,576]{1,0:T(8,128)(2,1)S(1)} %get-tuple-element.64), channel_id=1, source_target_pairs={{0,16},{16,0},{1,17},{17,1},{2,18},{18,2},{3,19},{19,3},{4,20},{20... | collective-permute-start | bytes 718856 | tf_op jit(solution)/shard_map/ppermute | solution.py:23
  5.3 9.5 %collective-permute-start.1 = (bf16[576,128]{1,0:T(8,128)(2,1)}, bf16[576,128]{1,0:T(8,128)(2,1)S(1)}, u32[]{:S(2)}, u32[]{:S(2)}) collective-permute-start(bf16[576,128]{1,0:T(8,128)(2,1)} %bitcast.142), channel_id=1, source_target_pairs={{0,128},{128,0},{1,129},{129,1},{2,130},{130,2},{3,131},{131,3},{4... | collective-permute-start | bytes 442376 | tf_op jit(solution)/shard_map/ppermute | solution.py:23
  11.9 27.2 %collective-permute-start.4 = (bf16[144,576]{1,0:T(8,128)(2,1)S(1)}, bf16[144,576]{1,0:T(8,128)(2,1)S(1)}, u32[]{:S(2)}, u32[]{:S(2)}) collective-permute-start(bf16[144,576]{1,0:T(8,128)(2,1)S(1)} %get-tuple-element.75), channel_id=1, source_target_pairs={{0,128},{128,0},{1,129},{129,1},{2,130},{130,2},{3,131},{131,3},{4... | collective-permute-start | bytes 497672 | tf_op jit(solution)/shard_map/ppermute | solution.py:23
  14.9 20.0 %collective-permute-start.5 = (bf16[144,576]{1,0:T(8,128)(2,1)S(1)}, bf16[144,576]{1,0:T(8,128)(2,1)S(1)}, u32[]{:S(2)}, u32[]{:S(2)}) collective-permute-start(bf16[144,576]{1,0:T(8,128)(2,1)S(1)} %get-tuple-element.76), channel_id=1, source_target_pairs={{0,128},{128,0},{1,129},{129,1},{2,130},{130,2},{3,131},{131,3},{4... | collective-permute-start | bytes 497672 | tf_op jit(solution)/shard_map/ppermute | solution.py:23
  20.2 16.0 %collective-permute-start.2 = (bf16[2,144,576]{2,1,0:T(8,128)(2,1)S(1)}, bf16[2,144,576]{2,1,0:T(8,128)(2,1)S(1)}, u32[]{:S(2)}, u32[]{:S(2)}) collective-permute-start(bf16[2,144,576]{2,1,0:T(8,128)(2,1)S(1)} %maximum_select_fusion), channel_id=1, source_target_pairs={{0,32},{32,64},{64,96},{96,0},{1,33},{33,65},{65,97},{97,1},{2,34}... | collective-permute-start | bytes 995336 | tf_op jit(solution)/shard_map/ppermute | solution.py:23
  21.5 14.8 %collective-permute-start.3 = (bf16[2,144,576]{2,1,0:T(8,128)(2,1)S(1)}, bf16[2,144,576]{2,1,0:T(8,128)(2,1)S(1)}, u32[]{:S(2)}, u32[]{:S(2)}) collective-permute-start(bf16[2,144,576]{2,1,0:T(8,128)(2,1)S(1)} %maximum_select_fusion), channel_id=1, source_target_pairs={{0,96},{32,0},{64,32},{96,64},{1,97},{33,1},{65,33},{97,65},{2,98}... | collective-permute-start | bytes 995336 | tf_op jit(solution)/shard_map/ppermute | solution.py:23
  23.0 37.1 %collective-permute-start.10 = (bf16[2,144,576]{2,1,0:T(8,128)(2,1)S(1)}, bf16[2,144,576]{2,1,0:T(8,128)(2,1)S(1)}, u32[]{:S(2)}, u32[]{:S(2)}) collective-permute-start(bf16[2,144,576]{2,1,0:T(8,128)(2,1)S(1)} %maximum_select_fusion), channel_id=1, source_target_pairs={{0,64},{32,96},{64,0},{96,32},{1,65},{33,97},{65,1},{97,33},{2,66}... | collective-permute-start | bytes 995336 | tf_op jit(solution)/shard_map/ppermute | solution.py:23
  34.9 5.7 %collective-permute-start.6 = (bf16[144,576]{1,0:T(8,128)(2,1)S(1)}, bf16[144,576]{1,0:T(8,128)(2,1)S(1)}, u32[]{:S(2)}, u32[]{:S(2)}) collective-permute-start(bf16[144,576]{1,0:T(8,128)(2,1)S(1)} %collective-permute-done.5), channel_id=1, source_target_pairs={{0,16},{16,0},{1,17},{17,1},{2,18},{18,2},{3,19},{19,3},{4,20},{20... | collective-permute-start | bytes 497672 | tf_op jit(solution)/shard_map/ppermute | solution.py:23
  36.3 6.9 %collective-permute-start.7 = (bf16[576,256]{1,0:T(8,128)(2,1)S(1)}, bf16[576,256]{1,0:T(8,128)(2,1)S(1)}, u32[]{:S(2)}, u32[]{:S(2)}) collective-permute-start(bf16[576,256]{1,0:T(8,128)(2,1)S(1)} %pad_maximum_fusion.7), channel_id=1, source_target_pairs={{0,1},{1,2},{2,3},{3,0},{4,5},{5,6},{6,7},{7,4},{8,9},{9,10},{10,1... | collective-permute-start | bytes 884744 | tf_op jit(solution)/shard_map/ppermute | solution.py:23
  37.6 11.5 %collective-permute-start.8 = (bf16[576,256]{1,0:T(8,128)(2,1)S(1)}, bf16[576,256]{1,0:T(8,128)(2,1)S(1)}, u32[]{:S(2)}, u32[]{:S(2)}) collective-permute-start(bf16[576,256]{1,0:T(8,128)(2,1)S(1)} %pad_maximum_fusion.7), channel_id=1, source_target_pairs={{0,3},{1,0},{2,1},{3,2},{4,7},{5,4},{6,5},{7,6},{8,11},{9,8},{10,9... | collective-permute-start | bytes 884744 | tf_op jit(solution)/shard_map/ppermute | solution.py:23
  39.1 13.3 %collective-permute-start.9 = (bf16[576,256]{1,0:T(8,128)(2,1)S(1)}, bf16[576,256]{1,0:T(8,128)(2,1)S(1)}, u32[]{:S(2)}, u32[]{:S(2)}) collective-permute-start(bf16[576,256]{1,0:T(8,128)(2,1)S(1)} %pad_maximum_fusion.7), channel_id=1, source_target_pairs={{0,2},{1,3},{2,0},{3,1},{4,6},{5,7},{6,4},{7,5},{8,10},{9,11},{10,... | collective-permute-start | bytes 884744 | tf_op jit(solution)/shard_map/ppermute | solution.py:23
  40.7 16.9 %collective-permute-start.12 = (bf16[2,144,576]{2,1,0:T(8,128)(2,1)S(1)}, bf16[2,144,576]{2,1,0:T(8,128)(2,1)S(1)}, u32[]{:S(2)}, u32[]{:S(2)}) collective-permute-start(bf16[2,144,576]{2,1,0:T(8,128)(2,1)S(1)} %maximum_select_fusion.1), channel_id=1, source_target_pairs={{0,32},{32,64},{64,96},{96,0},{1,33},{33,65},{65,97},{97,1},{2,34}... | collective-permute-start | bytes 995336 | tf_op jit(solution)/shard_map/ppermute | solution.py:23
  43.2 17.2 %collective-permute-start.14 = (bf16[2,144,576]{2,1,0:T(8,128)(2,1)S(1)}, bf16[2,144,576]{2,1,0:T(8,128)(2,1)S(1)}, u32[]{:S(2)}, u32[]{:S(2)}) collective-permute-start(bf16[2,144,576]{2,1,0:T(8,128)(2,1)S(1)} %maximum_select_fusion.1), channel_id=1, source_target_pairs={{0,64},{32,96},{64,0},{96,32},{1,65},{33,97},{65,1},{97,33},{2,66}... | collective-permute-start | bytes 995336 | tf_op jit(solution)/shard_map/ppermute | solution.py:23
  49.0 16.2 %collective-permute-start.16 = (bf16[2,144,576]{2,1,0:T(8,128)(2,1)S(1)}, bf16[2,144,576]{2,1,0:T(8,128)(2,1)S(1)}, u32[]{:S(2)}, u32[]{:S(2)}) collective-permute-start(bf16[2,144,576]{2,1,0:T(8,128)(2,1)S(1)} %maximum_select_fusion.1), channel_id=1, source_target_pairs={{0,96},{32,0},{64,32},{96,64},{1,97},{33,1},{65,33},{97,65},{2,98}... | collective-permute-start | bytes 995336 | tf_op jit(solution)/shard_map/ppermute | solution.py:23
  52.4 10.2 %collective-permute-start.11 = (bf16[2,64,576]{2,1,0:T(8,128)(2,1)S(1)}, bf16[2,64,576]{2,1,0:T(8,128)(2,1)S(1)}, u32[]{:S(2)}, u32[]{:S(2)}) collective-permute-start(bf16[2,64,576]{2,1,0:T(8,128)(2,1)S(1)} %get-tuple-element.85), channel_id=1, source_target_pairs={{0,128},{128,0},{1,129},{129,1},{2,130},{130,2},{3,131},{131,3},{4... | collective-permute-start | bytes 442376 | tf_op jit(solution)/shard_map/ppermute | solution.py:23
  57.7 4.9 %collective-permute-start.13 = (bf16[2304,256]{1,0:T(8,128)(2,1)S(1)}, bf16[2304,256]{1,0:T(8,128)(2,1)S(1)}, u32[]{:S(2)}, u32[]{:S(2)}) collective-permute-start(bf16[2304,256]{1,0:T(8,128)(2,1)S(1)} %multiply_convert_fusion), channel_id=1, source_target_pairs={{0,16},{16,0},{1,17},{17,1},{2,18},{18,2},{3,19},{19,3},{4,20},{20... | collective-permute-start | bytes 3538952 | tf_op jit(solution)/shard_map/ppermute | solution.py:23
  73.6 10.6 %collective-permute-start.19 = (bf16[288,576]{1,0:T(8,128)(2,1)S(1)}, bf16[288,576]{1,0:T(8,128)(2,1)S(1)}, u32[]{:S(2)}, u32[]{:S(2)}) collective-permute-start(bf16[288,576]{1,0:T(8,128)(2,1)S(1)} %convolution_convert_fusion.5), channel_id=1, source_target_pairs={{0,96},{32,0},{64,32},{96,64},{1,97},{33,1},{65,33},{97,65},{2,98}... | collective-permute-start | bytes 995336 | tf_op jit(solution)/shard_map/ppermute | solution.py:23
  75.1 11.2 %collective-permute-start.18 = (bf16[288,576]{1,0:T(8,128)(2,1)S(1)}, bf16[288,576]{1,0:T(8,128)(2,1)S(1)}, u32[]{:S(2)}, u32[]{:S(2)}) collective-permute-start(bf16[288,576]{1,0:T(8,128)(2,1)S(1)} %convolution_convert_fusion.6), channel_id=1, source_target_pairs={{0,32},{32,64},{64,96},{96,0},{1,33},{33,65},{65,97},{97,1},{2,34}... | collective-permute-start | bytes 995336 | tf_op jit(solution)/shard_map/ppermute | solution.py:23
  86.3 9.7 %collective-permute-start.21 = (bf16[592,256]{1,0:T(8,128)(2,1)S(1)}, bf16[592,256]{1,0:T(8,128)(2,1)S(1)}, u32[]{:S(2)}, u32[]{:S(2)}) collective-permute-start(bf16[592,256]{1,0:T(8,128)(2,1)S(1)} %get-tuple-element.95), channel_id=1, source_target_pairs={{0,1},{1,2},{2,3},{3,0},{4,5},{5,6},{6,7},{7,4},{8,9},{9,10},{10,1... | collective-permute-start | bytes 909320 | tf_op jit(solution)/shard_map/ppermute | solution.py:23
  86.8 9.2 %collective-permute-start.22 = (bf16[592,256]{1,0:T(8,128)(2,1)S(1)}, bf16[592,256]{1,0:T(8,128)(2,1)S(1)}, u32[]{:S(2)}, u32[]{:S(2)}) collective-permute-start(bf16[592,256]{1,0:T(8,128)(2,1)S(1)} %get-tuple-element.96), channel_id=1, source_target_pairs={{0,3},{1,0},{2,1},{3,2},{4,7},{5,4},{6,5},{7,6},{8,11},{9,8},{10,9... | collective-permute-start | bytes 909320 | tf_op jit(solution)/shard_map/ppermute | solution.py:23
  90.0 13.4 %collective-permute-start.23 = (bf16[592,256]{1,0:T(8,128)(2,1)S(1)}, bf16[592,256]{1,0:T(8,128)(2,1)S(1)}, u32[]{:S(2)}, u32[]{:S(2)}) collective-permute-start(bf16[592,256]{1,0:T(8,128)(2,1)S(1)} %get-tuple-element.97), channel_id=1, source_target_pairs={{0,2},{1,3},{2,0},{3,1},{4,6},{5,7},{6,4},{7,5},{8,10},{9,11},{10,... | collective-permute-start | bytes 909320 | tf_op jit(solution)/shard_map/ppermute | solution.py:23
  92.1 11.5 %collective-permute-start.24 = (bf16[288,576]{1,0:T(8,128)(2,1)S(1)}, bf16[288,576]{1,0:T(8,128)(2,1)S(1)}, u32[]{:S(2)}, u32[]{:S(2)}) collective-permute-start(bf16[288,576]{1,0:T(8,128)(2,1)S(1)} %convolution_convert_fusion.4), channel_id=1, source_target_pairs={{0,64},{32,96},{64,0},{96,32},{1,65},{33,97},{65,1},{97,33},{2,66}... | collective-permute-start | bytes 995336 | tf_op jit(solution)/shard_map/ppermute | solution.py:23
  103.9 6.1 %collective-permute-start.25 = (bf16[160,256]{1,0:T(8,128)(2,1)S(1)}, bf16[160,256]{1,0:T(8,128)(2,1)S(1)}, u32[]{:S(2)}, u32[]{:S(2)}) collective-permute-start(bf16[160,256]{1,0:T(8,128)(2,1)S(1)} %get-tuple-element.160), channel_id=1, source_target_pairs={{0,4},{4,8},{8,12},{12,0},{1,5},{5,9},{9,13},{13,1},{2,6},{6,10},{... | collective-permute-start | bytes 245768 | tf_op jit(solution)/shard_map/ppermute | solution.py:23
  105.8 4.3 %collective-permute-start.26 = (bf16[160,256]{1,0:T(8,128)(2,1)S(1)}, bf16[160,256]{1,0:T(8,128)(2,1)S(1)}, u32[]{:S(2)}, u32[]{:S(2)}) collective-permute-start(bf16[160,256]{1,0:T(8,128)(2,1)S(1)} %get-tuple-element.161), channel_id=1, source_target_pairs={{0,12},{4,0},{8,4},{12,8},{1,13},{5,1},{9,5},{13,9},{2,14},{6,2},{... | collective-permute-start | bytes 245768 | tf_op jit(solution)/shard_map/ppermute | solution.py:23
  107.3 7.7 %collective-permute-start.27 = (bf16[160,256]{1,0:T(8,128)(2,1)S(1)}, bf16[160,256]{1,0:T(8,128)(2,1)S(1)}, u32[]{:S(2)}, u32[]{:S(2)}) collective-permute-start(bf16[160,256]{1,0:T(8,128)(2,1)S(1)} %get-tuple-element.162), channel_id=1, source_target_pairs={{0,8},{4,12},{8,0},{12,4},{1,9},{5,13},{9,1},{13,5},{2,10},{6,14},... | collective-permute-start | bytes 245768 | tf_op jit(solution)/shard_map/ppermute | solution.py:23
  107.3 8.8 %collective-permute-start.28 = (bf16[288,576]{1,0:T(8,128)(2,1)S(1)}, bf16[288,576]{1,0:T(8,128)(2,1)S(1)}, u32[]{:S(2)}, u32[]{:S(2)}) collective-permute-start(bf16[288,576]{1,0:T(8,128)(2,1)S(1)} %convolution_convert_fusion.3), channel_id=1, source_target_pairs={{0,32},{32,64},{64,96},{96,0},{1,33},{33,65},{65,97},{97,1},{2,34}... | collective-permute-start | bytes 995336 | tf_op jit(solution)/shard_map/ppermute | solution.py:23
  107.3 8.8 %collective-permute-start.29 = (bf16[288,576]{1,0:T(8,128)(2,1)S(1)}, bf16[288,576]{1,0:T(8,128)(2,1)S(1)}, u32[]{:S(2)}, u32[]{:S(2)}) collective-permute-start(bf16[288,576]{1,0:T(8,128)(2,1)S(1)} %convolution_convert_fusion.2), channel_id=1, source_target_pairs={{0,96},{32,0},{64,32},{96,64},{1,97},{33,1},{65,33},{97,65},{2,98}... | collective-permute-start | bytes 995336 | tf_op jit(solution)/shard_map/ppermute | solution.py:23
  110.0 13.0 %collective-permute-start.35 = (bf16[288,576]{1,0:T(8,128)(2,1)S(1)}, bf16[288,576]{1,0:T(8,128)(2,1)S(1)}, u32[]{:S(2)}, u32[]{:S(2)}) collective-permute-start(bf16[288,576]{1,0:T(8,128)(2,1)S(1)} %convolution_convert_fusion.1), channel_id=1, source_target_pairs={{0,64},{32,96},{64,0},{96,32},{1,65},{33,97},{65,1},{97,33},{2,66}... | collective-permute-start | bytes 995336 | tf_op jit(solution)/shard_map/ppermute | solution.py:23
  110.1 13.3 %collective-permute-start.37 = (bf16[144,576]{1,0:T(8,128)(2,1)S(1)}, bf16[144,576]{1,0:T(8,128)(2,1)S(1)}, u32[]{:S(2)}, u32[]{:S(2)}) collective-permute-start(bf16[144,576]{1,0:T(8,128)(2,1)S(1)} %get-tuple-element.138), channel_id=1, source_target_pairs={{0,128},{128,0},{1,129},{129,1},{2,130},{130,2},{3,131},{131,3},{4... | collective-permute-start | bytes 497672 | tf_op jit(solution)/shard_map/ppermute | solution.py:23
  114.9 36.6 %collective-permute-start.36 = (bf16[144,576]{1,0:T(8,128)(2,1)S(1)}, bf16[144,576]{1,0:T(8,128)(2,1)S(1)}, u32[]{:S(2)}, u32[]{:S(2)}) collective-permute-start(bf16[144,576]{1,0:T(8,128)(2,1)S(1)} %get-tuple-element.139), channel_id=1, source_target_pairs={{0,128},{128,0},{1,129},{129,1},{2,130},{130,2},{3,131},{131,3},{4... | collective-permute-start | bytes 497672 | tf_op jit(solution)/shard_map/ppermute | solution.py:23
  116.1 24.4 %collective-permute-start.30 = (bf16[160,128]{1,0:T(8,128)(2,1)S(1)}, bf16[160,128]{1,0:T(8,128)(2,1)S(1)}, u32[]{:S(2)}, u32[]{:S(2)}) collective-permute-start(bf16[160,128]{1,0:T(8,128)(2,1)S(1)} %pad_maximum_fusion.11), channel_id=1, source_target_pairs={{0,128},{128,0},{1,129},{129,1},{2,130},{130,2},{3,131},{131,3},{4... | collective-permute-start | bytes 122888 | tf_op jit(solution)/shard_map/ppermute | solution.py:23
  123.5 28.0 %collective-permute-start.38 = (bf16[2,144,576]{2,1,0:T(8,128)(2,1)S(1)}, bf16[2,144,576]{2,1,0:T(8,128)(2,1)S(1)}, u32[]{:S(2)}, u32[]{:S(2)}) collective-permute-start(bf16[2,144,576]{2,1,0:T(8,128)(2,1)S(1)} %pad_maximum_fusion.6), channel_id=1, source_target_pairs={{0,16},{16,0},{1,17},{17,1},{2,18},{18,2},{3,19},{19,3},{4,20},{20... | collective-permute-start | bytes 995336 | tf_op jit(solution)/shard_map/ppermute | solution.py:23
  (12 other events, 82.9 us)

commit v7 on v4

--- a/solution.py
+++ b/solution.py
@@ -263,10 +263,11 @@
         return jnp.dot(as_block(by_rows, zplace, xplace), d_both, preferred_element_type=F32)
 
     away_parts = [part(far_zh, x_to[by]).astype(BF16) for by in steps]
-    near_parts = [part(zh, x_to[by]).astype(BF16) for by in steps]
     away_got = [turned(away_parts[k], "x", steps[k]) for k in (0, 1)]
 
     got = swapped(d_normed(d_both[2 * group :]).astype(BF16), "core")
+    got, near_zh = barrier((got, zh))
+    near_parts = [part(near_zh, x_to[by]).astype(BF16) for by in steps]
     row = row_part[: 2 * group] + swapped(row_part[2 * group :], "core")
     mine = d_normed(d_both[: 2 * group]) + got.astype(F32)
     mine = mine.reshape(4, 4, own_rows, 2 * group)

time: 152 us -> 152 us (level)
  no operation moved by 1% of the time
where the time goes in v7:
time: 152 us
  starting transfers between devices  82.9 us (55%)
  waiting for transfers between devices  47.6 us (31%)
  matrix products  7.46 us (5%)
  Pallas kernels  4.93 us (3%)
  other arithmetic  4.58 us (3%)
  local copies, waits for them, and re-layouts  3.36 us (2%)
    ppermute x39, starting transfers between devices, turned(): return lax.ppermute(array, axis, [(i, (i + by) % n) for i in range(n)])  82.9 us
    ppermute x39, waiting for transfers between devices, turned(): return lax.ppermute(array, axis, [(i, (i + by) % n) for i in range(n)])  47.6 us
    dot_general x8, matrix products, part(): jnp.dot(as_block(by_rows, zplace, xplace), d_both, preferred_element_type...  3.15 us
  transfers between devices with their start and end apart: 39, of which 15 were waited for; matrix products, arithmetic and copies ran while one was open for 5% of the time, Pallas kernels for 1%

profile of v7, /device:TPU:1, one launch (start us, length us, event | category | flops | bytes accessed | tf_op | source)
XLA Modules:
  0.0 152.1 jit_solution(4607599638531583871)
XLA Ops:
  2.0 3.3 %collective-permute-start = (bf16[208,576]{1,0:T(8,128)(2,1)S(1)}, bf16[208,576]{1,0:T(8,128)(2,1)S(1)}, u32[]{:S(2)}, u32[]{:S(2)}) collective-permute-start(bf16[208,576]{1,0:T(8,128)(2,1)S(1)} %get-tuple-element.65), channel_id=1, source_target_pairs={{0,16},{16,0},{1,17},{17,1},{2,18},{18,2},{3,19},{19,3},{4,20},{20... | collective-permute-start | bytes 718856 | tf_op jit(solution)/shard_map/ppermute | solution.py:23
  5.3 5.2 %collective-permute-start.1 = (bf16[576,128]{1,0:T(8,128)(2,1)}, bf16[576,128]{1,0:T(8,128)(2,1)S(1)}, u32[]{:S(2)}, u32[]{:S(2)}) collective-permute-start(bf16[576,128]{1,0:T(8,128)(2,1)} %bitcast.142), channel_id=1, source_target_pairs={{0,128},{128,0},{1,129},{129,1},{2,130},{130,2},{3,131},{131,3},{4... | collective-permute-start | bytes 442376 | tf_op jit(solution)/shard_map/ppermute | solution.py:23
  12.5 2.4 %collective-permute-done.1 = bf16[576,128]{1,0:T(8,128)(2,1)S(1)} collective-permute-done((bf16[576,128]{1,0:T(8,128)(2,1)}, bf16[576,128]{1,0:T(8,128)(2,1)S(1)}, u32[]{:S(2)}, u32[]{:S(2)}) %collective-permute-start.1) | collective-permute-done | bytes 147488 | tf_op jit(solution)/shard_map/ppermute | solution.py:23
  14.9 5.2 %collective-permute-start.5 = (bf16[144,576]{1,0:T(8,128)(2,1)S(1)}, bf16[144,576]{1,0:T(8,128)(2,1)S(1)}, u32[]{:S(2)}, u32[]{:S(2)}) collective-permute-start(bf16[144,576]{1,0:T(8,128)(2,1)S(1)} %get-tuple-element.77), channel_id=1, source_target_pairs={{0,128},{128,0},{1,129},{129,1},{2,130},{130,2},{3,131},{131,3},{4... | collective-permute-start | bytes 497672 | tf_op jit(solution)/shard_map/ppermute | solution.py:23
  24.8 10.1 %collective-permute-done.5 = bf16[144,576]{1,0:T(8,128)(2,1)S(1)} collective-permute-done((bf16[144,576]{1,0:T(8,128)(2,1)S(1)}, bf16[144,576]{1,0:T(8,128)(2,1)S(1)}, u32[]{:S(2)}, u32[]{:S(2)}) %collective-permute-start.5) | collective-permute-done | bytes 165920 | tf_op jit(solution)/shard_map/ppermute | solution.py:23
  37.6 1.5 %collective-permute-start.8 = (bf16[576,256]{1,0:T(8,128)(2,1)S(1)}, bf16[576,256]{1,0:T(8,128)(2,1)S(1)}, u32[]{:S(2)}, u32[]{:S(2)}) collective-permute-start(bf16[576,256]{1,0:T(8,128)(2,1)S(1)} %pad_maximum_fusion.7), channel_id=1, source_target_pairs={{0,3},{1,0},{2,1},{3,2},{4,7},{5,4},{6,5},{7,6},{8,11},{9,8},{10,9... | collective-permute-start | bytes 884744 | tf_op jit(solution)/shard_map/ppermute | solution.py:23
  39.1 1.6 %collective-permute-start.9 = (bf16[576,256]{1,0:T(8,128)(2,1)S(1)}, bf16[576,256]{1,0:T(8,128)(2,1)S(1)}, u32[]{:S(2)}, u32[]{:S(2)}) collective-permute-start(bf16[576,256]{1,0:T(8,128)(2,1)S(1)} %pad_maximum_fusion.7), channel_id=1, source_target_pairs={{0,2},{1,3},{2,0},{3,1},{4,6},{5,7},{6,4},{7,5},{8,10},{9,11},{10,... | collective-permute-start | bytes 884744 | tf_op jit(solution)/shard_map/ppermute | solution.py:23
  43.2 5.8 %collective-permute-start.15 = (bf16[2,144,576]{2,1,0:T(8,128)(2,1)S(1)}, bf16[2,144,576]{2,1,0:T(8,128)(2,1)S(1)}, u32[]{:S(2)}, u32[]{:S(2)}) collective-permute-start(bf16[2,144,576]{2,1,0:T(8,128)(2,1)S(1)} %maximum_select_fusion.1), channel_id=1, source_target_pairs={{0,64},{32,96},{64,0},{96,32},{1,65},{33,97},{65,1},{97,33},{2,66}... | collective-permute-start | bytes 995336 | tf_op jit(solution)/shard_map/ppermute | solution.py:23
  49.2 3.2 %collective-permute-done.9 = bf16[576,256]{1,0:T(8,128)(2,1)S(1)} collective-permute-done((bf16[576,256]{1,0:T(8,128)(2,1)S(1)}, bf16[576,256]{1,0:T(8,128)(2,1)S(1)}, u32[]{:S(2)}, u32[]{:S(2)}) %collective-permute-start.9) | collective-permute-done | bytes 294944 | tf_op jit(solution)/shard_map/ppermute | solution.py:23
  52.4 4.5 %collective-permute-start.11 = (bf16[2,64,576]{2,1,0:T(8,128)(2,1)S(1)}, bf16[2,64,576]{2,1,0:T(8,128)(2,1)S(1)}, u32[]{:S(2)}, u32[]{:S(2)}) collective-permute-start(bf16[2,64,576]{2,1,0:T(8,128)(2,1)S(1)} %get-tuple-element.86), channel_id=1, source_target_pairs={{0,128},{128,0},{1,129},{129,1},{2,130},{130,2},{3,131},{131,3},{4... | collective-permute-start | bytes 442376 | tf_op jit(solution)/shard_map/ppermute | solution.py:23
  57.7 2.4 %collective-permute-start.14 = (bf16[2304,256]{1,0:T(8,128)(2,1)S(1)}, bf16[2304,256]{1,0:T(8,128)(2,1)S(1)}, u32[]{:S(2)}, u32[]{:S(2)}) collective-permute-start(bf16[2304,256]{1,0:T(8,128)(2,1)S(1)} %multiply_convert_fusion), channel_id=1, source_target_pairs={{0,16},{16,0},{1,17},{17,1},{2,18},{18,2},{3,19},{19,3},{4,20},{20... | collective-permute-start | bytes 3538952 | tf_op jit(solution)/shard_map/ppermute | solution.py:23
  60.4 2.2 %collective-permute-done.14 = bf16[2304,256]{1,0:T(8,128)(2,1)S(1)} collective-permute-done((bf16[2304,256]{1,0:T(8,128)(2,1)S(1)}, bf16[2304,256]{1,0:T(8,128)(2,1)S(1)}, u32[]{:S(2)}, u32[]{:S(2)}) %collective-permute-start.14) | collective-permute-done | bytes 1179680 | tf_op jit(solution)/shard_map/ppermute | solution.py:23
  63.0 2.1 %fusion.82 = f32[512,576]{1,0:T(8,128)S(1)} fusion(bf16[2304,512]{1,0:T(8,128)(2,1)S(1)} %constant_dynamic-update-slice_fusion, bf16[2304,576]{1,0:T(8,128)(2,1)S(1)} %bitcast.116), kind=kOutput, calls=%fused_computation.191 | convolution fusion | flops 1358954496 | bytes 6193152 | tf_op jit(solution)/shard_map/dot_general | solution.py:248
  65.2 2.4 %collective-permute-start.16 = (bf16[64,576]{1,0:T(8,128)(2,1)S(1)}, bf16[64,576]{1,0:T(8,128)(2,1)S(1)}, u32[]{:S(2)}, u32[]{:S(2)}) collective-permute-start(bf16[64,576]{1,0:T(8,128)(2,1)S(1)} %get-tuple-element.150), channel_id=1, source_target_pairs={{0,16},{16,0},{1,17},{17,1},{2,18},{18,2},{3,19},{19,3},{4,20},{20... | collective-permute-start | bytes 221192 | tf_op jit(solution)/shard_map/ppermute | solution.py:23
  74.3 2.0 %collective-permute-start.19 = (bf16[288,576]{1,0:T(8,128)(2,1)S(1)}, bf16[288,576]{1,0:T(8,128)(2,1)S(1)}, u32[]{:S(2)}, u32[]{:S(2)}) collective-permute-start(bf16[288,576]{1,0:T(8,128)(2,1)S(1)} %convolution_convert_fusion.5), channel_id=1, source_target_pairs={{0,96},{32,0},{64,32},{96,64},{1,97},{33,1},{65,33},{97,65},{2,98}... | collective-permute-start | bytes 995336 | tf_op jit(solution)/shard_map/ppermute | solution.py:23
  77.6 7.3 %collective-permute-done.19 = bf16[288,576]{1,0:T(8,128)(2,1)S(1)} collective-permute-done((bf16[288,576]{1,0:T(8,128)(2,1)S(1)}, bf16[288,576]{1,0:T(8,128)(2,1)S(1)}, u32[]{:S(2)}, u32[]{:S(2)}) %collective-permute-start.19) | collective-permute-done | bytes 331808 | tf_op jit(solution)/shard_map/ppermute | solution.py:23
  84.9 2.1 %collective-permute-done.18 = bf16[288,576]{1,0:T(8,128)(2,1)S(1)} collective-permute-done((bf16[288,576]{1,0:T(8,128)(2,1)S(1)}, bf16[288,576]{1,0:T(8,128)(2,1)S(1)}, u32[]{:S(2)}, u32[]{:S(2)}) %collective-permute-start.18) | collective-permute-done | bytes 331808 | tf_op jit(solution)/shard_map/ppermute | solution.py:23
  87.5 3.2 %collective-permute-start.22 = (bf16[592,256]{1,0:T(8,128)(2,1)S(1)}, bf16[592,256]{1,0:T(8,128)(2,1)S(1)}, u32[]{:S(2)}, u32[]{:S(2)}) collective-permute-start(bf16[592,256]{1,0:T(8,128)(2,1)S(1)} %get-tuple-element.97), channel_id=1, source_target_pairs={{0,3},{1,0},{2,1},{3,2},{4,7},{5,4},{6,5},{7,6},{8,11},{9,8},{10,9... | collective-permute-start | bytes 909320 | tf_op jit(solution)/shard_map/ppermute | solution.py:23
  90.7 1.7 %collective-permute-start.23 = (bf16[592,256]{1,0:T(8,128)(2,1)S(1)}, bf16[592,256]{1,0:T(8,128)(2,1)S(1)}, u32[]{:S(2)}, u32[]{:S(2)}) collective-permute-start(bf16[592,256]{1,0:T(8,128)(2,1)S(1)} %get-tuple-element.98), channel_id=1, source_target_pairs={{0,2},{1,3},{2,0},{3,1},{4,6},{5,7},{6,4},{7,5},{8,10},{9,11},{10,... | collective-permute-start | bytes 909320 | tf_op jit(solution)/shard_map/ppermute | solution.py:23
  93.7 3.0 %collective-permute-done.21 = bf16[592,256]{1,0:T(8,128)(2,1)S(1)} collective-permute-done((bf16[592,256]{1,0:T(8,128)(2,1)S(1)}, bf16[592,256]{1,0:T(8,128)(2,1)S(1)}, u32[]{:S(2)}, u32[]{:S(2)}) %collective-permute-start.21) | collective-permute-done | bytes 303136 | tf_op jit(solution)/shard_map/ppermute | solution.py:23
  96.7 7.4 %collective-permute-done.23 = bf16[592,256]{1,0:T(8,128)(2,1)S(1)} collective-permute-done((bf16[592,256]{1,0:T(8,128)(2,1)S(1)}, bf16[592,256]{1,0:T(8,128)(2,1)S(1)}, u32[]{:S(2)}, u32[]{:S(2)}) %collective-permute-start.23) | collective-permute-done | bytes 303136 | tf_op jit(solution)/shard_map/ppermute | solution.py:23
  104.6 1.9 %collective-permute-start.25 = (bf16[160,256]{1,0:T(8,128)(2,1)S(1)}, bf16[160,256]{1,0:T(8,128)(2,1)S(1)}, u32[]{:S(2)}, u32[]{:S(2)}) collective-permute-start(bf16[160,256]{1,0:T(8,128)(2,1)S(1)} %get-tuple-element.162), channel_id=1, source_target_pairs={{0,4},{4,8},{8,12},{12,0},{1,5},{5,9},{9,13},{13,1},{2,6},{6,10},{... | collective-permute-start | bytes 245768 | tf_op jit(solution)/shard_map/ppermute | solution.py:23
  107.9 2.7 %collective-permute-start.29 = (bf16[288,576]{1,0:T(8,128)(2,1)S(1)}, bf16[288,576]{1,0:T(8,128)(2,1)S(1)}, u32[]{:S(2)}, u32[]{:S(2)}) collective-permute-start(bf16[288,576]{1,0:T(8,128)(2,1)S(1)} %convolution_convert_fusion.2), channel_id=1, source_target_pairs={{0,96},{32,0},{64,32},{96,64},{1,97},{33,1},{65,33},{97,65},{2,98}... | collective-permute-start | bytes 995336 | tf_op jit(solution)/shard_map/ppermute | solution.py:23
  110.8 2.1 %collective-permute-start.37 = (bf16[144,576]{1,0:T(8,128)(2,1)S(1)}, bf16[144,576]{1,0:T(8,128)(2,1)S(1)}, u32[]{:S(2)}, u32[]{:S(2)}) collective-permute-start(bf16[144,576]{1,0:T(8,128)(2,1)S(1)} %get-tuple-element.140), channel_id=1, source_target_pairs={{0,128},{128,0},{1,129},{129,1},{2,130},{130,2},{3,131},{131,3},{4... | collective-permute-start | bytes 497672 | tf_op jit(solution)/shard_map/ppermute | solution.py:23
  112.9 2.7 %collective-permute-done.27 = bf16[160,256]{1,0:T(8,128)(2,1)S(1)} collective-permute-done((bf16[160,256]{1,0:T(8,128)(2,1)S(1)}, bf16[160,256]{1,0:T(8,128)(2,1)S(1)}, u32[]{:S(2)}, u32[]{:S(2)}) %collective-permute-start.27) | collective-permute-done | bytes 81952 | tf_op jit(solution)/shard_map/ppermute | solution.py:23
  117.3 4.1 %collective-permute-start.30 = (bf16[160,128]{1,0:T(8,128)(2,1)S(1)}, bf16[160,128]{1,0:T(8,128)(2,1)S(1)}, u32[]{:S(2)}, u32[]{:S(2)}) collective-permute-start(bf16[160,128]{1,0:T(8,128)(2,1)S(1)} %pad_maximum_fusion.11), channel_id=1, source_target_pairs={{0,128},{128,0},{1,129},{129,1},{2,130},{130,2},{3,131},{131,3},{4... | collective-permute-start | bytes 122888 | tf_op jit(solution)/shard_map/ppermute | solution.py:23
  121.4 2.2 %collective-permute-done.35 = bf16[288,576]{1,0:T(8,128)(2,1)S(1)} collective-permute-done((bf16[288,576]{1,0:T(8,128)(2,1)S(1)}, bf16[288,576]{1,0:T(8,128)(2,1)S(1)}, u32[]{:S(2)}, u32[]{:S(2)}) %collective-permute-start.35) | collective-permute-done | bytes 331808 | tf_op jit(solution)/shard_map/ppermute | solution.py:23
  124.1 10.3 %collective-permute-start.38 = (bf16[2,144,576]{2,1,0:T(8,128)(2,1)S(1)}, bf16[2,144,576]{2,1,0:T(8,128)(2,1)S(1)}, u32[]{:S(2)}, u32[]{:S(2)}) collective-permute-start(bf16[2,144,576]{2,1,0:T(8,128)(2,1)S(1)} %pad_maximum_fusion.6), channel_id=1, source_target_pairs={{0,16},{16,0},{1,17},{17,1},{2,18},{18,2},{3,19},{19,3},{4,20},{20... | collective-permute-start | bytes 995336 | tf_op jit(solution)/shard_map/ppermute | solution.py:23
  134.8 2.6 %collective-permute-start.31 = (f32[144]{0:T(256)S(1)}, f32[144]{0:T(256)S(1)}, u32[]{:S(2)}, u32[]{:S(2)}) collective-permute-start(f32[144]{0:T(256)S(1)} %slice_add_fusion.1), channel_id=1, source_target_pairs={{0,16},{16,0},{1,17},{17,1},{2,18},{18,2},{3,19},{19,3},{4,20},{20... | collective-permute-start | bytes 1736 | tf_op jit(solution)/shard_map/ppermute | solution.py:23
  138.2 4.6 %collective-permute-start.32 = (f32[144]{0:T(256)S(1)}, f32[144]{0:T(256)S(1)}, u32[]{:S(2)}, u32[]{:S(2)}) collective-permute-start(f32[144]{0:T(256)S(1)} %add.232), channel_id=1, source_target_pairs={{0,32},{32,64},{64,96},{96,0},{1,33},{33,65},{65,97},{97,1},{2,34}... | collective-permute-start | bytes 1736 | tf_op jit(solution)/shard_map/ppermute | solution.py:23
  145.9 2.0 %collective-permute-done.34 = f32[144]{0:T(256)S(1)} collective-permute-done((f32[144]{0:T(256)S(1)}, f32[144]{0:T(256)S(1)}, u32[]{:S(2)}, u32[]{:S(2)}) %collective-permute-start.34) | collective-permute-done | bytes 608 | tf_op jit(solution)/shard_map/ppermute | solution.py:23
  149.9 2.2 %join.1 = (bf16[144,1152]{1,0:T(8,128)(2,1)}, bf16[144,1152]{1,0:T(8,128)(2,1)}) custom-call(bf16[2,144,576]{2,1,0:T(8,128)(2,1)} %bitcast.132, bf16[144,576]{1,0:T(8,128)(2,1)} %copy-done.2, bf16[2,144,576]{2,1,0:T(8,128)(2,1)} %copy-done.1), custom_call_target="tpu_custom_call" | custom-call | tf_op jit(solution)/shard_map/join/pallas_call | solution.py:122
  (158 shorter events, 34.8 us)
Async XLA Ops:
  2.0 18.1 %collective-permute-start = (bf16[208,576]{1,0:T(8,128)(2,1)S(1)}, bf16[208,576]{1,0:T(8,128)(2,1)S(1)}, u32[]{:S(2)}, u32[]{:S(2)}) collective-permute-start(bf16[208,576]{1,0:T(8,128)(2,1)S(1)} %get-tuple-element.65), channel_id=1, source_target_pairs={{0,16},{16,0},{1,17},{17,1},{2,18},{18,2},{3,19},{19,3},{4,20},{20... | collective-permute-start | bytes 718856 | tf_op jit(solution)/shard_map/ppermute | solution.py:23
  5.3 9.5 %collective-permute-start.1 = (bf16[576,128]{1,0:T(8,128)(2,1)}, bf16[576,128]{1,0:T(8,128)(2,1)S(1)}, u32[]{:S(2)}, u32[]{:S(2)}) collective-permute-start(bf16[576,128]{1,0:T(8,128)(2,1)} %bitcast.142), channel_id=1, source_target_pairs={{0,128},{128,0},{1,129},{129,1},{2,130},{130,2},{3,131},{131,3},{4... | collective-permute-start | bytes 442376 | tf_op jit(solution)/shard_map/ppermute | solution.py:23
  11.9 27.2 %collective-permute-start.4 = (bf16[144,576]{1,0:T(8,128)(2,1)S(1)}, bf16[144,576]{1,0:T(8,128)(2,1)S(1)}, u32[]{:S(2)}, u32[]{:S(2)}) collective-permute-start(bf16[144,576]{1,0:T(8,128)(2,1)S(1)} %get-tuple-element.76), channel_id=1, source_target_pairs={{0,128},{128,0},{1,129},{129,1},{2,130},{130,2},{3,131},{131,3},{4... | collective-permute-start | bytes 497672 | tf_op jit(solution)/shard_map/ppermute | solution.py:23
  14.9 20.0 %collective-permute-start.5 = (bf16[144,576]{1,0:T(8,128)(2,1)S(1)}, bf16[144,576]{1,0:T(8,128)(2,1)S(1)}, u32[]{:S(2)}, u32[]{:S(2)}) collective-permute-start(bf16[144,576]{1,0:T(8,128)(2,1)S(1)} %get-tuple-element.77), channel_id=1, source_target_pairs={{0,128},{128,0},{1,129},{129,1},{2,130},{130,2},{3,131},{131,3},{4... | collective-permute-start | bytes 497672 | tf_op jit(solution)/shard_map/ppermute | solution.py:23
  20.2 16.0 %collective-permute-start.2 = (bf16[2,144,576]{2,1,0:T(8,128)(2,1)S(1)}, bf16[2,144,576]{2,1,0:T(8,128)(2,1)S(1)}, u32[]{:S(2)}, u32[]{:S(2)}) collective-permute-start(bf16[2,144,576]{2,1,0:T(8,128)(2,1)S(1)} %maximum_select_fusion), channel_id=1, source_target_pairs={{0,32},{32,64},{64,96},{96,0},{1,33},{33,65},{65,97},{97,1},{2,34}... | collective-permute-start | bytes 995336 | tf_op jit(solution)/shard_map/ppermute | solution.py:23
  21.5 14.8 %collective-permute-start.3 = (bf16[2,144,576]{2,1,0:T(8,128)(2,1)S(1)}, bf16[2,144,576]{2,1,0:T(8,128)(2,1)S(1)}, u32[]{:S(2)}, u32[]{:S(2)}) collective-permute-start(bf16[2,144,576]{2,1,0:T(8,128)(2,1)S(1)} %maximum_select_fusion), channel_id=1, source_target_pairs={{0,96},{32,0},{64,32},{96,64},{1,97},{33,1},{65,33},{97,65},{2,98}... | collective-permute-start | bytes 995336 | tf_op jit(solution)/shard_map/ppermute | solution.py:23
  23.0 37.1 %collective-permute-start.10 = (bf16[2,144,576]{2,1,0:T(8,128)(2,1)S(1)}, bf16[2,144,576]{2,1,0:T(8,128)(2,1)S(1)}, u32[]{:S(2)}, u32[]{:S(2)}) collective-permute-start(bf16[2,144,576]{2,1,0:T(8,128)(2,1)S(1)} %maximum_select_fusion), channel_id=1, source_target_pairs={{0,64},{32,96},{64,0},{96,32},{1,65},{33,97},{65,1},{97,33},{2,66}... | collective-permute-start | bytes 995336 | tf_op jit(solution)/shard_map/ppermute | solution.py:23
  34.9 5.7 %collective-permute-start.6 = (bf16[144,576]{1,0:T(8,128)(2,1)S(1)}, bf16[144,576]{1,0:T(8,128)(2,1)S(1)}, u32[]{:S(2)}, u32[]{:S(2)}) collective-permute-start(bf16[144,576]{1,0:T(8,128)(2,1)S(1)} %collective-permute-done.5), channel_id=1, source_target_pairs={{0,16},{16,0},{1,17},{17,1},{2,18},{18,2},{3,19},{19,3},{4,20},{20... | collective-permute-start | bytes 497672 | tf_op jit(solution)/shard_map/ppermute | solution.py:23
  36.3 6.9 %collective-permute-start.7 = (bf16[576,256]{1,0:T(8,128)(2,1)S(1)}, bf16[576,256]{1,0:T(8,128)(2,1)S(1)}, u32[]{:S(2)}, u32[]{:S(2)}) collective-permute-start(bf16[576,256]{1,0:T(8,128)(2,1)S(1)} %pad_maximum_fusion.7), channel_id=1, source_target_pairs={{0,1},{1,2},{2,3},{3,0},{4,5},{5,6},{6,7},{7,4},{8,9},{9,10},{10,1... | collective-permute-start | bytes 884744 | tf_op jit(solution)/shard_map/ppermute | solution.py:23
  37.6 11.5 %collective-permute-start.8 = (bf16[576,256]{1,0:T(8,128)(2,1)S(1)}, bf16[576,256]{1,0:T(8,128)(2,1)S(1)}, u32[]{:S(2)}, u32[]{:S(2)}) collective-permute-start(bf16[576,256]{1,0:T(8,128)(2,1)S(1)} %pad_maximum_fusion.7), channel_id=1, source_target_pairs={{0,3},{1,0},{2,1},{3,2},{4,7},{5,4},{6,5},{7,6},{8,11},{9,8},{10,9... | collective-permute-start | bytes 884744 | tf_op jit(solution)/shard_map/ppermute | solution.py:23
  39.1 13.3 %collective-permute-start.9 = (bf16[576,256]{1,0:T(8,128)(2,1)S(1)}, bf16[576,256]{1,0:T(8,128)(2,1)S(1)}, u32[]{:S(2)}, u32[]{:S(2)}) collective-permute-start(bf16[576,256]{1,0:T(8,128)(2,1)S(1)} %pad_maximum_fusion.7), channel_id=1, source_target_pairs={{0,2},{1,3},{2,0},{3,1},{4,6},{5,7},{6,4},{7,5},{8,10},{9,11},{10,... | collective-permute-start | bytes 884744 | tf_op jit(solution)/shard_map/ppermute | solution.py:23
  40.7 16.9 %collective-permute-start.12 = (bf16[2,144,576]{2,1,0:T(8,128)(2,1)S(1)}, bf16[2,144,576]{2,1,0:T(8,128)(2,1)S(1)}, u32[]{:S(2)}, u32[]{:S(2)}) collective-permute-start(bf16[2,144,576]{2,1,0:T(8,128)(2,1)S(1)} %maximum_select_fusion.1), channel_id=1, source_target_pairs={{0,32},{32,64},{64,96},{96,0},{1,33},{33,65},{65,97},{97,1},{2,34}... | collective-permute-start | bytes 995336 | tf_op jit(solution)/shard_map/ppermute | solution.py:23
  43.2 17.2 %collective-permute-start.15 = (bf16[2,144,576]{2,1,0:T(8,128)(2,1)S(1)}, bf16[2,144,576]{2,1,0:T(8,128)(2,1)S(1)}, u32[]{:S(2)}, u32[]{:S(2)}) collective-permute-start(bf16[2,144,576]{2,1,0:T(8,128)(2,1)S(1)} %maximum_select_fusion.1), channel_id=1, source_target_pairs={{0,64},{32,96},{64,0},{96,32},{1,65},{33,97},{65,1},{97,33},{2,66}... | collective-permute-start | bytes 995336 | tf_op jit(solution)/shard_map/ppermute | solution.py:23
  49.0 13.5 %collective-permute-start.13 = (bf16[2,144,576]{2,1,0:T(8,128)(2,1)S(1)}, bf16[2,144,576]{2,1,0:T(8,128)(2,1)S(1)}, u32[]{:S(2)}, u32[]{:S(2)}) collective-permute-start(bf16[2,144,576]{2,1,0:T(8,128)(2,1)S(1)} %maximum_select_fusion.1), channel_id=1, source_target_pairs={{0,96},{32,0},{64,32},{96,64},{1,97},{33,1},{65,33},{97,65},{2,98}... | collective-permute-start | bytes 995336 | tf_op jit(solution)/shard_map/ppermute | solution.py:23
  52.4 10.2 %collective-permute-start.11 = (bf16[2,64,576]{2,1,0:T(8,128)(2,1)S(1)}, bf16[2,64,576]{2,1,0:T(8,128)(2,1)S(1)}, u32[]{:S(2)}, u32[]{:S(2)}) collective-permute-start(bf16[2,64,576]{2,1,0:T(8,128)(2,1)S(1)} %get-tuple-element.86), channel_id=1, source_target_pairs={{0,128},{128,0},{1,129},{129,1},{2,130},{130,2},{3,131},{131,3},{4... | collective-permute-start | bytes 442376 | tf_op jit(solution)/shard_map/ppermute | solution.py:23
  57.7 4.9 %collective-permute-start.14 = (bf16[2304,256]{1,0:T(8,128)(2,1)S(1)}, bf16[2304,256]{1,0:T(8,128)(2,1)S(1)}, u32[]{:S(2)}, u32[]{:S(2)}) collective-permute-start(bf16[2304,256]{1,0:T(8,128)(2,1)S(1)} %multiply_convert_fusion), channel_id=1, source_target_pairs={{0,16},{16,0},{1,17},{17,1},{2,18},{18,2},{3,19},{19,3},{4,20},{20... | collective-permute-start | bytes 3538952 | tf_op jit(solution)/shard_map/ppermute | solution.py:23
  74.3 10.6 %collective-permute-start.19 = (bf16[288,576]{1,0:T(8,128)(2,1)S(1)}, bf16[288,576]{1,0:T(8,128)(2,1)S(1)}, u32[]{:S(2)}, u32[]{:S(2)}) collective-permute-start(bf16[288,576]{1,0:T(8,128)(2,1)S(1)} %convolution_convert_fusion.5), channel_id=1, source_target_pairs={{0,96},{32,0},{64,32},{96,64},{1,97},{33,1},{65,33},{97,65},{2,98}... | collective-permute-start | bytes 995336 | tf_op jit(solution)/shard_map/ppermute | solution.py:23
  76.2 10.7 %collective-permute-start.18 = (bf16[288,576]{1,0:T(8,128)(2,1)S(1)}, bf16[288,576]{1,0:T(8,128)(2,1)S(1)}, u32[]{:S(2)}, u32[]{:S(2)}) collective-permute-start(bf16[288,576]{1,0:T(8,128)(2,1)S(1)} %convolution_convert_fusion.6), channel_id=1, source_target_pairs={{0,32},{32,64},{64,96},{96,0},{1,33},{33,65},{65,97},{97,1},{2,34}... | collective-permute-start | bytes 995336 | tf_op jit(solution)/shard_map/ppermute | solution.py:23
  86.9 9.7 %collective-permute-start.21 = (bf16[592,256]{1,0:T(8,128)(2,1)S(1)}, bf16[592,256]{1,0:T(8,128)(2,1)S(1)}, u32[]{:S(2)}, u32[]{:S(2)}) collective-permute-start(bf16[592,256]{1,0:T(8,128)(2,1)S(1)} %get-tuple-element.96), channel_id=1, source_target_pairs={{0,1},{1,2},{2,3},{3,0},{4,5},{5,6},{6,7},{7,4},{8,9},{9,10},{10,1... | collective-permute-start | bytes 909320 | tf_op jit(solution)/shard_map/ppermute | solution.py:23
  87.5 9.2 %collective-permute-start.22 = (bf16[592,256]{1,0:T(8,128)(2,1)S(1)}, bf16[592,256]{1,0:T(8,128)(2,1)S(1)}, u32[]{:S(2)}, u32[]{:S(2)}) collective-permute-start(bf16[592,256]{1,0:T(8,128)(2,1)S(1)} %get-tuple-element.97), channel_id=1, source_target_pairs={{0,3},{1,0},{2,1},{3,2},{4,7},{5,4},{6,5},{7,6},{8,11},{9,8},{10,9... | collective-permute-start | bytes 909320 | tf_op jit(solution)/shard_map/ppermute | solution.py:23
  90.7 13.4 %collective-permute-start.23 = (bf16[592,256]{1,0:T(8,128)(2,1)S(1)}, bf16[592,256]{1,0:T(8,128)(2,1)S(1)}, u32[]{:S(2)}, u32[]{:S(2)}) collective-permute-start(bf16[592,256]{1,0:T(8,128)(2,1)S(1)} %get-tuple-element.98), channel_id=1, source_target_pairs={{0,2},{1,3},{2,0},{3,1},{4,6},{5,7},{6,4},{7,5},{8,10},{9,11},{10,... | collective-permute-start | bytes 909320 | tf_op jit(solution)/shard_map/ppermute | solution.py:23
  92.4 11.9 %collective-permute-start.24 = (bf16[288,576]{1,0:T(8,128)(2,1)S(1)}, bf16[288,576]{1,0:T(8,128)(2,1)S(1)}, u32[]{:S(2)}, u32[]{:S(2)}) collective-permute-start(bf16[288,576]{1,0:T(8,128)(2,1)S(1)} %convolution_convert_fusion.4), channel_id=1, source_target_pairs={{0,64},{32,96},{64,0},{96,32},{1,65},{33,97},{65,1},{97,33},{2,66}... | collective-permute-start | bytes 995336 | tf_op jit(solution)/shard_map/ppermute | solution.py:23
  104.6 6.1 %collective-permute-start.25 = (bf16[160,256]{1,0:T(8,128)(2,1)S(1)}, bf16[160,256]{1,0:T(8,128)(2,1)S(1)}, u32[]{:S(2)}, u32[]{:S(2)}) collective-permute-start(bf16[160,256]{1,0:T(8,128)(2,1)S(1)} %get-tuple-element.162), channel_id=1, source_target_pairs={{0,4},{4,8},{8,12},{12,0},{1,5},{5,9},{9,13},{13,1},{2,6},{6,10},{... | collective-permute-start | bytes 245768 | tf_op jit(solution)/shard_map/ppermute | solution.py:23
  107.9 7.7 %collective-permute-start.27 = (bf16[160,256]{1,0:T(8,128)(2,1)S(1)}, bf16[160,256]{1,0:T(8,128)(2,1)S(1)}, u32[]{:S(2)}, u32[]{:S(2)}) collective-permute-start(bf16[160,256]{1,0:T(8,128)(2,1)S(1)} %get-tuple-element.164), channel_id=1, source_target_pairs={{0,8},{4,12},{8,0},{12,4},{1,9},{5,13},{9,1},{13,5},{2,10},{6,14},... | collective-permute-start | bytes 245768 | tf_op jit(solution)/shard_map/ppermute | solution.py:23
  107.9 9.4 %collective-permute-start.28 = (bf16[288,576]{1,0:T(8,128)(2,1)S(1)}, bf16[288,576]{1,0:T(8,128)(2,1)S(1)}, u32[]{:S(2)}, u32[]{:S(2)}) collective-permute-start(bf16[288,576]{1,0:T(8,128)(2,1)S(1)} %convolution_convert_fusion.3), channel_id=1, source_target_pairs={{0,32},{32,64},{64,96},{96,0},{1,33},{33,65},{65,97},{97,1},{2,34}... | collective-permute-start | bytes 995336 | tf_op jit(solution)/shard_map/ppermute | solution.py:23
  107.9 9.4 %collective-permute-start.29 = (bf16[288,576]{1,0:T(8,128)(2,1)S(1)}, bf16[288,576]{1,0:T(8,128)(2,1)S(1)}, u32[]{:S(2)}, u32[]{:S(2)}) collective-permute-start(bf16[288,576]{1,0:T(8,128)(2,1)S(1)} %convolution_convert_fusion.2), channel_id=1, source_target_pairs={{0,96},{32,0},{64,32},{96,64},{1,97},{33,1},{65,33},{97,65},{2,98}... | collective-permute-start | bytes 995336 | tf_op jit(solution)/shard_map/ppermute | solution.py:23
  110.6 13.0 %collective-permute-start.35 = (bf16[288,576]{1,0:T(8,128)(2,1)S(1)}, bf16[288,576]{1,0:T(8,128)(2,1)S(1)}, u32[]{:S(2)}, u32[]{:S(2)}) collective-permute-start(bf16[288,576]{1,0:T(8,128)(2,1)S(1)} %convolution_convert_fusion.1), channel_id=1, source_target_pairs={{0,64},{32,96},{64,0},{96,32},{1,65},{33,97},{65,1},{97,33},{2,66}... | collective-permute-start | bytes 995336 | tf_op jit(solution)/shard_map/ppermute | solution.py:23
  110.8 13.3 %collective-permute-start.37 = (bf16[144,576]{1,0:T(8,128)(2,1)S(1)}, bf16[144,576]{1,0:T(8,128)(2,1)S(1)}, u32[]{:S(2)}, u32[]{:S(2)}) collective-permute-start(bf16[144,576]{1,0:T(8,128)(2,1)S(1)} %get-tuple-element.140), channel_id=1, source_target_pairs={{0,128},{128,0},{1,129},{129,1},{2,130},{130,2},{3,131},{131,3},{4... | collective-permute-start | bytes 497672 | tf_op jit(solution)/shard_map/ppermute | solution.py:23
  115.6 32.8 %collective-permute-start.36 = (bf16[144,576]{1,0:T(8,128)(2,1)S(1)}, bf16[144,576]{1,0:T(8,128)(2,1)S(1)}, u32[]{:S(2)}, u32[]{:S(2)}) collective-permute-start(bf16[144,576]{1,0:T(8,128)(2,1)S(1)} %get-tuple-element.141), channel_id=1, source_target_pairs={{0,128},{128,0},{1,129},{129,1},{2,130},{130,2},{3,131},{131,3},{4... | collective-permute-start | bytes 497672 | tf_op jit(solution)/shard_map/ppermute | solution.py:23
  117.3 17.4 %collective-permute-start.30 = (bf16[160,128]{1,0:T(8,128)(2,1)S(1)}, bf16[160,128]{1,0:T(8,128)(2,1)S(1)}, u32[]{:S(2)}, u32[]{:S(2)}) collective-permute-start(bf16[160,128]{1,0:T(8,128)(2,1)S(1)} %pad_maximum_fusion.11), channel_id=1, source_target_pairs={{0,128},{128,0},{1,129},{129,1},{2,130},{130,2},{3,131},{131,3},{4... | collective-permute-start | bytes 122888 | tf_op jit(solution)/shard_map/ppermute | solution.py:23
  124.1 24.3 %collective-permute-start.38 = (bf16[2,144,576]{2,1,0:T(8,128)(2,1)S(1)}, bf16[2,144,576]{2,1,0:T(8,128)(2,1)S(1)}, u32[]{:S(2)}, u32[]{:S(2)}) collective-permute-start(bf16[2,144,576]{2,1,0:T(8,128)(2,1)S(1)} %pad_maximum_fusion.6), channel_id=1, source_target_pairs={{0,16},{16,0},{1,17},{17,1},{2,18},{18,2},{3,19},{19,3},{4,20},{20... | collective-permute-start | bytes 995336 | tf_op jit(solution)/shard_map/ppermute | solution.py:23
  138.2 7.7 %collective-permute-start.32 = (f32[144]{0:T(256)S(1)}, f32[144]{0:T(256)S(1)}, u32[]{:S(2)}, u32[]{:S(2)}) collective-permute-start(f32[144]{0:T(256)S(1)} %add.232), channel_id=1, source_target_pairs={{0,32},{32,64},{64,96},{96,0},{1,33},{33,65},{65,97},{97,1},{2,34}... | collective-permute-start | bytes 1736 | tf_op jit(solution)/shard_map/ppermute | solution.py:23
  (12 other events, 80.2 us)
